TPU v7x, 32 devices: a whole 2x2x4 slice. The times are simulated.
32 devices in a mesh: groups: 2 (over x), seq: 16 (over z, y, core).
Axes of the slice: x: 2, y: 2, z: 4, core: 2. Of those that a mesh axis runs over, the one named last changes fastest.
Arguments:
- queries: bfloat16 [8192, 1024], P(('groups', 'seq')), parts along dimension 0, may hold values from -6 to 6
- keys: bfloat16 [8192, 1024], P(('groups', 'seq')), parts along dimension 0, may hold values from -6 to 6
- values: bfloat16 [8192, 1024], P(('groups', 'seq')), parts along dimension 0, may hold values from -6 to 6
- grad_out: bfloat16 [8192, 1024], P(('groups', 'seq')), parts along dimension 0, may hold values from -0.0078125 to 0.0078125
Outputs:
- grad_queries: bfloat16 [1024, 8192], P('seq', 'groups'), parts along dimension 1
- grad_keys: bfloat16 [1024, 8192], P('seq', 'groups'), parts along dimension 1
- grad_values: bfloat16 [1024, 8192], P('seq', 'groups'), parts along dimension 1
There are 2 independent parts, one for each index of `groups`. A program takes and returns all parts, laid end to end along the dimension named above; each array names one. Nothing has to cross between parts.
All inputs are finite; a program needn't handle non-finite values.
Results may differ from a plain program's by a relative error of at most 0.005.
Values may be sent and summed in bfloat16 or wider, within the bound.
No kernel may reach another device: no remote copies, remote signals or barrier semaphores. Data moves between devices by JAX's collectives and lax.ppermute only.
A program may use at most 256 MiB of HBM per device.

v0:
```python
import jax
import jax.numpy as jnp
from jax import lax
from jax.sharding import PartitionSpec as P

HDIM = 128


def entering(shard, axis, combine, identity, reverse):
    size, position = (lax.axis_size(axis), lax.axis_index(axis))
    everything = lax.all_gather(shard, axis)
    start = jnp.broadcast_to(jnp.asarray(identity, shard.dtype), shard.shape)

    def lap(k, before):
        at = size - 1 - k if reverse else k
        reached = at > position if reverse else at < position
        new = combine(before, everything[at])
        return jnp.where(reached, new, before)

    return lax.fori_loop(0, size, lap, start)


def accumulate(earlier, later):
    return earlier + later


def body(queries, keys, values, grad_out):
    length = queries.shape[0]
    head_count = queries.shape[1] // HDIM
    query_heads = jnp.transpose(queries.reshape(length, head_count, HDIM), (1, 0, 2))
    key_heads = jnp.transpose(keys.reshape(length, head_count, HDIM), (1, 0, 2))
    value_heads = jnp.transpose(values.reshape(length, head_count, HDIM), (1, 0, 2))
    gradient_heads = jnp.transpose(grad_out.reshape(length, head_count, HDIM), (1, 0, 2))
    positions = lax.iota(jnp.int32, length)
    causal = positions[:, None] >= positions[None, :]
    scores_qk = jnp.einsum(
        "htd,hsd->hts", query_heads, key_heads, preferred_element_type=jnp.float32
    )
    scores_gv = jnp.einsum(
        "htd,hsd->hts", gradient_heads, value_heads, preferred_element_type=jnp.float32
    )
    masked_query_key = jnp.where(causal[None], scores_qk, 0.0).astype(jnp.bfloat16)
    masked_gv = jnp.where(causal[None], scores_gv, 0.0).astype(jnp.bfloat16)
    state_own = jnp.einsum(
        "hsd,hse->hde", key_heads, value_heads, preferred_element_type=jnp.float32
    )
    grad_own = jnp.einsum(
        "htf,htb->hfb", query_heads, gradient_heads, preferred_element_type=jnp.float32
    )
    zeros_state = jnp.zeros_like(state_own)
    state_before = entering(state_own, "seq", accumulate, zeros_state, False)
    grad_after = entering(grad_own, "seq", accumulate, zeros_state, True)
    state_half = state_before.astype(jnp.bfloat16)
    gradient_halves = grad_after.astype(jnp.bfloat16)
    grad_query = jnp.einsum(
        "hsd,hts->hdt", key_heads, masked_gv, preferred_element_type=jnp.float32
    )
    grad_query = grad_query + jnp.einsum(
        "hdv,htv->hdt", state_half, gradient_heads, preferred_element_type=jnp.float32
    )
    grad_key = jnp.einsum(
        "htd,hts->hds", query_heads, masked_gv, preferred_element_type=jnp.float32
    )
    grad_key = grad_key + jnp.einsum(
        "hdv,hsv->hds", gradient_halves, value_heads, preferred_element_type=jnp.float32
    )
    value_gradient = jnp.einsum(
        "htd,hts->hds", gradient_heads, masked_query_key, preferred_element_type=jnp.float32
    )
    value_gradient = value_gradient + jnp.einsum(
        "hfb,hsf->hbs", gradient_halves, key_heads, preferred_element_type=jnp.float32
    )
    width = head_count * HDIM
    query_rows = grad_query.reshape(width, length).astype(jnp.bfloat16)
    key_rows = grad_key.reshape(width, length).astype(jnp.bfloat16)
    value_rows = value_gradient.reshape(width, length).astype(jnp.bfloat16)
    return (
        lax.all_to_all(query_rows, "seq", split_axis=0, concat_axis=1, tiled=True),
        lax.all_to_all(key_rows, "seq", split_axis=0, concat_axis=1, tiled=True),
        lax.all_to_all(value_rows, "seq", split_axis=0, concat_axis=1, tiled=True),
    )


def solution(mesh):
    in_specs = (
        P(("groups", "seq"), None),
        P(("groups", "seq"), None),
        P(("groups", "seq"), None),
        P(("groups", "seq"), None),
    )
    out_specs = (P("seq", "groups"), P("seq", "groups"), P("seq", "groups"))
    return jax.shard_map(body, mesh=mesh, in_specs=in_specs, out_specs=out_specs, check_vma=False)
```

profile of v0, /device:TPU:19, one launch (start us, length us, event | category | flops | bytes accessed | tf_op | source)
XLA Modules:
  0.0 229.8 jit_solution(18054935360016273277)
XLA Ops:
  7.2 1.2 copy.50
  11.8 1.5 convolution_bitcast_fusion.1
  13.3 1.3 convolution_bitcast_fusion
  14.6 71.7 %all-gather.5.cloned.1.call-done = f32[128,128,128]{2,1,0:T(8,128)} async-done(((f32[8,128,128]{2,1,0:T(8,128)}), f32[128,128,128]{2,1,0:T(8,128)}) %all-gather.5.cloned.1.call-update) | async-done | bytes 8388624 | tf_op jit(solution)/shard_map/all_gather | solution.py:11
  86.3 20.1 %while.30 = (s32[]{:T(128)}, f32[8,128,128]{2,1,0:T(8,128)S(1)}, s32[]{:T(128)}, f32[16,8,128,128]{3,2,1,0:T(8,128)}, s32[]{:T(128)}, /*index=5*/s32[]{:T(128)}) while((s32[]{:T(128)}, f32[8,128,128]{2,1,0:T(8,128)S(1)}, s32[]{:T(128)}, f32[16,8,128,128]{3,2,1,0:T(8,128)}, s32[]{:T(128)}, /*index=5*/s32[]{:T(128)}) %tuple.82), condition=%wide.region_1.2_spmd.clone, body=%wide.region_0.1_spmd.clone.sunk | while | flops 393220 | bytes 1572965 | solution.py:20
  87.6 1.2 add_select_fusion.4
  88.8 1.2 add_select_fusion.4
  90.1 1.2 add_select_fusion.4
  91.3 1.2 add_select_fusion.4
  92.6 1.2 add_select_fusion.4
  93.8 1.2 add_select_fusion.4
  95.1 1.3 add_select_fusion.4
  96.4 1.2 add_select_fusion.4
  97.6 1.2 add_select_fusion.4
  98.9 1.2 add_select_fusion.4
  100.1 1.2 add_select_fusion.4
  101.4 1.2 add_select_fusion.4
  102.6 1.2 add_select_fusion.4
  105.1 1.2 add_select_fusion.4
  106.4 2.3 %fusion.4 = bf16[8,128,256]{2,1,0:T(8,128)(2,1)} fusion(f32[8,128,256]{2,1,0:T(8,128)} %convolution_bitcast_fusion.1, bf16[8,256,128]{1,2,0:T(8,128)(2,1)S(1)} %bitcast.92, f32[8,128,128]{2,1,0:T(8,128)S(1)} %get-tuple-element.192), kind=kOutput, calls=%fused_computation.12 | convolution fusion | flops 67764224 | bytes 2621440 | tf_op jit(solution)/shard_map/hdv,htv->hdt/dot_general | solution.py:58
  108.7 5.3 %all-to-all-start = ((bf16[16,64,256]{2,1,0:T(8,128)(2,1)}), bf16[16,64,256]{2,1,0:T(8,128)(2,1)}, u32[]{:S(2)}, u32[]{:S(2)}) async-start(bf16[16,64,256]{2,1,0:T(8,128)(2,1)} %bitcast.9), calls=%async_computation | async-start | bytes 1048576 | tf_op jit(solution)/shard_map/all_to_all | solution.py:78
  114.0 49.3 %all-gather.7.cloned.1.call-done = f32[128,128,128]{2,1,0:T(8,128)} async-done(((f32[8,128,128]{2,1,0:T(8,128)}), f32[128,128,128]{2,1,0:T(8,128)}) %all-gather.7.cloned.1.call-update) | async-done | bytes 8388624 | tf_op jit(solution)/shard_map/all_gather | solution.py:11
  163.3 20.2 %while.31 = (s32[]{:T(128)}, f32[8,128,128]{2,1,0:T(8,128)S(1)}, s32[]{:T(128)}, f32[16,8,128,128]{3,2,1,0:T(8,128)}, s32[]{:T(128)}, /*index=5*/s32[]{:T(128)}, s32[]{:T(128)}, s32[]{:T(128)}) while((s32[]{:T(128)}, f32[8,128,128]{2,1,0:T(8,128)S(1)}, s32[]{:T(128)}, f32[16,8,128,128]{3,2,1,0:T(8,128)}, s32[]{:T(128)}, ...), condition=%wide.region_3.4_spmd.clone, body=%wide.region_2.3_spmd.clone.sunk | while | flops 393224 | bytes 1573027 | solution.py:20
  163.3 1.3 add_select_fusion.5
  169.7 1.2 add_select_fusion.5
  184.6 5.8 %all-to-all-start.1 = ((bf16[16,64,256]{2,1,0:T(8,128)(2,1)}), bf16[16,64,256]{2,1,0:T(8,128)(2,1)S(1)}, u32[]{:S(2)}, u32[]{:S(2)}) async-start(bf16[16,64,256]{2,1,0:T(8,128)(2,1)} %bitcast.99), calls=%async_computation.1 | async-start | bytes 1048576 | tf_op jit(solution)/shard_map/all_to_all | solution.py:79
  190.4 2.4 %fusion.8 = f32[8,128,256]{2,1,0:T(8,128)} fusion(f32[8,128,128]{2,1,0:T(8,128)S(1)} %get-tuple-element.193, bf16[256,1024]{1,0:T(8,128)(2,1)} %param.9), kind=kOutput, calls=%fused_computation.17 | convolution fusion | flops 67239936 | bytes 2097152 | tf_op jit(solution)/shard_map/hfb,hsf->hbs/dot_general | solution.py:70
  192.8 2.7 %fusion.3 = bf16[8,128,256]{2,1,0:T(8,128)(2,1)} fusion(f32[8,128,256]{2,1,0:T(8,128)} %fusion.8, bf16[8,256,128]{1,2,0:T(8,128)(2,1)S(1)} %bitcast.93, bf16[8,256,128]{1,2,0:T(8,128)(2,1)S(1)} %bitcast.96, pred[256,256]{1,0:T(8,128)(4,1)S(1)} %iota_compare_fusion, bf16[256,1024]{1,0:T(8,128)(2,1)S(1)} %copy-done.2), kind=kOutput, calls=%fused_computation.11 | convolution fusion | flops 270008320 | bytes 3211264 | tf_op jit(solution)/shard_map/htd,hts->hds/dot_general | solution.py:67
  195.4 8.2 %all-to-all-done.1 = bf16[16,64,256]{2,1,0:T(8,128)(2,1)S(1)} async-done(((bf16[16,64,256]{2,1,0:T(8,128)(2,1)}), bf16[16,64,256]{2,1,0:T(8,128)(2,1)S(1)}, u32[]{:S(2)}, u32[]{:S(2)}) %all-to-all-start.1) | async-done | bytes 524320 | tf_op jit(solution)/shard_map/all_to_all | solution.py:79
  203.6 5.3 %all-to-all-start.2 = ((bf16[16,64,256]{2,1,0:T(8,128)(2,1)}), bf16[16,64,256]{2,1,0:T(8,128)(2,1)S(1)}, u32[]{:S(2)}, u32[]{:S(2)}) async-start(bf16[16,64,256]{2,1,0:T(8,128)(2,1)} %bitcast.19), calls=%async_computation.2 | async-start | bytes 1048576 | tf_op jit(solution)/shard_map/all_to_all | solution.py:80
  208.9 1.9 copy.47
  211.6 10.5 %all-to-all-done.2 = bf16[16,64,256]{2,1,0:T(8,128)(2,1)S(1)} async-done(((bf16[16,64,256]{2,1,0:T(8,128)(2,1)}), bf16[16,64,256]{2,1,0:T(8,128)(2,1)S(1)}, u32[]{:S(2)}, u32[]{:S(2)}) %all-to-all-start.2) | async-done | bytes 524320 | tf_op jit(solution)/shard_map/all_to_all | solution.py:80
  (42 shorter events, 25.7 us)
Async XLA Ops:
  7.2 1.3 copy-start
  7.2 2.5 %copy-start.3 = (bf16[256,1024]{1,0:T(8,128)(2,1)S(1)}, bf16[256,1024]{1,0:T(8,128)(2,1)}, u32[]{:S(2)}) copy-start(bf16[256,1024]{1,0:T(8,128)(2,1)} %param.11) | copy-start | bytes 1572868
  7.2 79.1 %all-gather.5.cloned.1.call-start = ((), (), s32[]{:S(2)}) async-start(), calls=%async_computation.3 | async-start | bytes 8912896 | tf_op jit(solution)/shard_map/all_gather | solution.py:11
  7.2 2.7 %copy-start.4 = (bf16[256,1024]{1,0:T(8,128)(2,1)S(1)}, bf16[256,1024]{1,0:T(8,128)(2,1)}, u32[]{:S(2)}) copy-start(bf16[256,1024]{1,0:T(8,128)(2,1)} %param.8) | copy-start | bytes 1572868
  9.7 153.6 %all-gather.7.cloned.1.call-start = ((), (), s32[]{:S(2)}) async-start(), calls=%async_computation.4 | async-start | bytes 8912896 | tf_op jit(solution)/shard_map/all_gather | solution.py:11
  108.7 75.9 %all-to-all-start = ((bf16[16,64,256]{2,1,0:T(8,128)(2,1)}), bf16[16,64,256]{2,1,0:T(8,128)(2,1)}, u32[]{:S(2)}, u32[]{:S(2)}) async-start(bf16[16,64,256]{2,1,0:T(8,128)(2,1)} %bitcast.9), calls=%async_computation | async-start | bytes 1048576 | tf_op jit(solution)/shard_map/all_to_all | solution.py:78
  163.3 20.2 %copy-start.1 = (f32[8,128,256]{2,1,0:T(8,128)S(1)}, f32[8,128,256]{2,1,0:T(8,128)}, u32[]{:S(2)}) copy-start(f32[8,128,256]{2,1,0:T(8,128)} %convolution_bitcast_fusion) | copy-start | bytes 3145732
  184.6 8.2 %copy-start.2 = (bf16[256,1024]{1,0:T(8,128)(2,1)S(1)}, bf16[256,1024]{1,0:T(8,128)(2,1)}, u32[]{:S(2)}) copy-start(bf16[256,1024]{1,0:T(8,128)(2,1)} %param.9) | copy-start | bytes 1572868
  184.6 19.0 %all-to-all-start.1 = ((bf16[16,64,256]{2,1,0:T(8,128)(2,1)}), bf16[16,64,256]{2,1,0:T(8,128)(2,1)S(1)}, u32[]{:S(2)}, u32[]{:S(2)}) async-start(bf16[16,64,256]{2,1,0:T(8,128)(2,1)} %bitcast.99), calls=%async_computation.1 | async-start | bytes 1048576 | tf_op jit(solution)/shard_map/all_to_all | solution.py:79
  203.6 18.5 %all-to-all-start.2 = ((bf16[16,64,256]{2,1,0:T(8,128)(2,1)}), bf16[16,64,256]{2,1,0:T(8,128)(2,1)S(1)}, u32[]{:S(2)}, u32[]{:S(2)}) async-start(bf16[16,64,256]{2,1,0:T(8,128)(2,1)} %bitcast.19), calls=%async_computation.2 | async-start | bytes 1048576 | tf_op jit(solution)/shard_map/all_to_all | solution.py:80
Sparse Core Ops, SparseCore 0:
  10.8 75.5 all-gather.4
  89.1 74.1 all-gather.6
where the time goes:
time: 234 us; the launch traced here: 230 us
  waiting for transfers between devices  140 us (60%)
  other arithmetic  39.4 us (17%)
  starting transfers between devices  16.5 us (7%)
  between operations  14.2 us (6%)
  matrix products  14 us (6%)
  local copies, waits for them, and re-layouts  5.19 us (2%)
    all_gather x2, waiting for transfers between devices, entering(): everything = lax.all_gather(shard, axis)  121 us
    select_n x32, other arithmetic, lap(): return jnp.where(reached, new, before)  39.4 us
    all_to_all x1, waiting for transfers between devices, body(): lax.all_to_all(value_rows, 'seq', split_axis=0, concat_axis=1, tiled=True)  10.5 us
    all_to_all x1, waiting for transfers between devices, body(): lax.all_to_all(key_rows, 'seq', split_axis=0, concat_axis=1, tiled=True)  8.15 us
    all_to_all x1, starting transfers between devices, body(): lax.all_to_all(key_rows, 'seq', split_axis=0, concat_axis=1, tiled=True)  5.81 us
    all_to_all x1, starting transfers between devices, body(): lax.all_to_all(value_rows, 'seq', split_axis=0, concat_axis=1, tiled=True)  5.34 us
    all_to_all x1, starting transfers between devices, body(): lax.all_to_all(query_rows, 'seq', split_axis=0, concat_axis=1, tiled=True)  5.32 us
  transfers between devices with their start and end apart: 5, of which 4 were waited for; matrix products, arithmetic and copies ran while one was open for 24% of the time, Pallas kernels for 0%

commit v1 on v0

v1 whole, which is shorter than its diff:
```python
import functools

import jax
import jax.numpy as jnp
from jax import lax
from jax.experimental import pallas as pl
from jax.experimental.pallas import tpu as pltpu
from jax.sharding import PartitionSpec as P

HDIM = 128
CORES = 2


def dot(a, b, contract):
    return lax.dot_general(a, b, (contract, ((), ())), preferred_element_type=jnp.float32)


NN = ((1,), (0,))
NT = ((1,), (1,))
TN = ((0,), (0,))


def entering(shard, axis, reverse):
    size, position = lax.axis_size(axis), lax.axis_index(axis)
    everything = lax.all_gather(shard, axis)
    start = jnp.zeros_like(shard)

    def lap(k, before):
        at = size - 1 - k if reverse else k
        reached = at > position if reverse else at < position
        return jnp.where(reached, before + everything[at], before)

    return lax.fori_loop(0, size, lap, start)


def general_body(queries, keys, values, grad_out):
    length = queries.shape[0]
    head_count = queries.shape[1] // HDIM
    split = lambda x: jnp.transpose(x.reshape(length, head_count, HDIM), (1, 0, 2))
    q, k, v, g = split(queries), split(keys), split(values), split(grad_out)
    einsum = functools.partial(jnp.einsum, preferred_element_type=jnp.float32)
    positions = lax.iota(jnp.int32, length)
    causal = positions[:, None] >= positions[None, :]
    scores_qk = jnp.where(causal[None], einsum("htd,hsd->hts", q, k), 0.0).astype(jnp.bfloat16)
    scores_gv = jnp.where(causal[None], einsum("htd,hsd->hts", g, v), 0.0).astype(jnp.bfloat16)
    state_half = entering(einsum("hsd,hse->hde", k, v), "seq", False).astype(jnp.bfloat16)
    grad_half = entering(einsum("htf,htb->hfb", q, g), "seq", True).astype(jnp.bfloat16)
    grad_q = einsum("hsd,hts->hdt", k, scores_gv) + einsum("hdv,htv->hdt", state_half, g)
    grad_k = einsum("htd,hts->hds", q, scores_gv) + einsum("hdv,hsv->hds", grad_half, v)
    grad_v = einsum("htd,hts->hds", g, scores_qk) + einsum("hfb,hsf->hbs", grad_half, k)
    width = head_count * HDIM
    rows = [x.reshape(width, length).astype(jnp.bfloat16) for x in (grad_q, grad_k, grad_v)]
    return tuple(lax.all_to_all(x, "seq", split_axis=0, concat_axis=1, tiled=True) for x in rows)


def pack_kernel(flips, tensors, meta, *refs):
    ins, outs, sems = refs[:tensors], refs[tensors:-1], refs[-1]
    copies = []
    for i, flip in enumerate(flips):
        head = meta[0] ^ flip
        for t in range(tensors):
            columns = pl.ds(pl.multiple_of(head * HDIM, HDIM), HDIM)
            copies.append(
                pltpu.make_async_copy(ins[t].at[:, columns], outs[i].at[t], sems.at[i, t])
            )
    for copy in copies:
        copy.start()
    for copy in copies:
        copy.wait()


def pack(meta, flips, arrays):
    length, tensors = arrays[0].shape[0], len(arrays)
    shape = jax.ShapeDtypeStruct((tensors, length, HDIM), arrays[0].dtype)
    any_spec = pl.BlockSpec(memory_space=pl.ANY)
    return pl.pallas_call(
        functools.partial(pack_kernel, flips, tensors),
        out_shape=[shape] * len(flips),
        in_specs=[pl.BlockSpec(memory_space=pltpu.SMEM)] + [any_spec] * tensors,
        out_specs=[any_spec] * len(flips),
        scratch_shapes=[pltpu.SemaphoreType.DMA((len(flips), tensors))],
    )(meta, *arrays)


def attend_kernel(chips, length, meta, *refs):
    n_blocks = chips * CORES
    blocks = refs[:n_blocks]
    out_q, out_k, out_v = refs[n_blocks : n_blocks + 3]
    states, grads, state_half, grad_half, intra, turned = refs[n_blocks + 3 :]
    chip, core = meta[0], meta[1]
    half = HDIM // CORES
    own_rows = pl.ds(pl.multiple_of(core * half, half), half)
    row = lax.broadcasted_iota(jnp.int32, (length, length), 0)
    column = lax.broadcasted_iota(jnp.int32, (length, length), 1)
    causal = row >= column

    def block_of(slot):
        flip, other = slot // CORES, slot % CORES
        return (chip ^ flip) * CORES + (core ^ other)

    for slot in range(n_blocks):
        at = block_of(slot)
        q, k, v, g = (blocks[slot][t] for t in range(4))
        scores_gv = jnp.where(causal, dot(g, v, NT), 0.0).astype(jnp.bfloat16)
        scores_qk = jnp.where(causal, dot(q, k, NT), 0.0).astype(jnp.bfloat16)
        turned[0] = k.T
        turned[1] = q.T
        turned[2] = g.T
        states[at] = dot(turned[0], v, NN)
        grads[at] = dot(turned[1], g, NN)
        intra[slot, 0] = dot(turned[0, own_rows, :], scores_gv, NT)
        intra[slot, 1] = dot(turned[1, own_rows, :], scores_gv, NN)
        intra[slot, 2] = dot(turned[2, own_rows, :], scores_qk, NN)

    total = jnp.zeros((HDIM, HDIM), jnp.float32)
    for b in range(n_blocks):
        state_half[b] = total.astype(jnp.bfloat16)
        total = total + states[b]
    total = jnp.zeros((HDIM, HDIM), jnp.float32)
    for b in reversed(range(n_blocks)):
        grad_half[b, 0] = total.astype(jnp.bfloat16)
        grad_half[b, 1] = total.T.astype(jnp.bfloat16)
        total = total + grads[b]

    for slot in range(n_blocks):
        at = block_of(slot)
        k, v, g = (blocks[slot][t] for t in range(1, 4))
        columns = pl.ds(pl.multiple_of(at * length, length), length)
        out_q[:, columns] = (
            intra[slot, 0] + dot(state_half[at, own_rows, :], g, NT)
        ).astype(out_q.dtype)
        out_k[:, columns] = (
            intra[slot, 1] + dot(grad_half[at, 0, own_rows, :], v, NT)
        ).astype(out_k.dtype)
        out_v[:, columns] = (
            intra[slot, 2] + dot(grad_half[at, 1, own_rows, :], k, NT)
        ).astype(out_v.dtype)


def attend(meta, blocks):
    n_blocks = len(blocks)
    length = blocks[0].shape[1]
    half = HDIM // CORES
    vmem = pl.BlockSpec(memory_space=pltpu.VMEM)
    out = jax.ShapeDtypeStruct((half, n_blocks * length), jnp.bfloat16)
    square = (n_blocks, HDIM, HDIM)
    return pl.pallas_call(
        functools.partial(attend_kernel, n_blocks // CORES, length),
        out_shape=[out] * 3,
        in_specs=[pl.BlockSpec(memory_space=pltpu.SMEM)] + [vmem] * n_blocks,
        out_specs=[vmem] * 3,
        scratch_shapes=[
            pltpu.VMEM(square, jnp.float32),
            pltpu.VMEM(square, jnp.float32),
            pltpu.VMEM(square, jnp.bfloat16),
            pltpu.VMEM((n_blocks, 2, HDIM, HDIM), jnp.bfloat16),
            pltpu.VMEM((n_blocks, 3, half, length), jnp.float32),
            pltpu.VMEM((3, HDIM, length), jnp.bfloat16),
        ],
        compiler_params=pltpu.CompilerParams(vmem_limit_bytes=40 * 1024 * 1024),
    )(meta, *blocks)


def chip_body(queries, keys, values, grad_out):
    size, position = lax.axis_size("seq"), lax.axis_index("seq")
    chips = size // CORES
    meta = jnp.stack([position // CORES, position % CORES]).astype(jnp.int32)
    arrays = (queries, keys, values, grad_out)
    order = sorted(range(chips), reverse=True)
    packed = dict(zip(order, pack(meta, order, arrays)))
    flipped = lambda x, flip: lax.ppermute(x, "seq", [(i, i ^ flip) for i in range(size)])
    blocks = {}
    for flip in order:
        mine = flipped(packed[flip], flip * CORES) if flip else packed[flip]
        blocks[flip] = (mine, flipped(mine, 1))
    return tuple(attend(meta, [x for flip in range(chips) for x in blocks[flip]]))


def solution(mesh):
    in_specs = (P(("groups", "seq"), None),) * 4
    out_specs = (P("seq", "groups"),) * 3

    def body(queries, keys, values, grad_out):
        heads = queries.shape[1] // HDIM
        chosen = chip_body if mesh.shape["seq"] == heads * CORES else general_body
        return chosen(queries, keys, values, grad_out)

    return jax.shard_map(body, mesh=mesh, in_specs=in_specs, out_specs=out_specs, check_vma=False)
```

time: 234 us -> 130 us (0.56); the launches traced: 230 us -> 130 us
  waiting for transfers between devices: 140 us -> 25.2 us
  Pallas kernels: 0 us -> 72.6 us
  other arithmetic: 39.4 us -> 0.61 us
  matrix products: 14 us -> 0 us
  starting transfers between devices: 16.5 us -> 30.1 us
  between operations: 14.2 us -> 0.67 us
  local copies, waits for them, and re-layouts: 5.19 us -> 0.95 us
    all_gather x2 -> x0, waiting for transfers between devices: 121 us -> none  [entering(): everything = lax.all_gather(shard, axis)]
    pallas_call x0 -> x2, Pallas kernels: none -> 72.6 us  [the longest x1 65.6 us: pack(): pl.pallas_call(functools.partial(pack_kernel, flips, tensors), out_shape=...]
    select_n x32 -> x0, other arithmetic: 39.4 us -> none  [lap(): return jnp.where(reached, new, before)]
    ppermute x0 -> x15, starting transfers between devices: none -> 30.1 us  [chip_body(): lax.ppermute(x, 'seq', [(i, i ^ flip) for i in range(size)])]
    ppermute x0 -> x15, waiting for transfers between devices: none -> 25.2 us  [chip_body(): lax.ppermute(x, 'seq', [(i, i ^ flip) for i in range(size)])]
    all_to_all x3 -> x0, waiting for transfers between devices: 18.6 us -> none  [the longest x1 10.5 us: body(): lax.all_to_all(value_rows, 'seq', split_axis=0, concat_axis=1, tiled=True)]
    all_to_all x3 -> x0, starting transfers between devices: 16.5 us -> none  [the longest x1 5.81 us: body(): lax.all_to_all(key_rows, 'seq', split_axis=0, concat_axis=1, tiled=True)]
    dot_general x9 -> x0, matrix products: 14 us -> none  [the longest x1 2.67 us: body(): jnp.einsum('htd,hts->hds', gradient_heads, masked_query_key, preferred_el...]
  transfers between devices with their start and end apart: 5 -> 15, of which waited for: 4 -> 10; matrix products, arithmetic and copies ran while one was open for 24% -> 0% of each run, Pallas kernels for 0% -> 0%
where the time goes in v1:
time: 130 us
  Pallas kernels  72.6 us (56%)
  starting transfers between devices  30.1 us (23%)
  waiting for transfers between devices  25.2 us (19%)
    pallas_call x1, Pallas kernels, pack(): pl.pallas_call(functools.partial(pack_kernel, flips, tensors), out_shape=...  65.6 us
    ppermute x15, starting transfers between devices, chip_body(): lax.ppermute(x, 'seq', [(i, i ^ flip) for i in range(size)])  30.1 us
    ppermute x15, waiting for transfers between devices, chip_body(): lax.ppermute(x, 'seq', [(i, i ^ flip) for i in range(size)])  25.2 us
    pallas_call x1, Pallas kernels, attend(): pl.pallas_call(functools.partial(attend_kernel, n_blocks // CORES, length...  7.02 us
  transfers between devices with their start and end apart: 15, of which 10 were waited for; matrix products, arithmetic and copies ran while one was open for 0% of the time, Pallas kernels for 0%

profile of v1, /device:TPU:19, one launch (start us, length us, event | category | flops | bytes accessed | tf_op | source)
XLA Modules:
  0.0 130.1 jit_solution(7376925716171600907)
XLA Ops:
  0.6 0.6 pad_add_fusion.meta
  1.3 65.6 %shard_map.67 = (bf16[4,256,128]{2,1,0:T(8,128)(2,1)}, bf16[4,256,128]{2,1,0:T(8,128)(2,1)}, bf16[4,256,128]{2,1,0:T(8,128)(2,1)}, bf16[4,256,128]{2,1,0:T(8,128...) custom-call(s32[2]{0:T(128)} %pad_add_fusion.meta, ...), custom_call_target="tpu_custom_call" | custom-call | tf_op jit(solution)/shard_map/pallas_call | solution.py:76
  66.8 1.3 %collective-permute-start.1 = (bf16[4,256,128]{2,1,0:T(8,128)(2,1)}, bf16[4,256,128]{2,1,0:T(8,128)(2,1)S(1)}, u32[]{:S(2)}, u32[]{:S(2)}) collective-permute-start(bf16[4,256,128]{2,1,0:T(8,128)(2,1)} %get-tuple-element.12), channel_id=1, source_target_pairs={{0,2},{1,3},{2,0},{3,1},{4,6},{5,7},{6,4},{7,5},{8,10},{9,11},{10,... | collective-permute-start | bytes 786440 | tf_op jit(solution)/shard_map/ppermute | solution.py:171
  68.1 1.3 collective-permute-start.3
  69.4 0.1 collective-permute-start.5
  69.6 0.1 collective-permute-start.7
  69.6 3.3 %collective-permute-start.9 = (bf16[4,256,128]{2,1,0:T(8,128)(2,1)}, bf16[4,256,128]{2,1,0:T(8,128)(2,1)S(1)}, u32[]{:S(2)}, u32[]{:S(2)}) collective-permute-start(bf16[4,256,128]{2,1,0:T(8,128)(2,1)} %get-tuple-element.16), channel_id=1, source_target_pairs={{0,10},{1,11},{2,8},{3,9},{4,14},{5,15},{6,12},{7,13},{8,2},{9,3},... | collective-permute-start | bytes 786440 | tf_op jit(solution)/shard_map/ppermute | solution.py:171
  72.9 1.4 %collective-permute-done.1.refs_2_ = bf16[4,256,128]{2,1,0:T(8,128)(2,1)S(1)} collective-permute-done((bf16[4,256,128]{2,1,0:T(8,128)(2,1)}, bf16[4,256,128]{2,1,0:T(8,128)(2,1)S(1)}, u32[]{:S(2)}, u32[]{:S(2)}) %collective-permute-start.1) | collective-permute-done | bytes 262176 | tf_op jit(solution)/shard_map/ppermute | solution.py:171
  74.3 0.2 collective-permute-start.11
  74.5 8.4 %collective-permute-done.3.refs_4_ = bf16[4,256,128]{2,1,0:T(8,128)(2,1)S(1)} collective-permute-done((bf16[4,256,128]{2,1,0:T(8,128)(2,1)}, bf16[4,256,128]{2,1,0:T(8,128)(2,1)S(1)}, u32[]{:S(2)}, u32[]{:S(2)}) %collective-permute-start.3) | collective-permute-done | bytes 262176 | tf_op jit(solution)/shard_map/ppermute | solution.py:171
  82.9 5.9 %collective-permute-done.5.refs_6_ = bf16[4,256,128]{2,1,0:T(8,128)(2,1)S(1)} collective-permute-done((bf16[4,256,128]{2,1,0:T(8,128)(2,1)}, bf16[4,256,128]{2,1,0:T(8,128)(2,1)S(1)}, u32[]{:S(2)}, u32[]{:S(2)}) %collective-permute-start.5) | collective-permute-done | bytes 262176 | tf_op jit(solution)/shard_map/ppermute | solution.py:171
  88.8 1.9 %collective-permute-start = (bf16[4,256,128]{2,1,0:T(8,128)(2,1)}, bf16[4,256,128]{2,1,0:T(8,128)(2,1)S(1)}, u32[]{:S(2)}, u32[]{:S(2)}) collective-permute-start(bf16[4,256,128]{2,1,0:T(8,128)(2,1)} %get-tuple-element.11.refs_0_), channel_id=1, source_target_pairs={{0,1},{1,0},{2,3},{3,2},{4,5},{5,4},{6,7},{7,6},{8,9},{9,8},{10,11... | collective-permute-start | bytes 786440 | tf_op jit(solution)/shard_map/ppermute | solution.py:171
  90.7 0.0 collective-permute-done.7.refs_8_
  90.7 0.0 collective-permute-start.2
  90.7 1.3 collective-permute-done.9.refs_10_
  91.9 14.6 %collective-permute-start.4 = (bf16[4,256,128]{2,1,0:T(8,128)(2,1)S(1)}, bf16[4,256,128]{2,1,0:T(8,128)(2,1)S(1)}, u32[]{:S(2)}, u32[]{:S(2)}) collective-permute-start(bf16[4,256,128]{2,1,0:T(8,128)(2,1)S(1)} %collective-permute-done.3.refs_4_), channel_id=1, source_target_pairs={{0,1},{1,0},{2,3},{3,2},{4,5},{5,4},{6,7},{7,6},{8,9},{9,8},{10,11... | collective-permute-start | bytes 786440 | tf_op jit(solution)/shard_map/ppermute | solution.py:171
  106.6 4.3 %collective-permute-done.11.refs_12_ = bf16[4,256,128]{2,1,0:T(8,128)(2,1)S(1)} collective-permute-done((bf16[4,256,128]{2,1,0:T(8,128)(2,1)}, bf16[4,256,128]{2,1,0:T(8,128)(2,1)S(1)}, u32[]{:S(2)}, u32[]{:S(2)}) %collective-permute-start.11) | collective-permute-done | bytes 262176 | tf_op jit(solution)/shard_map/ppermute | solution.py:171
  110.9 4.4 %collective-permute-start.6 = (bf16[4,256,128]{2,1,0:T(8,128)(2,1)S(1)}, bf16[4,256,128]{2,1,0:T(8,128)(2,1)S(1)}, u32[]{:S(2)}, u32[]{:S(2)}) collective-permute-start(bf16[4,256,128]{2,1,0:T(8,128)(2,1)S(1)} %collective-permute-done.5.refs_6_), channel_id=1, source_target_pairs={{0,1},{1,0},{2,3},{3,2},{4,5},{5,4},{6,7},{7,6},{8,9},{9,8},{10,11... | collective-permute-start | bytes 786440 | tf_op jit(solution)/shard_map/ppermute | solution.py:171
  115.2 2.2 %collective-permute-done.13.refs_14_ = bf16[4,256,128]{2,1,0:T(8,128)(2,1)S(1)} collective-permute-done((bf16[4,256,128]{2,1,0:T(8,128)(2,1)}, bf16[4,256,128]{2,1,0:T(8,128)(2,1)S(1)}, u32[]{:S(2)}, u32[]{:S(2)}) %collective-permute-start.13) | collective-permute-done | bytes 262176 | tf_op jit(solution)/shard_map/ppermute | solution.py:171
  117.4 2.4 %collective-permute-start.8 = (bf16[4,256,128]{2,1,0:T(8,128)(2,1)S(1)}, bf16[4,256,128]{2,1,0:T(8,128)(2,1)S(1)}, u32[]{:S(2)}, u32[]{:S(2)}) collective-permute-start(bf16[4,256,128]{2,1,0:T(8,128)(2,1)S(1)} %collective-permute-done.7.refs_8_), channel_id=1, source_target_pairs={{0,1},{1,0},{2,3},{3,2},{4,5},{5,4},{6,7},{7,6},{8,9},{9,8},{10,11... | collective-permute-start | bytes 786440 | tf_op jit(solution)/shard_map/ppermute | solution.py:171
  119.8 0.0 collective-permute-done.refs_1_
  119.8 0.0 collective-permute-start.10
  119.8 0.0 collective-permute-done.2.refs_3_
  119.8 0.5 collective-permute-start.12
  120.3 0.0 collective-permute-done.4.refs_5_
  120.4 0.1 collective-permute-start.14
  120.4 0.6 collective-permute-done.8.refs_9_
  121.0 0.4 collective-permute-done.10.refs_11_
  121.4 0.4 collective-permute-done.12.refs_13_
  121.7 0.4 collective-permute-done.14.refs_15_
  122.1 0.9 copy-done
  123.1 7.0 %shard_map.68 = (bf16[64,4096]{1,0:T(8,128)(2,1)}, bf16[64,4096]{1,0:T(8,128)(2,1)}, bf16[64,4096]{1,0:T(8,128)(2,1)}) custom-call(s32[2]{0:T(128)S(1)} %copy-done.1, bf16[4,256,128]{2,1,0:T(8,128)(2,1)S(1)} %copy-done, bf16[4,256,128]{2,1,0:T(8,128)(2,1)S(1)} %collective-permute-done.refs_1_, bf16[4,256,128]{2,1,0:T(8,128)(2,1)S(1)} %collective-permute-done.1.refs_2_, ...), custom_call_target="tpu_custom_call" | custom-call | tf_op jit(solution)/shard_map/pallas_call | solution.py:147
  (5 shorter events, 0.0 us)
Async XLA Ops:
  66.8 7.5 %collective-permute-start.1 = (bf16[4,256,128]{2,1,0:T(8,128)(2,1)}, bf16[4,256,128]{2,1,0:T(8,128)(2,1)S(1)}, u32[]{:S(2)}, u32[]{:S(2)}) collective-permute-start(bf16[4,256,128]{2,1,0:T(8,128)(2,1)} %get-tuple-element.12), channel_id=1, source_target_pairs={{0,2},{1,3},{2,0},{3,1},{4,6},{5,7},{6,4},{7,5},{8,10},{9,11},{10,... | collective-permute-start | bytes 786440 | tf_op jit(solution)/shard_map/ppermute | solution.py:171
  68.1 14.8 %collective-permute-start.3 = (bf16[4,256,128]{2,1,0:T(8,128)(2,1)}, bf16[4,256,128]{2,1,0:T(8,128)(2,1)S(1)}, u32[]{:S(2)}, u32[]{:S(2)}) collective-permute-start(bf16[4,256,128]{2,1,0:T(8,128)(2,1)} %get-tuple-element.13), channel_id=1, source_target_pairs={{0,4},{1,5},{2,6},{3,7},{4,0},{5,1},{6,2},{7,3},{8,12},{9,13},{10,... | collective-permute-start | bytes 786440 | tf_op jit(solution)/shard_map/ppermute | solution.py:171
  69.4 19.3 %collective-permute-start.5 = (bf16[4,256,128]{2,1,0:T(8,128)(2,1)}, bf16[4,256,128]{2,1,0:T(8,128)(2,1)S(1)}, u32[]{:S(2)}, u32[]{:S(2)}) collective-permute-start(bf16[4,256,128]{2,1,0:T(8,128)(2,1)} %get-tuple-element.14), channel_id=1, source_target_pairs={{0,6},{1,7},{2,4},{3,5},{4,2},{5,3},{6,0},{7,1},{8,14},{9,15},{10,... | collective-permute-start | bytes 786440 | tf_op jit(solution)/shard_map/ppermute | solution.py:171
  69.6 21.1 %collective-permute-start.7 = (bf16[4,256,128]{2,1,0:T(8,128)(2,1)}, bf16[4,256,128]{2,1,0:T(8,128)(2,1)S(1)}, u32[]{:S(2)}, u32[]{:S(2)}) collective-permute-start(bf16[4,256,128]{2,1,0:T(8,128)(2,1)} %get-tuple-element.15), channel_id=1, source_target_pairs={{0,8},{1,9},{2,10},{3,11},{4,12},{5,13},{6,14},{7,15},{8,0},{9,1},... | collective-permute-start | bytes 786440 | tf_op jit(solution)/shard_map/ppermute | solution.py:171
  69.6 22.3 %collective-permute-start.9 = (bf16[4,256,128]{2,1,0:T(8,128)(2,1)}, bf16[4,256,128]{2,1,0:T(8,128)(2,1)S(1)}, u32[]{:S(2)}, u32[]{:S(2)}) collective-permute-start(bf16[4,256,128]{2,1,0:T(8,128)(2,1)} %get-tuple-element.16), channel_id=1, source_target_pairs={{0,10},{1,11},{2,8},{3,9},{4,14},{5,15},{6,12},{7,13},{8,2},{9,3},... | collective-permute-start | bytes 786440 | tf_op jit(solution)/shard_map/ppermute | solution.py:171
  74.3 36.6 %collective-permute-start.11 = (bf16[4,256,128]{2,1,0:T(8,128)(2,1)}, bf16[4,256,128]{2,1,0:T(8,128)(2,1)S(1)}, u32[]{:S(2)}, u32[]{:S(2)}) collective-permute-start(bf16[4,256,128]{2,1,0:T(8,128)(2,1)} %get-tuple-element.17), channel_id=1, source_target_pairs={{0,12},{1,13},{2,14},{3,15},{4,8},{5,9},{6,10},{7,11},{8,4},{9,5},... | collective-permute-start | bytes 786440 | tf_op jit(solution)/shard_map/ppermute | solution.py:171
  82.9 39.2 %copy-start.1 = (s32[2]{0:T(128)S(1)}, s32[2]{0:T(128)}, u32[]{:S(2)}) copy-start(s32[2]{0:T(128)} %pad_add_fusion.meta) | copy-start | bytes 28
  82.9 34.5 %collective-permute-start.13 = (bf16[4,256,128]{2,1,0:T(8,128)(2,1)}, bf16[4,256,128]{2,1,0:T(8,128)(2,1)S(1)}, u32[]{:S(2)}, u32[]{:S(2)}) collective-permute-start(bf16[4,256,128]{2,1,0:T(8,128)(2,1)} %get-tuple-element.18), channel_id=1, source_target_pairs={{0,14},{1,15},{2,12},{3,13},{4,10},{5,11},{6,8},{7,9},{8,6},{9,7},... | collective-permute-start | bytes 786440 | tf_op jit(solution)/shard_map/ppermute | solution.py:171
  88.8 31.0 %collective-permute-start = (bf16[4,256,128]{2,1,0:T(8,128)(2,1)}, bf16[4,256,128]{2,1,0:T(8,128)(2,1)S(1)}, u32[]{:S(2)}, u32[]{:S(2)}) collective-permute-start(bf16[4,256,128]{2,1,0:T(8,128)(2,1)} %get-tuple-element.11.refs_0_), channel_id=1, source_target_pairs={{0,1},{1,0},{2,3},{3,2},{4,5},{5,4},{6,7},{7,6},{8,9},{9,8},{10,11... | collective-permute-start | bytes 786440 | tf_op jit(solution)/shard_map/ppermute | solution.py:171
  90.7 29.2 %collective-permute-start.2 = (bf16[4,256,128]{2,1,0:T(8,128)(2,1)S(1)}, bf16[4,256,128]{2,1,0:T(8,128)(2,1)S(1)}, u32[]{:S(2)}, u32[]{:S(2)}) collective-permute-start(bf16[4,256,128]{2,1,0:T(8,128)(2,1)S(1)} %collective-permute-done.1.refs_2_), channel_id=1, source_target_pairs={{0,1},{1,0},{2,3},{3,2},{4,5},{5,4},{6,7},{7,6},{8,9},{9,8},{10,11... | collective-permute-start | bytes 786440 | tf_op jit(solution)/shard_map/ppermute | solution.py:171
  91.9 28.4 %collective-permute-start.4 = (bf16[4,256,128]{2,1,0:T(8,128)(2,1)S(1)}, bf16[4,256,128]{2,1,0:T(8,128)(2,1)S(1)}, u32[]{:S(2)}, u32[]{:S(2)}) collective-permute-start(bf16[4,256,128]{2,1,0:T(8,128)(2,1)S(1)} %collective-permute-done.3.refs_4_), channel_id=1, source_target_pairs={{0,1},{1,0},{2,3},{3,2},{4,5},{5,4},{6,7},{7,6},{8,9},{9,8},{10,11... | collective-permute-start | bytes 786440 | tf_op jit(solution)/shard_map/ppermute | solution.py:171
  110.9 9.6 %collective-permute-start.6 = (bf16[4,256,128]{2,1,0:T(8,128)(2,1)S(1)}, bf16[4,256,128]{2,1,0:T(8,128)(2,1)S(1)}, u32[]{:S(2)}, u32[]{:S(2)}) collective-permute-start(bf16[4,256,128]{2,1,0:T(8,128)(2,1)S(1)} %collective-permute-done.5.refs_6_), channel_id=1, source_target_pairs={{0,1},{1,0},{2,3},{3,2},{4,5},{5,4},{6,7},{7,6},{8,9},{9,8},{10,11... | collective-permute-start | bytes 786440 | tf_op jit(solution)/shard_map/ppermute | solution.py:171
  117.4 3.6 %collective-permute-start.8 = (bf16[4,256,128]{2,1,0:T(8,128)(2,1)S(1)}, bf16[4,256,128]{2,1,0:T(8,128)(2,1)S(1)}, u32[]{:S(2)}, u32[]{:S(2)}) collective-permute-start(bf16[4,256,128]{2,1,0:T(8,128)(2,1)S(1)} %collective-permute-done.7.refs_8_), channel_id=1, source_target_pairs={{0,1},{1,0},{2,3},{3,2},{4,5},{5,4},{6,7},{7,6},{8,9},{9,8},{10,11... | collective-permute-start | bytes 786440 | tf_op jit(solution)/shard_map/ppermute | solution.py:171
  119.8 1.5 %collective-permute-start.10 = (bf16[4,256,128]{2,1,0:T(8,128)(2,1)S(1)}, bf16[4,256,128]{2,1,0:T(8,128)(2,1)S(1)}, u32[]{:S(2)}, u32[]{:S(2)}) collective-permute-start(bf16[4,256,128]{2,1,0:T(8,128)(2,1)S(1)} %collective-permute-done.9.refs_10_), channel_id=1, source_target_pairs={{0,1},{1,0},{2,3},{3,2},{4,5},{5,4},{6,7},{7,6},{8,9},{9,8},{10,11... | collective-permute-start | bytes 786440 | tf_op jit(solution)/shard_map/ppermute | solution.py:171
  119.8 1.9 %collective-permute-start.12 = (bf16[4,256,128]{2,1,0:T(8,128)(2,1)S(1)}, bf16[4,256,128]{2,1,0:T(8,128)(2,1)S(1)}, u32[]{:S(2)}, u32[]{:S(2)}) collective-permute-start(bf16[4,256,128]{2,1,0:T(8,128)(2,1)S(1)} %collective-permute-done.11.refs_12_), channel_id=1, source_target_pairs={{0,1},{1,0},{2,3},{3,2},{4,5},{5,4},{6,7},{7,6},{8,9},{9,8},{10,11... | collective-permute-start | bytes 786440 | tf_op jit(solution)/shard_map/ppermute | solution.py:171
  120.4 1.8 %collective-permute-start.14 = (bf16[4,256,128]{2,1,0:T(8,128)(2,1)S(1)}, bf16[4,256,128]{2,1,0:T(8,128)(2,1)S(1)}, u32[]{:S(2)}, u32[]{:S(2)}) collective-permute-start(bf16[4,256,128]{2,1,0:T(8,128)(2,1)S(1)} %collective-permute-done.13.refs_14_), channel_id=1, source_target_pairs={{0,1},{1,0},{2,3},{3,2},{4,5},{5,4},{6,7},{7,6},{8,9},{9,8},{10,11... | collective-permute-start | bytes 786440 | tf_op jit(solution)/shard_map/ppermute | solution.py:171
  122.1 1.0 copy-start

commit v2 on v1

v2 whole, which is shorter than its diff:
```python
import functools

import jax
import jax.numpy as jnp
from jax import lax
from jax.experimental import pallas as pl
from jax.experimental.pallas import tpu as pltpu
from jax.sharding import PartitionSpec as P

HDIM = 128
CORES = 2


def dot(a, b, contract):
    return lax.dot_general(a, b, (contract, ((), ())), preferred_element_type=jnp.float32)


NN = ((1,), (0,))
NT = ((1,), (1,))
TN = ((0,), (0,))


def entering(shard, axis, reverse):
    size, position = lax.axis_size(axis), lax.axis_index(axis)
    everything = lax.all_gather(shard, axis)
    start = jnp.zeros_like(shard)

    def lap(k, before):
        at = size - 1 - k if reverse else k
        reached = at > position if reverse else at < position
        return jnp.where(reached, before + everything[at], before)

    return lax.fori_loop(0, size, lap, start)


def general_body(queries, keys, values, grad_out):
    length = queries.shape[0]
    head_count = queries.shape[1] // HDIM
    split = lambda x: jnp.transpose(x.reshape(length, head_count, HDIM), (1, 0, 2))
    q, k, v, g = split(queries), split(keys), split(values), split(grad_out)
    einsum = functools.partial(jnp.einsum, preferred_element_type=jnp.float32)
    positions = lax.iota(jnp.int32, length)
    causal = positions[:, None] >= positions[None, :]
    scores_qk = jnp.where(causal[None], einsum("htd,hsd->hts", q, k), 0.0).astype(jnp.bfloat16)
    scores_gv = jnp.where(causal[None], einsum("htd,hsd->hts", g, v), 0.0).astype(jnp.bfloat16)
    state_half = entering(einsum("hsd,hse->hde", k, v), "seq", False).astype(jnp.bfloat16)
    grad_half = entering(einsum("htf,htb->hfb", q, g), "seq", True).astype(jnp.bfloat16)
    grad_q = einsum("hsd,hts->hdt", k, scores_gv) + einsum("hdv,htv->hdt", state_half, g)
    grad_k = einsum("htd,hts->hds", q, scores_gv) + einsum("hdv,hsv->hds", grad_half, v)
    grad_v = einsum("htd,hts->hds", g, scores_qk) + einsum("hfb,hsf->hbs", grad_half, k)
    width = head_count * HDIM
    rows = [x.reshape(width, length).astype(jnp.bfloat16) for x in (grad_q, grad_k, grad_v)]
    return tuple(lax.all_to_all(x, "seq", split_axis=0, concat_axis=1, tiled=True) for x in rows)


def place():
    position = lax.axis_index("seq")
    return position // CORES, position % CORES


SMALL = pl.CostEstimate(flops=1, transcendentals=0, bytes_accessed=1)


def pack_kernel(flips, tensors, *refs):
    ins, outs, sems = refs[:tensors], refs[tensors:-1], refs[-1]
    chip, _ = place()
    copies = []
    for i, flip in enumerate(flips):
        columns = pl.ds(pl.multiple_of((chip ^ flip) * HDIM, HDIM), HDIM)
        for t in range(tensors):
            copies.append(
                pltpu.make_async_copy(ins[t].at[:, columns], outs[i].at[t], sems.at[i, t])
            )
    for copy in copies:
        copy.start()
    for copy in copies:
        copy.wait()


def pack(flips, arrays):
    length, tensors = arrays[0].shape[0], len(arrays)
    shape = pltpu.VMEM((tensors, length, HDIM), arrays[0].dtype)
    return pl.pallas_call(
        functools.partial(pack_kernel, flips, tensors),
        out_shape=[shape] * len(flips),
        in_specs=[pl.BlockSpec(memory_space=pl.ANY)] * tensors,
        out_specs=[pl.BlockSpec(memory_space=pltpu.VMEM)] * len(flips),
        scratch_shapes=[pltpu.SemaphoreType.DMA((len(flips), tensors))],
        cost_estimate=SMALL,
    )(*arrays)


def within_blocks(blocks, core, turned, states, grads, intra):
    length = blocks[0].shape[1]
    half = HDIM // CORES
    own_rows = pl.ds(pl.multiple_of(core * half, half), half)
    row = lax.broadcasted_iota(jnp.int32, (length, length), 0)
    column = lax.broadcasted_iota(jnp.int32, (length, length), 1)
    causal = row >= column
    for i, block in enumerate(blocks):
        q, k, v, g = (block[t] for t in range(4))
        scores_gv = jnp.where(causal, dot(g, v, NT), 0.0).astype(jnp.bfloat16)
        scores_qk = jnp.where(causal, dot(q, k, NT), 0.0).astype(jnp.bfloat16)
        turned[i, 0] = k.T
        turned[i, 1] = q.T
        turned[i, 2] = g.T
        states[i] = dot(turned[i, 0], v, NN)
        grads[i] = dot(turned[i, 1], g, NN)
        intra[i, 0] = dot(turned[i, 0, own_rows, :], scores_gv, NT)
        intra[i, 1] = dot(turned[i, 1, own_rows, :], scores_gv, NN)
        intra[i, 2] = dot(turned[i, 2, own_rows, :], scores_qk, NN)


def within_shapes(count, length):
    return [
        ((count, HDIM, HDIM), jnp.float32),
        ((count, HDIM, HDIM), jnp.float32),
        ((count, 3, HDIM // CORES, length), jnp.float32),
    ]


def turned_scratch(count, length):
    return pltpu.VMEM((count, 3, HDIM, length), jnp.bfloat16)


VMEM_SPEC = pl.BlockSpec(memory_space=pltpu.VMEM)
PARAMS = pltpu.CompilerParams(vmem_limit_bytes=40 * 1024 * 1024)


def within_kernel(count, *refs):
    _, core = place()
    within_blocks(refs[:count], core, refs[-1], *refs[count:-1])


def within(blocks):
    count, length = len(blocks), blocks[0].shape[1]
    return pl.pallas_call(
        functools.partial(within_kernel, count),
        out_shape=[jax.ShapeDtypeStruct(*s) for s in within_shapes(count, length)],
        in_specs=[VMEM_SPEC] * count,
        out_specs=[VMEM_SPEC] * 3,
        scratch_shapes=[turned_scratch(count, length)],
        cost_estimate=SMALL,
        compiler_params=PARAMS,
    )(*blocks)


def finish_kernel(flips, sizes, *refs):
    n_blocks = sum(sizes)
    blocks = refs[:n_blocks]
    done = [refs[n_blocks + 3 * i : n_blocks + 3 * i + 3] for i in range(len(sizes) - 1)]
    at = n_blocks + 3 * len(done)
    outs, (state_half, grad_half, in_order), last, turned = (
        refs[at : at + 3],
        refs[at + 3 : at + 6],
        refs[at + 6 : at + 9],
        refs[at + 9],
    )
    chip, core = place()
    half, length = HDIM // CORES, blocks[0].shape[1]
    own_rows = pl.ds(pl.multiple_of(core * half, half), half)
    within_blocks(blocks[n_blocks - sizes[-1] :], core, turned, *last)
    done.append(last)

    slots = []
    for size, (states, grads, intra) in zip(sizes, done):
        for i in range(size):
            slot = len(slots)
            b = (chip ^ flips[slot // CORES]) * CORES + (core ^ (slot % CORES))
            in_order[b, 0] = states[i]
            in_order[b, 1] = grads[i]
            slots.append((b, intra.at[i]))

    total = jnp.zeros((HDIM, HDIM), jnp.float32)
    for b in range(n_blocks):
        state_half[b] = total.astype(jnp.bfloat16)
        total = total + in_order[b, 0]
    total = jnp.zeros((HDIM, HDIM), jnp.float32)
    for b in reversed(range(n_blocks)):
        grad_half[b, 0] = total.astype(jnp.bfloat16)
        grad_half[b, 1] = total.T.astype(jnp.bfloat16)
        total = total + in_order[b, 1]

    for block, (b, intra) in zip(blocks, slots):
        k, v, g = (block[t] for t in range(1, 4))
        columns = pl.ds(pl.multiple_of(b * length, length), length)
        across = (
            dot(state_half[b, own_rows, :], g, NT),
            dot(grad_half[b, 0, own_rows, :], v, NT),
            dot(grad_half[b, 1, own_rows, :], k, NT),
        )
        for j, out in enumerate(outs):
            out[:, columns] = (intra[j] + across[j]).astype(out.dtype)


def finish(flips, blocks, done, sizes):
    n_blocks, length = len(blocks), blocks[0].shape[1]
    half = HDIM // CORES
    out = jax.ShapeDtypeStruct((half, n_blocks * length), jnp.bfloat16)
    return pl.pallas_call(
        functools.partial(finish_kernel, flips, sizes),
        out_shape=[out] * 3,
        in_specs=[VMEM_SPEC] * (n_blocks + len(done)),
        out_specs=[VMEM_SPEC] * 3,
        scratch_shapes=[
            pltpu.VMEM((n_blocks, HDIM, HDIM), jnp.bfloat16),
            pltpu.VMEM((n_blocks, 2, HDIM, HDIM), jnp.bfloat16),
            pltpu.VMEM((n_blocks, 2, HDIM, HDIM), jnp.float32),
        ]
        + [pltpu.VMEM(*s) for s in within_shapes(sizes[-1], length)]
        + [turned_scratch(sizes[-1], length)],
        compiler_params=PARAMS,
    )(*blocks, *done)


def after(x, *others):
    return lax.optimization_barrier((x, *others))[0]


def chip_body(queries, keys, values, grad_out):
    size = lax.axis_size("seq")
    chips = size // CORES
    arrays = (queries, keys, values, grad_out)
    near, far = list(range(chips // 2)), list(range(chips // 2, chips))[::-1]
    packed = dict(zip(far, pack(far, arrays))) | dict(zip(near, pack(near, arrays)))
    flipped = lambda x, flip: lax.ppermute(x, "seq", [(i, i ^ flip) for i in range(size)])
    order = [flip for pair in zip(far, near[1:] + [0]) for flip in pair]
    order.remove(0)
    held, before = {0: packed[0]}, []
    for flip in order:
        held[flip] = flipped(packed[flip], flip * CORES)
        held[flip] = after(held[flip], *before)
        before = [held[flip]]
    groups = (near, far[:-1], far[-1:])
    done, sizes, blocks = [], [], []
    for group in groups:
        some = []
        for flip in group:
            mine = after(held[flip], *done)
            some += [mine, flipped(mine, 1)]
        blocks += some
        sizes.append(len(some))
        if group is not groups[-1]:
            done += within(some)
    flips = [flip for group in groups for flip in group]
    return tuple(finish(flips, blocks, done, tuple(sizes)))


def solution(mesh):
    in_specs = (P(("groups", "seq"), None),) * 4
    out_specs = (P("seq", "groups"),) * 3

    def body(queries, keys, values, grad_out):
        heads = queries.shape[1] // HDIM
        chosen = chip_body if mesh.shape["seq"] == heads * CORES else general_body
        return chosen(queries, keys, values, grad_out)

    return jax.shard_map(body, mesh=mesh, in_specs=in_specs, out_specs=out_specs, check_vma=False)
```

time: 130 us -> 63.4 us (0.49)
  the two profiles are of different devices: /device:TPU:19 before, /device:TPU:0 now
where the time goes in v2:
time: 63.4 us; the launch traced here: 63.1 us
  starting transfers between devices  26.6 us (42%)
  waiting for transfers between devices  26 us (41%)
  Pallas kernels  9.81 us (15%)
  between operations  0.67 us (1%)
    ppermute x15, starting transfers between devices, chip_body(): lax.ppermute(x, 'seq', [(i, i ^ flip) for i in range(size)])  26.6 us
    ppermute x15, waiting for transfers between devices, chip_body(): lax.ppermute(x, 'seq', [(i, i ^ flip) for i in range(size)])  26 us
    pallas_call x2, Pallas kernels, within(): pl.pallas_call(functools.partial(within_kernel, count), out_shape=[jax.Sh...  3.87 us
    pallas_call x1, Pallas kernels, finish(): pl.pallas_call(functools.partial(finish_kernel, flips, sizes), out_shape=...  3.12 us
    pallas_call x2, Pallas kernels, pack(): pl.pallas_call(functools.partial(pack_kernel, flips, tensors), out_shape=...  2.82 us
  transfers between devices with their start and end apart: 15, of which 5 were waited for; matrix products, arithmetic and copies ran while one was open for 0% of the time, Pallas kernels for 6%

profile of v2, /device:TPU:0, one launch (start us, length us, event | category | flops | bytes accessed | tf_op | source)
XLA Modules:
  0.0 63.1 jit_solution(5993197163405312592)
XLA Ops:
  0.6 1.4 %shard_map.68 = (bf16[4,256,128]{2,1,0:T(8,128)(2,1)S(1)}, bf16[4,256,128]{2,1,0:T(8,128)(2,1)S(1)}, bf16[4,256,128]{2,1,0:T(8,128)(2,1)S(1)}, bf16[4,256,128]{2,1,0:T(8,128)(2,1)S(1)}) custom-call(bf16[256,1024]{1,0:T(8,128)(2,1)} %refs_0_.3, bf16[256,1024]{1,0:T(8,128)(2,1)} %refs_1_.3, bf16[256,1024]{1,0:T(8,128)(2,1)} %refs_2_.3, bf16[256,1024]{1,0:T(8,128)(2,1)} %refs_3_.3), custom_call_target="tpu_custom_call" | custom-call | flops 1 | bytes 1 | tf_op jit(solution)/shard_map/pallas_call | solution.py:83
  2.1 6.1 %collective-permute-start.2 = (bf16[4,256,128]{2,1,0:T(8,128)(2,1)S(1)}, bf16[4,256,128]{2,1,0:T(8,128)(2,1)S(1)}, u32[]{:S(2)}, u32[]{:S(2)}) collective-permute-start(bf16[4,256,128]{2,1,0:T(8,128)(2,1)S(1)} %get-tuple-element.29), channel_id=1, source_target_pairs={{0,14},{1,15},{2,12},{3,13},{4,10},{5,11},{6,8},{7,9},{8,6},{9,7},... | collective-permute-start | bytes 786440 | tf_op jit(solution)/shard_map/ppermute | solution.py:226
  8.1 1.4 %shard_map.67 = (bf16[4,256,128]{2,1,0:T(8,128)(2,1)S(1)}, bf16[4,256,128]{2,1,0:T(8,128)(2,1)S(1)}, bf16[4,256,128]{2,1,0:T(8,128)(2,1)S(1)}, bf16[4,256,128]{2,1,0:T(8,128)(2,1)S(1)}) custom-call(bf16[256,1024]{1,0:T(8,128)(2,1)} %refs_0_.3, bf16[256,1024]{1,0:T(8,128)(2,1)} %refs_1_.3, bf16[256,1024]{1,0:T(8,128)(2,1)} %refs_2_.3, bf16[256,1024]{1,0:T(8,128)(2,1)} %refs_3_.3), custom_call_target="tpu_custom_call" | custom-call | flops 1 | bytes 1 | tf_op jit(solution)/shard_map/pallas_call | solution.py:83
  9.5 0.6 collective-permute-start.1
  10.1 0.1 collective-permute-start.5
  10.2 0.0 collective-permute-start.4
  10.2 5.2 %collective-permute-start.8 = (bf16[4,256,128]{2,1,0:T(8,128)(2,1)S(1)}, bf16[4,256,128]{2,1,0:T(8,128)(2,1)S(1)}, u32[]{:S(2)}, u32[]{:S(2)}) collective-permute-start(bf16[4,256,128]{2,1,0:T(8,128)(2,1)S(1)} %get-tuple-element.36), channel_id=1, source_target_pairs={{0,10},{1,11},{2,8},{3,9},{4,14},{5,15},{6,12},{7,13},{8,2},{9,3},... | collective-permute-start | bytes 786440 | tf_op jit(solution)/shard_map/ppermute | solution.py:226
  15.5 0.0 collective-permute-done.2.refs_0_.refs_8_
  15.5 12.8 %collective-permute-start.7 = (bf16[4,256,128]{2,1,0:T(8,128)(2,1)S(1)}, bf16[4,256,128]{2,1,0:T(8,128)(2,1)S(1)}, u32[]{:S(2)}, u32[]{:S(2)}) collective-permute-start(bf16[4,256,128]{2,1,0:T(8,128)(2,1)S(1)} %get-tuple-element.35), channel_id=1, source_target_pairs={{0,6},{1,7},{2,4},{3,5},{4,2},{5,3},{6,0},{7,1},{8,14},{9,15},{10,... | collective-permute-start | bytes 786440 | tf_op jit(solution)/shard_map/ppermute | solution.py:226
  28.3 0.0 collective-permute-done.1.refs_2_
  28.3 0.0 collective-permute-start
  28.3 0.0 collective-permute-done.5.refs_2_.refs_10_
  28.3 0.5 collective-permute-start.3
  28.8 0.0 collective-permute-done.4.refs_4_
  28.8 12.8 %collective-permute-done.8.refs_4_.refs_12_ = bf16[4,256,128]{2,1,0:T(8,128)(2,1)S(1)} collective-permute-done((bf16[4,256,128]{2,1,0:T(8,128)(2,1)S(1)}, bf16[4,256,128]{2,1,0:T(8,128)(2,1)S(1)}, u32[]{:S(2)}, u32[]{:S(2)}) %collective-permute-start.8) | collective-permute-done | bytes 262176 | tf_op jit(solution)/shard_map/ppermute | solution.py:226
  41.6 0.0 collective-permute-start.6
  41.6 0.0 collective-permute-done.7.refs_6_
  41.6 0.5 collective-permute-start.9
  42.1 0.0 collective-permute-done.refs_1_
  42.1 0.0 collective-permute-done.3.refs_3_
  42.1 1.0 %collective-permute-done.6.refs_5_ = bf16[4,256,128]{2,1,0:T(8,128)(2,1)S(1)} collective-permute-done((bf16[4,256,128]{2,1,0:T(8,128)(2,1)S(1)}, bf16[4,256,128]{2,1,0:T(8,128)(2,1)S(1)}, u32[]{:S(2)}, u32[]{:S(2)}) %collective-permute-start.6) | collective-permute-done | bytes 262176 | tf_op jit(solution)/shard_map/ppermute | solution.py:226
  43.2 0.4 collective-permute-done.9.refs_7_
  43.5 2.2 %shard_map.69 = (f32[8,128,128]{2,1,0:T(8,128)S(1)}, f32[8,128,128]{2,1,0:T(8,128)S(1)}, f32[8,3,64,256]{3,2,1,0:T(8,128)S(1)}) custom-call(bf16[4,256,128]{2,1,0:T(8,128)(2,1)S(1)} %get-tuple-element.27.refs_0_, bf16[4,256,128]{2,1,0:T(8,128)(2,1)S(1)} %collective-permute-done.refs_1_, bf16[4,256,128]{2,1,0:T(8,128)(2,1)S(1)} %collective-permute-done.1.refs_2_, ...), custom_call_target="tpu_custom_call" | custom-call | flops 1 | bytes 1 | tf_op jit(solution)/shard_map/pallas_call | solution.py:137
  45.7 0.2 collective-permute-start.10
  45.9 0.4 collective-permute-start.11
  46.3 0.1 collective-permute-start.12
  46.4 10.3 %collective-permute-done.13.refs_14_ = bf16[4,256,128]{2,1,0:T(8,128)(2,1)S(1)} collective-permute-done((bf16[4,256,128]{2,1,0:T(8,128)(2,1)S(1)}, bf16[4,256,128]{2,1,0:T(8,128)(2,1)S(1)}, u32[]{:S(2)}, u32[]{:S(2)}) %collective-permute-start.13) | collective-permute-done | bytes 262176 | tf_op jit(solution)/shard_map/ppermute | solution.py:226
  56.7 0.0 collective-permute-done.12.refs_5_.refs_13_
  56.7 1.7 %shard_map.70 = (f32[6,128,128]{2,1,0:T(8,128)S(1)}, f32[6,128,128]{2,1,0:T(8,128)S(1)}, f32[6,3,64,256]{3,2,1,0:T(8,128)S(1)}) custom-call(bf16[4,256,128]{2,1,0:T(8,128)(2,1)S(1)} %collective-permute-done.2.refs_0_.refs_8_, bf16[4,256,128]{2,1,0:T(8,128)(2,1)S(1)} %collective-permute-done.10.refs_1_.refs_9_, ...), custom_call_target="tpu_custom_call" | custom-call | flops 1 | bytes 1 | tf_op jit(solution)/shard_map/pallas_call | solution.py:137
  58.4 0.1 collective-permute-start.14
  58.5 1.5 %collective-permute-done.14.refs_15_ = bf16[4,256,128]{2,1,0:T(8,128)(2,1)S(1)} collective-permute-done((bf16[4,256,128]{2,1,0:T(8,128)(2,1)S(1)}, bf16[4,256,128]{2,1,0:T(8,128)(2,1)S(1)}, u32[]{:S(2)}, u32[]{:S(2)}) %collective-permute-start.14) | collective-permute-done | bytes 262176 | tf_op jit(solution)/shard_map/ppermute | solution.py:226
  60.0 3.1 %shard_map.71 = (bf16[64,4096]{1,0:T(8,128)(2,1)}, bf16[64,4096]{1,0:T(8,128)(2,1)}, bf16[64,4096]{1,0:T(8,128)(2,1)}) custom-call(bf16[4,256,128]{2,1,0:T(8,128)(2,1)S(1)} %get-tuple-element.27.refs_0_, bf16[4,256,128]{2,1,0:T(8,128)(2,1)S(1)} %collective-permute-done.refs_1_, bf16[4,256,128]{2,1,0:T(8,128)(2,1)S(1)} %collective-permute-done.1.refs_2_, ...), custom_call_target="tpu_custom_call" | custom-call | tf_op jit(solution)/shard_map/pallas_call | solution.py:200
  (3 shorter events, 0.0 us)
Async XLA Ops:
  2.1 13.4 %collective-permute-start.2 = (bf16[4,256,128]{2,1,0:T(8,128)(2,1)S(1)}, bf16[4,256,128]{2,1,0:T(8,128)(2,1)S(1)}, u32[]{:S(2)}, u32[]{:S(2)}) collective-permute-start(bf16[4,256,128]{2,1,0:T(8,128)(2,1)S(1)} %get-tuple-element.29), channel_id=1, source_target_pairs={{0,14},{1,15},{2,12},{3,13},{4,10},{5,11},{6,8},{7,9},{8,6},{9,7},... | collective-permute-start | bytes 786440 | tf_op jit(solution)/shard_map/ppermute | solution.py:226
  9.5 18.7 %collective-permute-start.1 = (bf16[4,256,128]{2,1,0:T(8,128)(2,1)S(1)}, bf16[4,256,128]{2,1,0:T(8,128)(2,1)S(1)}, u32[]{:S(2)}, u32[]{:S(2)}) collective-permute-start(bf16[4,256,128]{2,1,0:T(8,128)(2,1)S(1)} %get-tuple-element.28), channel_id=1, source_target_pairs={{0,2},{1,3},{2,0},{3,1},{4,6},{5,7},{6,4},{7,5},{8,10},{9,11},{10,... | collective-permute-start | bytes 786440 | tf_op jit(solution)/shard_map/ppermute | solution.py:226
  10.1 18.2 %collective-permute-start.5 = (bf16[4,256,128]{2,1,0:T(8,128)(2,1)S(1)}, bf16[4,256,128]{2,1,0:T(8,128)(2,1)S(1)}, u32[]{:S(2)}, u32[]{:S(2)}) collective-permute-start(bf16[4,256,128]{2,1,0:T(8,128)(2,1)S(1)} %get-tuple-element.32), channel_id=1, source_target_pairs={{0,12},{1,13},{2,14},{3,15},{4,8},{5,9},{6,10},{7,11},{8,4},{9,5},... | collective-permute-start | bytes 786440 | tf_op jit(solution)/shard_map/ppermute | solution.py:226
  10.2 18.6 %collective-permute-start.4 = (bf16[4,256,128]{2,1,0:T(8,128)(2,1)S(1)}, bf16[4,256,128]{2,1,0:T(8,128)(2,1)S(1)}, u32[]{:S(2)}, u32[]{:S(2)}) collective-permute-start(bf16[4,256,128]{2,1,0:T(8,128)(2,1)S(1)} %get-tuple-element.31), channel_id=1, source_target_pairs={{0,4},{1,5},{2,6},{3,7},{4,0},{5,1},{6,2},{7,3},{8,12},{9,13},{10,... | collective-permute-start | bytes 786440 | tf_op jit(solution)/shard_map/ppermute | solution.py:226
  10.2 31.4 %collective-permute-start.8 = (bf16[4,256,128]{2,1,0:T(8,128)(2,1)S(1)}, bf16[4,256,128]{2,1,0:T(8,128)(2,1)S(1)}, u32[]{:S(2)}, u32[]{:S(2)}) collective-permute-start(bf16[4,256,128]{2,1,0:T(8,128)(2,1)S(1)} %get-tuple-element.36), channel_id=1, source_target_pairs={{0,10},{1,11},{2,8},{3,9},{4,14},{5,15},{6,12},{7,13},{8,2},{9,3},... | collective-permute-start | bytes 786440 | tf_op jit(solution)/shard_map/ppermute | solution.py:226
  15.5 26.2 %collective-permute-start.7 = (bf16[4,256,128]{2,1,0:T(8,128)(2,1)S(1)}, bf16[4,256,128]{2,1,0:T(8,128)(2,1)S(1)}, u32[]{:S(2)}, u32[]{:S(2)}) collective-permute-start(bf16[4,256,128]{2,1,0:T(8,128)(2,1)S(1)} %get-tuple-element.35), channel_id=1, source_target_pairs={{0,6},{1,7},{2,4},{3,5},{4,2},{5,3},{6,0},{7,1},{8,14},{9,15},{10,... | collective-permute-start | bytes 786440 | tf_op jit(solution)/shard_map/ppermute | solution.py:226
  28.3 13.9 %collective-permute-start = (bf16[4,256,128]{2,1,0:T(8,128)(2,1)S(1)}, bf16[4,256,128]{2,1,0:T(8,128)(2,1)S(1)}, u32[]{:S(2)}, u32[]{:S(2)}) collective-permute-start(bf16[4,256,128]{2,1,0:T(8,128)(2,1)S(1)} %get-tuple-element.27.refs_0_), channel_id=1, source_target_pairs={{0,1},{1,0},{2,3},{3,2},{4,5},{5,4},{6,7},{7,6},{8,9},{9,8},{10,11... | collective-permute-start | bytes 786440 | tf_op jit(solution)/shard_map/ppermute | solution.py:226
  28.3 13.9 %collective-permute-start.3 = (bf16[4,256,128]{2,1,0:T(8,128)(2,1)S(1)}, bf16[4,256,128]{2,1,0:T(8,128)(2,1)S(1)}, u32[]{:S(2)}, u32[]{:S(2)}) collective-permute-start(bf16[4,256,128]{2,1,0:T(8,128)(2,1)S(1)} %collective-permute-done.1.refs_2_), channel_id=1, source_target_pairs={{0,1},{1,0},{2,3},{3,2},{4,5},{5,4},{6,7},{7,6},{8,9},{9,8},{10,11... | collective-permute-start | bytes 786440 | tf_op jit(solution)/shard_map/ppermute | solution.py:226
  41.6 1.5 %collective-permute-start.6 = (bf16[4,256,128]{2,1,0:T(8,128)(2,1)S(1)}, bf16[4,256,128]{2,1,0:T(8,128)(2,1)S(1)}, u32[]{:S(2)}, u32[]{:S(2)}) collective-permute-start(bf16[4,256,128]{2,1,0:T(8,128)(2,1)S(1)} %collective-permute-done.4.refs_4_), channel_id=1, source_target_pairs={{0,1},{1,0},{2,3},{3,2},{4,5},{5,4},{6,7},{7,6},{8,9},{9,8},{10,11... | collective-permute-start | bytes 786440 | tf_op jit(solution)/shard_map/ppermute | solution.py:226
  41.6 1.9 %collective-permute-start.9 = (bf16[4,256,128]{2,1,0:T(8,128)(2,1)S(1)}, bf16[4,256,128]{2,1,0:T(8,128)(2,1)S(1)}, u32[]{:S(2)}, u32[]{:S(2)}) collective-permute-start(bf16[4,256,128]{2,1,0:T(8,128)(2,1)S(1)} %collective-permute-done.7.refs_6_), channel_id=1, source_target_pairs={{0,1},{1,0},{2,3},{3,2},{4,5},{5,4},{6,7},{7,6},{8,9},{9,8},{10,11... | collective-permute-start | bytes 786440 | tf_op jit(solution)/shard_map/ppermute | solution.py:226
  42.1 14.6 %collective-permute-start.13 = (bf16[4,256,128]{2,1,0:T(8,128)(2,1)S(1)}, bf16[4,256,128]{2,1,0:T(8,128)(2,1)S(1)}, u32[]{:S(2)}, u32[]{:S(2)}) collective-permute-start(bf16[4,256,128]{2,1,0:T(8,128)(2,1)S(1)} %get-tuple-element.45), channel_id=1, source_target_pairs={{0,8},{1,9},{2,10},{3,11},{4,12},{5,13},{6,14},{7,15},{8,0},{9,1},... | collective-permute-start | bytes 786440 | tf_op jit(solution)/shard_map/ppermute | solution.py:226
  45.7 11.0 %collective-permute-start.10 = (bf16[4,256,128]{2,1,0:T(8,128)(2,1)S(1)}, bf16[4,256,128]{2,1,0:T(8,128)(2,1)S(1)}, u32[]{:S(2)}, u32[]{:S(2)}) collective-permute-start(bf16[4,256,128]{2,1,0:T(8,128)(2,1)S(1)} %collective-permute-done.2.refs_0_.refs_8_), channel_id=1, source_target_pairs={{0,1},{1,0},{2,3},{3,2},{4,5},{5,4},{6,7},{7,6},{8,9},{9,8},{10,11... | collective-permute-start | bytes 786440 | tf_op jit(solution)/shard_map/ppermute | solution.py:226
  45.9 10.8 %collective-permute-start.11 = (bf16[4,256,128]{2,1,0:T(8,128)(2,1)S(1)}, bf16[4,256,128]{2,1,0:T(8,128)(2,1)S(1)}, u32[]{:S(2)}, u32[]{:S(2)}) collective-permute-start(bf16[4,256,128]{2,1,0:T(8,128)(2,1)S(1)} %collective-permute-done.5.refs_2_.refs_10_), channel_id=1, source_target_pairs={{0,1},{1,0},{2,3},{3,2},{4,5},{5,4},{6,7},{7,6},{8,9},{9,8},{10,11... | collective-permute-start | bytes 786440 | tf_op jit(solution)/shard_map/ppermute | solution.py:226
  46.3 10.4 %collective-permute-start.12 = (bf16[4,256,128]{2,1,0:T(8,128)(2,1)S(1)}, bf16[4,256,128]{2,1,0:T(8,128)(2,1)S(1)}, u32[]{:S(2)}, u32[]{:S(2)}) collective-permute-start(bf16[4,256,128]{2,1,0:T(8,128)(2,1)S(1)} %collective-permute-done.8.refs_4_.refs_12_), channel_id=1, source_target_pairs={{0,1},{1,0},{2,3},{3,2},{4,5},{5,4},{6,7},{7,6},{8,9},{9,8},{10,11... | collective-permute-start | bytes 786440 | tf_op jit(solution)/shard_map/ppermute | solution.py:226
  58.4 1.6 %collective-permute-start.14 = (bf16[4,256,128]{2,1,0:T(8,128)(2,1)S(1)}, bf16[4,256,128]{2,1,0:T(8,128)(2,1)S(1)}, u32[]{:S(2)}, u32[]{:S(2)}) collective-permute-start(bf16[4,256,128]{2,1,0:T(8,128)(2,1)S(1)} %collective-permute-done.13.refs_14_), channel_id=1, source_target_pairs={{0,1},{1,0},{2,3},{3,2},{4,5},{5,4},{6,7},{7,6},{8,9},{9,8},{10,11... | collective-permute-start | bytes 786440 | tf_op jit(solution)/shard_map/ppermute | solution.py:226

commit v3 on v2

v3 whole, which is shorter than its diff:
```python
import functools

import jax
import jax.numpy as jnp
from jax import lax
from jax.experimental import pallas as pl
from jax.experimental.pallas import tpu as pltpu
from jax.sharding import PartitionSpec as P

HDIM = 128
CORES = 2


def dot(a, b, contract):
    return lax.dot_general(a, b, (contract, ((), ())), preferred_element_type=jnp.float32)


NN = ((1,), (0,))
NT = ((1,), (1,))
TN = ((0,), (0,))


def entering(shard, axis, reverse):
    size, position = lax.axis_size(axis), lax.axis_index(axis)
    everything = lax.all_gather(shard, axis)
    start = jnp.zeros_like(shard)

    def lap(k, before):
        at = size - 1 - k if reverse else k
        reached = at > position if reverse else at < position
        return jnp.where(reached, before + everything[at], before)

    return lax.fori_loop(0, size, lap, start)


def general_body(queries, keys, values, grad_out):
    length = queries.shape[0]
    head_count = queries.shape[1] // HDIM
    split = lambda x: jnp.transpose(x.reshape(length, head_count, HDIM), (1, 0, 2))
    q, k, v, g = split(queries), split(keys), split(values), split(grad_out)
    einsum = functools.partial(jnp.einsum, preferred_element_type=jnp.float32)
    positions = lax.iota(jnp.int32, length)
    causal = positions[:, None] >= positions[None, :]
    scores_qk = jnp.where(causal[None], einsum("htd,hsd->hts", q, k), 0.0).astype(jnp.bfloat16)
    scores_gv = jnp.where(causal[None], einsum("htd,hsd->hts", g, v), 0.0).astype(jnp.bfloat16)
    state_half = entering(einsum("hsd,hse->hde", k, v), "seq", False).astype(jnp.bfloat16)
    grad_half = entering(einsum("htf,htb->hfb", q, g), "seq", True).astype(jnp.bfloat16)
    grad_q = einsum("hsd,hts->hdt", k, scores_gv) + einsum("hdv,htv->hdt", state_half, g)
    grad_k = einsum("htd,hts->hds", q, scores_gv) + einsum("hdv,hsv->hds", grad_half, v)
    grad_v = einsum("htd,hts->hds", g, scores_qk) + einsum("hfb,hsf->hbs", grad_half, k)
    width = head_count * HDIM
    rows = [x.reshape(width, length).astype(jnp.bfloat16) for x in (grad_q, grad_k, grad_v)]
    return tuple(lax.all_to_all(x, "seq", split_axis=0, concat_axis=1, tiled=True) for x in rows)


CHIPS = 8
OWN, NEAR, FAR = 0, (1, 2, 3), (7, 6, 5, 4)
ISSUED = (7, 1, 6, 2, 5, 3, 4)
RELAYS = ((0, 1, 2), (3, 7, 6), (5, 4))
TENSORS = 4
VMEM_SPEC = pl.BlockSpec(memory_space=pltpu.VMEM)
PARAMS = pltpu.CompilerParams(vmem_limit_bytes=40 * 1024 * 1024)
SMALL = pl.CostEstimate(flops=1, transcendentals=0, bytes_accessed=1)


def place():
    position = lax.axis_index("seq")
    return position // CORES, position % CORES


def after(x, *others):
    return lax.optimization_barrier((x, *others))[0]


def pack_kernel(flips, *refs):
    ins, outs, sems = refs[:TENSORS], refs[TENSORS:-1], refs[-1]
    chip, _ = place()
    copies = []
    for i, flip in enumerate(flips):
        columns = pl.ds(pl.multiple_of((chip ^ flip) * HDIM, HDIM), HDIM)
        for t in range(TENSORS):
            copies.append(
                pltpu.make_async_copy(ins[t].at[:, columns], outs[i].at[t], sems.at[i, t])
            )
    for copy in copies:
        copy.start()
    for copy in copies:
        copy.wait()


def pack(flips, arrays):
    shape = pltpu.VMEM((TENSORS, arrays[0].shape[0], HDIM), arrays[0].dtype)
    packed = pl.pallas_call(
        functools.partial(pack_kernel, flips),
        out_shape=[shape] * len(flips),
        in_specs=[pl.BlockSpec(memory_space=pl.ANY)] * TENSORS,
        out_specs=[VMEM_SPEC] * len(flips),
        scratch_shapes=[pltpu.SemaphoreType.DMA((len(flips), TENSORS))],
        cost_estimate=SMALL,
    )(*arrays)
    return dict(zip(flips, packed))


def within_blocks(blocks, core, turned, states, grads, intra):
    length = turned.shape[-1]
    half = HDIM // CORES
    own_rows = pl.ds(pl.multiple_of(core * half, half), half)
    row = lax.broadcasted_iota(jnp.int32, (length, length), 0)
    column = lax.broadcasted_iota(jnp.int32, (length, length), 1)
    causal = row >= column
    for i, block in enumerate(blocks):
        q, k, v, g = (block[t] for t in range(TENSORS))
        scores_gv = jnp.where(causal, dot(g, v, NT), 0.0).astype(jnp.bfloat16)
        scores_qk = jnp.where(causal, dot(q, k, NT), 0.0).astype(jnp.bfloat16)
        turned[i, 0] = k.T
        turned[i, 1] = q.T
        turned[i, 2] = g.T
        states[i] = dot(turned[i, 0], v, NN)
        grads[i] = dot(turned[i, 1], g, NN)
        intra[i, 0] = dot(turned[i, 0, own_rows, :], scores_gv, NT)
        intra[i, 1] = dot(turned[i, 1, own_rows, :], scores_gv, NN)
        intra[i, 2] = dot(turned[i, 2, own_rows, :], scores_qk, NN)


def within_shapes(count, length):
    return [
        ((count, HDIM, HDIM), jnp.float32),
        ((count, HDIM, HDIM), jnp.float32),
        ((count, 3, HDIM // CORES, length), jnp.float32),
    ]


def turned_scratch(count, length):
    return pltpu.VMEM((count, 3, HDIM, length), jnp.bfloat16)


def bind(where, refs):
    return [refs[array].at[pl.ds(at * TENSORS, TENSORS)] for array, at in where]


def within_kernel(where, n_arrays, *refs):
    _, core = place()
    within_blocks(bind(where, refs), core, refs[-1], *refs[n_arrays:-1])


def within(where, arrays):
    count, length = len(where), arrays[0].shape[1]
    return pl.pallas_call(
        functools.partial(within_kernel, where, len(arrays)),
        out_shape=[jax.ShapeDtypeStruct(*s) for s in within_shapes(count, length)],
        in_specs=[VMEM_SPEC] * len(arrays),
        out_specs=[VMEM_SPEC] * 3,
        scratch_shapes=[turned_scratch(count, length)],
        cost_estimate=SMALL,
        compiler_params=PARAMS,
    )(*arrays)


def finish_kernel(where, slots, sizes, n_arrays, *refs):
    n_blocks = sum(sizes)
    blocks = bind(where, refs)
    done = [refs[n_arrays + 3 * i : n_arrays + 3 * i + 3] for i in range(len(sizes) - 1)]
    rest = refs[n_arrays + 3 * len(done) :]
    outs, (state_half, grad_half, in_order), last, turned = rest[:3], rest[3:6], rest[6:9], rest[9]
    chip, core = place()
    half, length = HDIM // CORES, turned.shape[-1]
    own_rows = pl.ds(pl.multiple_of(core * half, half), half)
    within_blocks(blocks[n_blocks - sizes[-1] :], core, turned, *last)
    done.append(last)

    found = []
    for size, (states, grads, intra) in zip(sizes, done):
        for i in range(size):
            flip, other = slots[len(found)]
            b = (chip ^ flip) * CORES + (core ^ other)
            in_order[b, 0] = states[i]
            in_order[b, 1] = grads[i]
            found.append((b, intra.at[i]))

    total = jnp.zeros((HDIM, HDIM), jnp.float32)
    for b in range(n_blocks):
        state_half[b] = total.astype(jnp.bfloat16)
        total = total + in_order[b, 0]
    total = jnp.zeros((HDIM, HDIM), jnp.float32)
    for b in reversed(range(n_blocks)):
        grad_half[b, 0] = total.astype(jnp.bfloat16)
        grad_half[b, 1] = total.T.astype(jnp.bfloat16)
        total = total + in_order[b, 1]

    for block, (b, intra) in zip(blocks, found):
        k, v, g = (block[t] for t in range(1, TENSORS))
        columns = pl.ds(pl.multiple_of(b * length, length), length)
        across = (
            dot(state_half[b, own_rows, :], g, NT),
            dot(grad_half[b, 0, own_rows, :], v, NT),
            dot(grad_half[b, 1, own_rows, :], k, NT),
        )
        for j, out in enumerate(outs):
            out[:, columns] = (intra[j] + across[j]).astype(out.dtype)


def finish(where, slots, arrays, sizes, done):
    n_blocks, length = sum(sizes), arrays[0].shape[1]
    out = jax.ShapeDtypeStruct((HDIM // CORES, n_blocks * length), jnp.bfloat16)
    return pl.pallas_call(
        functools.partial(finish_kernel, where, slots, sizes, len(arrays)),
        out_shape=[out] * 3,
        in_specs=[VMEM_SPEC] * (len(arrays) + len(done)),
        out_specs=[VMEM_SPEC] * 3,
        scratch_shapes=[
            pltpu.VMEM((n_blocks, HDIM, HDIM), jnp.bfloat16),
            pltpu.VMEM((n_blocks, 2, HDIM, HDIM), jnp.bfloat16),
            pltpu.VMEM((n_blocks, 2, HDIM, HDIM), jnp.float32),
        ]
        + [pltpu.VMEM(*s) for s in within_shapes(sizes[-1], length)]
        + [turned_scratch(sizes[-1], length)],
        compiler_params=PARAMS,
    )(*arrays, *done)


def chip_body(queries, keys, values, grad_out):
    size = lax.axis_size("seq")
    given = (queries, keys, values, grad_out)
    packed = pack(FAR, given) | pack((OWN,) + NEAR, given)
    flipped = lambda x, flip: lax.ppermute(x, "seq", [(i, i ^ flip) for i in range(size)])
    mine, previous = {OWN: packed[OWN]}, ()
    for flip in ISSUED:
        mine[flip] = after(flipped(packed[flip], flip * CORES), *previous)
        previous = (mine[flip],)

    early = (OWN,) + NEAR + FAR[:-1]
    done = within(tuple((i, 0) for i in range(len(early))), [mine[flip] for flip in early])
    relayed = []
    for flips in RELAYS:
        held = [after(mine[flip], *done) if flips is RELAYS[-1] else mine[flip] for flip in flips]
        relayed.append(flipped(jnp.concatenate(held), 1))
    theirs = [(flip, j, at) for j, flips in enumerate(RELAYS) for at, flip in enumerate(flips)]
    soon, late = theirs[: -len(RELAYS[-1])], theirs[-len(RELAYS[-1]) :]
    done += within(tuple((j, at) for _, j, at in soon), relayed[:-1])

    own = early + FAR[-1:]
    arrays = [mine[flip] for flip in own] + relayed
    where = {(flip, 0): (i, 0) for i, flip in enumerate(own)}
    where |= {(flip, 1): (len(own) + j, at) for flip, j, at in theirs}
    slots = tuple((flip, 0) for flip in early) + tuple((flip, 1) for flip, _, _ in soon)
    slots += ((FAR[-1], 0),) + tuple((flip, 1) for flip, _, _ in late)
    sizes = (len(early), len(soon), 1 + len(late))
    return tuple(finish(tuple(where[slot] for slot in slots), slots, arrays, sizes, done))


def solution(mesh):
    in_specs = (P(("groups", "seq"), None),) * 4
    out_specs = (P("seq", "groups"),) * 3

    def body(queries, keys, values, grad_out):
        heads = queries.shape[1] // HDIM
        one_head_per_chip = heads == CHIPS and mesh.shape["seq"] == CHIPS * CORES
        chosen = chip_body if one_head_per_chip else general_body
        return chosen(queries, keys, values, grad_out)

    return jax.shard_map(body, mesh=mesh, in_specs=in_specs, out_specs=out_specs, check_vma=False)
```

time: 63.4 us -> 58.6 us (0.924)
  waiting for transfers between devices: 26 us -> 22.1 us
  starting transfers between devices: 26.6 us -> 25.4 us
    ppermute x15 -> x10, waiting for transfers between devices: 26 us -> 22.1 us  [chip_body(): lax.ppermute(x, 'seq', [(i, i ^ flip) for i in range(size)])]
    ppermute x15 -> x10, starting transfers between devices: 26.6 us -> 25.4 us  [chip_body(): lax.ppermute(x, 'seq', [(i, i ^ flip) for i in range(size)])]
  transfers between devices with their start and end apart: 15 -> 10, of which waited for: 5 -> 3; matrix products, arithmetic and copies ran while one was open for 0% -> 0% of each run, Pallas kernels for 6% -> 9%
where the time goes in v3:
time: 58.6 us; the launch traced here: 58.3 us
  starting transfers between devices  25.4 us (43%)
  waiting for transfers between devices  22.1 us (38%)
  Pallas kernels  9.8 us (17%)
  between operations  0.72 us (1%)
    ppermute x10, starting transfers between devices, chip_body(): lax.ppermute(x, 'seq', [(i, i ^ flip) for i in range(size)])  25.4 us
    ppermute x10, waiting for transfers between devices, chip_body(): lax.ppermute(x, 'seq', [(i, i ^ flip) for i in range(size)])  22.1 us
    pallas_call x2, Pallas kernels, within(): pl.pallas_call(functools.partial(within_kernel, where, len(arrays)), out_...  3.61 us
    pallas_call x1, Pallas kernels, finish(): pl.pallas_call(functools.partial(finish_kernel, where, slots, sizes, len(...  3.36 us
    pallas_call x2, Pallas kernels, pack(): pl.pallas_call(functools.partial(pack_kernel, flips), out_shape=[shape] *...  2.82 us
  transfers between devices with their start and end apart: 10, of which 3 were waited for; matrix products, arithmetic and copies ran while one was open for 0% of the time, Pallas kernels for 9%

profile of v3, /device:TPU:0, one launch (start us, length us, event | category | flops | bytes accessed | tf_op | source)
XLA Modules:
  0.0 58.3 jit_solution(4145544973873008325)
XLA Ops:
  0.6 1.4 %shard_map.68 = (bf16[4,256,128]{2,1,0:T(8,128)(2,1)S(1)}, bf16[4,256,128]{2,1,0:T(8,128)(2,1)S(1)}, bf16[4,256,128]{2,1,0:T(8,128)(2,1)S(1)}, bf16[4,256,128]{2,1,0:T(8,128)(2,1)S(1)}) custom-call(bf16[256,1024]{1,0:T(8,128)(2,1)} %refs_0_.3, bf16[256,1024]{1,0:T(8,128)(2,1)} %refs_1_.3, bf16[256,1024]{1,0:T(8,128)(2,1)} %refs_2_.3, bf16[256,1024]{1,0:T(8,128)(2,1)} %refs_3_.3), custom_call_target="tpu_custom_call" | custom-call | flops 1 | bytes 1 | tf_op jit(solution)/shard_map/pallas_call | solution.py:93
  2.1 6.1 %collective-permute-start.1 = (bf16[4,256,128]{2,1,0:T(8,128)(2,1)S(1)}, bf16[4,256,128]{2,1,0:T(8,128)(2,1)S(1)}, u32[]{:S(2)}, u32[]{:S(2)}) collective-permute-start(bf16[4,256,128]{2,1,0:T(8,128)(2,1)S(1)} %get-tuple-element.27), channel_id=1, source_target_pairs={{0,14},{1,15},{2,12},{3,13},{4,10},{5,11},{6,8},{7,9},{8,6},{9,7},... | collective-permute-start | bytes 786440 | tf_op jit(solution)/shard_map/ppermute | solution.py:225
  8.1 1.4 %shard_map.67 = (bf16[4,256,128]{2,1,0:T(8,128)(2,1)S(1)}, bf16[4,256,128]{2,1,0:T(8,128)(2,1)S(1)}, bf16[4,256,128]{2,1,0:T(8,128)(2,1)S(1)}, bf16[4,256,128]{2,1,0:T(8,128)(2,1)S(1)}) custom-call(bf16[256,1024]{1,0:T(8,128)(2,1)} %refs_0_.3, bf16[256,1024]{1,0:T(8,128)(2,1)} %refs_1_.3, bf16[256,1024]{1,0:T(8,128)(2,1)} %refs_2_.3, bf16[256,1024]{1,0:T(8,128)(2,1)} %refs_3_.3), custom_call_target="tpu_custom_call" | custom-call | flops 1 | bytes 1 | tf_op jit(solution)/shard_map/pallas_call | solution.py:93
  9.5 0.6 collective-permute-start
  10.1 0.1 collective-permute-start.3
  10.2 0.0 collective-permute-start.2
  10.2 5.2 %collective-permute-start.5 = (bf16[4,256,128]{2,1,0:T(8,128)(2,1)S(1)}, bf16[4,256,128]{2,1,0:T(8,128)(2,1)S(1)}, u32[]{:S(2)}, u32[]{:S(2)}) collective-permute-start(bf16[4,256,128]{2,1,0:T(8,128)(2,1)S(1)} %get-tuple-element.34), channel_id=1, source_target_pairs={{0,10},{1,11},{2,8},{3,9},{4,14},{5,15},{6,12},{7,13},{8,2},{9,3},... | collective-permute-start | bytes 786440 | tf_op jit(solution)/shard_map/ppermute | solution.py:225
  15.5 0.0 collective-permute-done.1.refs_4_
  15.5 12.8 %collective-permute-start.4 = (bf16[4,256,128]{2,1,0:T(8,128)(2,1)S(1)}, bf16[4,256,128]{2,1,0:T(8,128)(2,1)S(1)}, u32[]{:S(2)}, u32[]{:S(2)}) collective-permute-start(bf16[4,256,128]{2,1,0:T(8,128)(2,1)S(1)} %get-tuple-element.33), channel_id=1, source_target_pairs={{0,6},{1,7},{2,4},{3,5},{4,2},{5,3},{6,0},{7,1},{8,14},{9,15},{10,... | collective-permute-start | bytes 786440 | tf_op jit(solution)/shard_map/ppermute | solution.py:225
  28.3 0.0 collective-permute-done.refs_1_
  28.3 0.0 collective-permute-start.6
  28.3 0.0 collective-permute-done.3.refs_5_
  28.3 0.0 collective-permute-done.2.refs_2_
  28.3 20.0 %collective-permute-done.5.refs_6_ = bf16[4,256,128]{2,1,0:T(8,128)(2,1)S(1)} collective-permute-done((bf16[4,256,128]{2,1,0:T(8,128)(2,1)S(1)}, bf16[4,256,128]{2,1,0:T(8,128)(2,1)S(1)}, u32[]{:S(2)}, u32[]{:S(2)}) %collective-permute-start.5) | collective-permute-done | bytes 262176 | tf_op jit(solution)/shard_map/ppermute | solution.py:225
  48.3 0.0 collective-permute-done.4.refs_3_
  48.3 0.1 pad_maximum_fusion.1
  48.4 0.1 pad_maximum_fusion
  48.4 0.1 collective-permute-start.7
  48.5 0.5 collective-permute-start.8
  49.0 1.9 %shard_map.69 = (f32[7,128,128]{2,1,0:T(8,128)S(1)}, f32[7,128,128]{2,1,0:T(8,128)S(1)}, f32[7,3,64,256]{3,2,1,0:T(8,128)S(1)}) custom-call(bf16[4,256,128]{2,1,0:T(8,128)(2,1)S(1)} %get-tuple-element.25.refs_0_, bf16[4,256,128]{2,1,0:T(8,128)(2,1)S(1)} %collective-permute-done.refs_1_, bf16[4,256,128]{2,1,0:T(8,128)(2,1)S(1)} %collective-permute-done.2.refs_2_, ...), custom_call_target="tpu_custom_call" | custom-call | flops 1 | bytes 1 | tf_op jit(solution)/shard_map/pallas_call | solution.py:148
  51.0 1.9 %collective-permute-done.6.refs_7_ = bf16[4,256,128]{2,1,0:T(8,128)(2,1)S(1)} collective-permute-done((bf16[4,256,128]{2,1,0:T(8,128)(2,1)S(1)}, bf16[4,256,128]{2,1,0:T(8,128)(2,1)S(1)}, u32[]{:S(2)}, u32[]{:S(2)}) %collective-permute-start.6) | collective-permute-done | bytes 262176 | tf_op jit(solution)/shard_map/ppermute | solution.py:225
  53.0 0.1 collective-permute-start.9
  53.0 0.0 collective-permute-done.7.refs_0_.refs_8_
  53.1 0.0 collective-permute-done.8.refs_1_.refs_9_
  53.1 1.7 %shard_map.70 = (f32[6,128,128]{2,1,0:T(8,128)S(1)}, f32[6,128,128]{2,1,0:T(8,128)S(1)}, f32[6,3,64,256]{3,2,1,0:T(8,128)S(1)}) custom-call(bf16[12,256,128]{2,1,0:T(8,128)(2,1)S(1)} %collective-permute-done.7.refs_0_.refs_8_, bf16[12,256,128]{2,1,0:T(8,128)(2,1)S(1)} %collective-permute-done.8.refs_1_.refs_9_), custom_call_target="tpu_custom_call" | custom-call | flops 1 | bytes 1 | tf_op jit(solution)/shard_map/pallas_call | solution.py:148
  54.7 0.2 collective-permute-done.9.refs_10_
  54.9 3.4 %shard_map.71 = (bf16[64,4096]{1,0:T(8,128)(2,1)}, bf16[64,4096]{1,0:T(8,128)(2,1)}, bf16[64,4096]{1,0:T(8,128)(2,1)}) custom-call(bf16[4,256,128]{2,1,0:T(8,128)(2,1)S(1)} %get-tuple-element.25.refs_0_, bf16[4,256,128]{2,1,0:T(8,128)(2,1)S(1)} %collective-permute-done.refs_1_, bf16[4,256,128]{2,1,0:T(8,128)(2,1)S(1)} %collective-permute-done.2.refs_2_, ...), custom_call_target="tpu_custom_call" | custom-call | tf_op jit(solution)/shard_map/pallas_call | solution.py:205
  (1 shorter events, 0.0 us)
Async XLA Ops:
  2.1 13.4 %collective-permute-start.1 = (bf16[4,256,128]{2,1,0:T(8,128)(2,1)S(1)}, bf16[4,256,128]{2,1,0:T(8,128)(2,1)S(1)}, u32[]{:S(2)}, u32[]{:S(2)}) collective-permute-start(bf16[4,256,128]{2,1,0:T(8,128)(2,1)S(1)} %get-tuple-element.27), channel_id=1, source_target_pairs={{0,14},{1,15},{2,12},{3,13},{4,10},{5,11},{6,8},{7,9},{8,6},{9,7},... | collective-permute-start | bytes 786440 | tf_op jit(solution)/shard_map/ppermute | solution.py:225
  9.5 18.7 %collective-permute-start = (bf16[4,256,128]{2,1,0:T(8,128)(2,1)S(1)}, bf16[4,256,128]{2,1,0:T(8,128)(2,1)S(1)}, u32[]{:S(2)}, u32[]{:S(2)}) collective-permute-start(bf16[4,256,128]{2,1,0:T(8,128)(2,1)S(1)} %get-tuple-element.26), channel_id=1, source_target_pairs={{0,2},{1,3},{2,0},{3,1},{4,6},{5,7},{6,4},{7,5},{8,10},{9,11},{10,... | collective-permute-start | bytes 786440 | tf_op jit(solution)/shard_map/ppermute | solution.py:225
  10.1 18.2 %collective-permute-start.3 = (bf16[4,256,128]{2,1,0:T(8,128)(2,1)S(1)}, bf16[4,256,128]{2,1,0:T(8,128)(2,1)S(1)}, u32[]{:S(2)}, u32[]{:S(2)}) collective-permute-start(bf16[4,256,128]{2,1,0:T(8,128)(2,1)S(1)} %get-tuple-element.30), channel_id=1, source_target_pairs={{0,12},{1,13},{2,14},{3,15},{4,8},{5,9},{6,10},{7,11},{8,4},{9,5},... | collective-permute-start | bytes 786440 | tf_op jit(solution)/shard_map/ppermute | solution.py:225
  10.2 18.1 %collective-permute-start.2 = (bf16[4,256,128]{2,1,0:T(8,128)(2,1)S(1)}, bf16[4,256,128]{2,1,0:T(8,128)(2,1)S(1)}, u32[]{:S(2)}, u32[]{:S(2)}) collective-permute-start(bf16[4,256,128]{2,1,0:T(8,128)(2,1)S(1)} %get-tuple-element.29), channel_id=1, source_target_pairs={{0,4},{1,5},{2,6},{3,7},{4,0},{5,1},{6,2},{7,3},{8,12},{9,13},{10,... | collective-permute-start | bytes 786440 | tf_op jit(solution)/shard_map/ppermute | solution.py:225
  10.2 38.0 %collective-permute-start.5 = (bf16[4,256,128]{2,1,0:T(8,128)(2,1)S(1)}, bf16[4,256,128]{2,1,0:T(8,128)(2,1)S(1)}, u32[]{:S(2)}, u32[]{:S(2)}) collective-permute-start(bf16[4,256,128]{2,1,0:T(8,128)(2,1)S(1)} %get-tuple-element.34), channel_id=1, source_target_pairs={{0,10},{1,11},{2,8},{3,9},{4,14},{5,15},{6,12},{7,13},{8,2},{9,3},... | collective-permute-start | bytes 786440 | tf_op jit(solution)/shard_map/ppermute | solution.py:225
  15.5 32.8 %collective-permute-start.4 = (bf16[4,256,128]{2,1,0:T(8,128)(2,1)S(1)}, bf16[4,256,128]{2,1,0:T(8,128)(2,1)S(1)}, u32[]{:S(2)}, u32[]{:S(2)}) collective-permute-start(bf16[4,256,128]{2,1,0:T(8,128)(2,1)S(1)} %get-tuple-element.33), channel_id=1, source_target_pairs={{0,6},{1,7},{2,4},{3,5},{4,2},{5,3},{6,0},{7,1},{8,14},{9,15},{10,... | collective-permute-start | bytes 786440 | tf_op jit(solution)/shard_map/ppermute | solution.py:225
  28.3 24.6 %collective-permute-start.6 = (bf16[4,256,128]{2,1,0:T(8,128)(2,1)S(1)}, bf16[4,256,128]{2,1,0:T(8,128)(2,1)S(1)}, u32[]{:S(2)}, u32[]{:S(2)}) collective-permute-start(bf16[4,256,128]{2,1,0:T(8,128)(2,1)S(1)} %get-tuple-element.37), channel_id=1, source_target_pairs={{0,8},{1,9},{2,10},{3,11},{4,12},{5,13},{6,14},{7,15},{8,0},{9,1},... | collective-permute-start | bytes 786440 | tf_op jit(solution)/shard_map/ppermute | solution.py:225
  48.4 4.6 %collective-permute-start.7 = (bf16[12,256,128]{2,1,0:T(8,128)(2,1)S(1)}, bf16[12,256,128]{2,1,0:T(8,128)(2,1)S(1)}, u32[]{:S(2)}, u32[]{:S(2)}) collective-permute-start(bf16[12,256,128]{2,1,0:T(8,128)(2,1)S(1)} %pad_maximum_fusion), channel_id=1, source_target_pairs={{0,1},{1,0},{2,3},{3,2},{4,5},{5,4},{6,7},{7,6},{8,9},{9,8},{10,11... | collective-permute-start | bytes 2359304 | tf_op jit(solution)/shard_map/ppermute | solution.py:225
  48.5 4.5 %collective-permute-start.8 = (bf16[12,256,128]{2,1,0:T(8,128)(2,1)S(1)}, bf16[12,256,128]{2,1,0:T(8,128)(2,1)S(1)}, u32[]{:S(2)}, u32[]{:S(2)}) collective-permute-start(bf16[12,256,128]{2,1,0:T(8,128)(2,1)S(1)} %pad_maximum_fusion.1), channel_id=1, source_target_pairs={{0,1},{1,0},{2,3},{3,2},{4,5},{5,4},{6,7},{7,6},{8,9},{9,8},{10,11... | collective-permute-start | bytes 2359304 | tf_op jit(solution)/shard_map/ppermute | solution.py:225
  53.0 2.0 %collective-permute-start.9 = (bf16[8,256,128]{2,1,0:T(8,128)(2,1)S(1)}, bf16[8,256,128]{2,1,0:T(8,128)(2,1)S(1)}, u32[]{:S(2)}, u32[]{:S(2)}) collective-permute-start(bf16[8,256,128]{2,1,0:T(8,128)(2,1)S(1)} %pad_maximum_fusion.2), channel_id=1, source_target_pairs={{0,1},{1,0},{2,3},{3,2},{4,5},{5,4},{6,7},{7,6},{8,9},{9,8},{10,11... | collective-permute-start | bytes 1572872 | tf_op jit(solution)/shard_map/ppermute | solution.py:225

commit v4 on v3

--- a/solution.py
+++ b/solution.py
@@ -54,9 +54,9 @@
 
 
 CHIPS = 8
-OWN, NEAR, FAR = 0, (1, 2, 3), (7, 6, 5, 4)
-ISSUED = (7, 1, 6, 2, 5, 3, 4)
-RELAYS = ((0, 1, 2), (3, 7, 6), (5, 4))
+OWN, NEAR, FAR = 0, (1, 2, 3), (4, 5, 6, 7)
+ISSUED = (4, 1, 5, 2, 6, 3, 7)
+RELAYS = ((0, 1, 2), (3, 4, 5), (6, 7))
 TENSORS = 4
 VMEM_SPEC = pl.BlockSpec(memory_space=pltpu.VMEM)
 PARAMS = pltpu.CompilerParams(vmem_limit_bytes=40 * 1024 * 1024)
@@ -161,7 +161,8 @@
     blocks = bind(where, refs)
     done = [refs[n_arrays + 3 * i : n_arrays + 3 * i + 3] for i in range(len(sizes) - 1)]
     rest = refs[n_arrays + 3 * len(done) :]
-    outs, (state_half, grad_half, in_order), last, turned = rest[:3], rest[3:6], rest[6:9], rest[9]
+    outs, (state_half, grad_half, in_order), last = rest[:3], rest[3:6], rest[6:9]
+    turned, ready, sems = rest[9:]
     chip, core = place()
     half, length = HDIM // CORES, turned.shape[-1]
     own_rows = pl.ds(pl.multiple_of(core * half, half), half)
@@ -183,20 +184,26 @@
         total = total + in_order[b, 0]
     total = jnp.zeros((HDIM, HDIM), jnp.float32)
     for b in reversed(range(n_blocks)):
-        grad_half[b, 0] = total.astype(jnp.bfloat16)
-        grad_half[b, 1] = total.T.astype(jnp.bfloat16)
+        rounded = total.astype(jnp.bfloat16)
+        grad_half[b, 0] = rounded
+        grad_half[b, 1] = rounded.T
         total = total + in_order[b, 1]
 
-    for block, (b, intra) in zip(blocks, found):
-        k, v, g = (block[t] for t in range(1, TENSORS))
-        columns = pl.ds(pl.multiple_of(b * length, length), length)
-        across = (
-            dot(state_half[b, own_rows, :], g, NT),
-            dot(grad_half[b, 0, own_rows, :], v, NT),
-            dot(grad_half[b, 1, own_rows, :], k, NT),
-        )
-        for j, out in enumerate(outs):
-            out[:, columns] = (intra[j] + across[j]).astype(out.dtype)
+    copies = []
+    factors = (
+        lambda b: state_half[b, own_rows, :],
+        lambda b: grad_half[b, 0, own_rows, :],
+        lambda b: grad_half[b, 1, own_rows, :],
+    )
+    for j, (factor, t) in enumerate(zip(factors, (3, 2, 1))):
+        for block, (b, intra) in zip(blocks, found):
+            columns = pl.ds(pl.multiple_of(b * length, length), length)
+            total = intra[j] + dot(factor(b), block[t], NT)
+            ready[j, :, columns] = total.astype(ready.dtype)
+        copies.append(pltpu.make_async_copy(ready.at[j], outs[j], sems.at[j]))
+        copies[-1].start()
+    for copy in copies:
+        copy.wait()
 
 
 def finish(where, slots, arrays, sizes, done):
@@ -206,14 +213,15 @@
         functools.partial(finish_kernel, where, slots, sizes, len(arrays)),
         out_shape=[out] * 3,
         in_specs=[VMEM_SPEC] * (len(arrays) + len(done)),
-        out_specs=[VMEM_SPEC] * 3,
+        out_specs=[pl.BlockSpec(memory_space=pl.ANY)] * 3,
         scratch_shapes=[
             pltpu.VMEM((n_blocks, HDIM, HDIM), jnp.bfloat16),
             pltpu.VMEM((n_blocks, 2, HDIM, HDIM), jnp.bfloat16),
             pltpu.VMEM((n_blocks, 2, HDIM, HDIM), jnp.float32),
         ]
         + [pltpu.VMEM(*s) for s in within_shapes(sizes[-1], length)]
-        + [turned_scratch(sizes[-1], length)],
+        + [turned_scratch(sizes[-1], length)]
+        + [pltpu.VMEM((3,) + out.shape, out.dtype), pltpu.SemaphoreType.DMA((3,))],
         compiler_params=PARAMS,
     )(*arrays, *done)
 
@@ -221,7 +229,7 @@
 def chip_body(queries, keys, values, grad_out):
     size = lax.axis_size("seq")
     given = (queries, keys, values, grad_out)
-    packed = pack(FAR, given) | pack((OWN,) + NEAR, given)
+    packed = pack(FAR[:1], given) | pack(FAR[1:] + (OWN,) + NEAR, given)
     flipped = lambda x, flip: lax.ppermute(x, "seq", [(i, i ^ flip) for i in range(size)])
     mine, previous = {OWN: packed[OWN]}, ()
     for flip in ISSUED:
@@ -236,7 +244,8 @@
         relayed.append(flipped(jnp.concatenate(held), 1))
     theirs = [(flip, j, at) for j, flips in enumerate(RELAYS) for at, flip in enumerate(flips)]
     soon, late = theirs[: -len(RELAYS[-1])], theirs[-len(RELAYS[-1]) :]
-    done += within(tuple((j, at) for _, j, at in soon), relayed[:-1])
+    beside = tuple((j, at) for _, j, at in soon) + ((len(relayed) - 1, 0),)
+    done += within(beside, relayed[:-1] + [mine[FAR[-1]]])
 
     own = early + FAR[-1:]
     arrays = [mine[flip] for flip in own] + relayed
@@ -244,7 +253,7 @@
     where |= {(flip, 1): (len(own) + j, at) for flip, j, at in theirs}
     slots = tuple((flip, 0) for flip in early) + tuple((flip, 1) for flip, _, _ in soon)
     slots += ((FAR[-1], 0),) + tuple((flip, 1) for flip, _, _ in late)
-    sizes = (len(early), len(soon), 1 + len(late))
+    sizes = (len(early), len(beside), len(late))
     return tuple(finish(tuple(where[slot] for slot in slots), slots, arrays, sizes, done))
 
 

time: 58.6 us -> 56.7 us (0.968)
  the two profiles are of different devices: /device:TPU:0 before, /device:TPU:19 now
where the time goes in v4:
time: 56.7 us; the launch traced here: 56.4 us
  waiting for transfers between devices  32.7 us (58%)
  starting transfers between devices  13.5 us (24%)
  Pallas kernels  9.36 us (17%)
  between operations  0.68 us (1%)
    ppermute x10, waiting for transfers between devices, chip_body(): lax.ppermute(x, 'seq', [(i, i ^ flip) for i in range(size)])  32.7 us
    ppermute x10, starting transfers between devices, chip_body(): lax.ppermute(x, 'seq', [(i, i ^ flip) for i in range(size)])  13.5 us
    pallas_call x2, Pallas kernels, within(): pl.pallas_call(functools.partial(within_kernel, where, len(arrays)), out_...  3.87 us
    pallas_call x2, Pallas kernels, pack(): pl.pallas_call(functools.partial(pack_kernel, flips), out_shape=[shape] *...  2.76 us
    pallas_call x1, Pallas kernels, finish(): pl.pallas_call(functools.partial(finish_kernel, where, slots, sizes, len(...  2.73 us
  transfers between devices with their start and end apart: 10, of which 4 were waited for; matrix products, arithmetic and copies ran while one was open for 0% of the time, Pallas kernels for 10%

profile of v4, /device:TPU:19, one launch (start us, length us, event | category | flops | bytes accessed | tf_op | source)
XLA Modules:
  0.0 56.4 jit_solution(1030681897950562161)
XLA Ops:
  0.6 1.0 %shard_map.68 = bf16[4,256,128]{2,1,0:T(8,128)(2,1)S(1)} custom-call(bf16[256,1024]{1,0:T(8,128)(2,1)} %refs_0_.3, bf16[256,1024]{1,0:T(8,128)(2,1)} %refs_1_.3, bf16[256,1024]{1,0:T(8,128)(2,1)} %refs_2_.3, bf16[256,1024]{1,0:T(8,128)(2,1)} %refs_3_.3), custom_call_target="tpu_custom_call" | custom-call | flops 1 | bytes 1 | tf_op jit(solution)/shard_map/pallas_call | solution.py:93
  1.6 0.1 collective-permute-start.1
  1.7 1.8 %shard_map.67 = (bf16[4,256,128]{2,1,0:T(8,128)(2,1)S(1)}, bf16[4,256,128]{2,1,0:T(8,128)(2,1)S(1)}, bf16[4,256,128]{2,1,0:T(8,128)(2,1)S(1)}, bf16[4,256,128]{2...) custom-call(bf16[256,1024]{1,0:T(8,128)(2,1)} %refs_0_.3, ...), custom_call_target="tpu_custom_call" | custom-call | flops 1 | bytes 1 | tf_op jit(solution)/shard_map/pallas_call | solution.py:93
  3.5 1.3 %collective-permute-start = (bf16[4,256,128]{2,1,0:T(8,128)(2,1)S(1)}, bf16[4,256,128]{2,1,0:T(8,128)(2,1)S(1)}, u32[]{:S(2)}, u32[]{:S(2)}) collective-permute-start(bf16[4,256,128]{2,1,0:T(8,128)(2,1)S(1)} %get-tuple-element.25), channel_id=1, source_target_pairs={{0,2},{1,3},{2,0},{3,1},{4,6},{5,7},{6,4},{7,5},{8,10},{9,11},{10,... | collective-permute-start | bytes 786440 | tf_op jit(solution)/shard_map/ppermute | solution.py:233
  4.8 2.3 %collective-permute-start.3 = (bf16[4,256,128]{2,1,0:T(8,128)(2,1)S(1)}, bf16[4,256,128]{2,1,0:T(8,128)(2,1)S(1)}, u32[]{:S(2)}, u32[]{:S(2)}) collective-permute-start(bf16[4,256,128]{2,1,0:T(8,128)(2,1)S(1)} %get-tuple-element.28), channel_id=1, source_target_pairs={{0,10},{1,11},{2,8},{3,9},{4,14},{5,15},{6,12},{7,13},{8,2},{9,3},... | collective-permute-start | bytes 786440 | tf_op jit(solution)/shard_map/ppermute | solution.py:233
  7.1 1.3 %collective-permute-start.2 = (bf16[4,256,128]{2,1,0:T(8,128)(2,1)S(1)}, bf16[4,256,128]{2,1,0:T(8,128)(2,1)S(1)}, u32[]{:S(2)}, u32[]{:S(2)}) collective-permute-start(bf16[4,256,128]{2,1,0:T(8,128)(2,1)S(1)} %get-tuple-element.27), channel_id=1, source_target_pairs={{0,4},{1,5},{2,6},{3,7},{4,0},{5,1},{6,2},{7,3},{8,12},{9,13},{10,... | collective-permute-start | bytes 786440 | tf_op jit(solution)/shard_map/ppermute | solution.py:233
  8.4 0.0 collective-permute-start.5
  8.4 9.6 %collective-permute-done.1.refs_4_ = bf16[4,256,128]{2,1,0:T(8,128)(2,1)S(1)} collective-permute-done((bf16[4,256,128]{2,1,0:T(8,128)(2,1)S(1)}, bf16[4,256,128]{2,1,0:T(8,128)(2,1)S(1)}, u32[]{:S(2)}, u32[]{:S(2)}) %collective-permute-start.1) | collective-permute-done | bytes 262176 | tf_op jit(solution)/shard_map/ppermute | solution.py:233
  18.0 7.2 %collective-permute-start.4 = (bf16[4,256,128]{2,1,0:T(8,128)(2,1)S(1)}, bf16[4,256,128]{2,1,0:T(8,128)(2,1)S(1)}, u32[]{:S(2)}, u32[]{:S(2)}) collective-permute-start(bf16[4,256,128]{2,1,0:T(8,128)(2,1)S(1)} %get-tuple-element.31), channel_id=1, source_target_pairs={{0,6},{1,7},{2,4},{3,5},{4,2},{5,3},{6,0},{7,1},{8,14},{9,15},{10,... | collective-permute-start | bytes 786440 | tf_op jit(solution)/shard_map/ppermute | solution.py:233
  25.2 0.0 collective-permute-done.refs_1_
  25.2 0.0 collective-permute-start.6
  25.2 4.1 %collective-permute-done.3.refs_5_ = bf16[4,256,128]{2,1,0:T(8,128)(2,1)S(1)} collective-permute-done((bf16[4,256,128]{2,1,0:T(8,128)(2,1)S(1)}, bf16[4,256,128]{2,1,0:T(8,128)(2,1)S(1)}, u32[]{:S(2)}, u32[]{:S(2)}) %collective-permute-start.3) | collective-permute-done | bytes 262176 | tf_op jit(solution)/shard_map/ppermute | solution.py:233
  29.3 0.0 collective-permute-done.2.refs_2_
  29.3 15.3 %collective-permute-done.5.refs_6_ = bf16[4,256,128]{2,1,0:T(8,128)(2,1)S(1)} collective-permute-done((bf16[4,256,128]{2,1,0:T(8,128)(2,1)S(1)}, bf16[4,256,128]{2,1,0:T(8,128)(2,1)S(1)}, u32[]{:S(2)}, u32[]{:S(2)}) %collective-permute-start.5) | collective-permute-done | bytes 262176 | tf_op jit(solution)/shard_map/ppermute | solution.py:233
  44.6 0.0 collective-permute-done.4.refs_3_
  44.6 0.1 pad_maximum_fusion.1
  44.7 0.1 pad_maximum_fusion
  44.8 0.7 %collective-permute-start.7 = (bf16[12,256,128]{2,1,0:T(8,128)(2,1)S(1)}, bf16[12,256,128]{2,1,0:T(8,128)(2,1)S(1)}, u32[]{:S(2)}, u32[]{:S(2)}) collective-permute-start(bf16[12,256,128]{2,1,0:T(8,128)(2,1)S(1)} %pad_maximum_fusion), channel_id=1, source_target_pairs={{0,1},{1,0},{2,3},{3,2},{4,5},{5,4},{6,7},{7,6},{8,9},{9,8},{10,11... | collective-permute-start | bytes 2359304 | tf_op jit(solution)/shard_map/ppermute | solution.py:233
  45.4 0.1 collective-permute-start.8
  45.5 1.9 %shard_map.69 = (f32[7,128,128]{2,1,0:T(8,128)S(1)}, f32[7,128,128]{2,1,0:T(8,128)S(1)}, f32[7,3,64,256]{3,2,1,0:T(8,128)S(1)}) custom-call(bf16[4,256,128]{2,1,0:T(8,128)(2,1)S(1)} %get-tuple-element.24.refs_0_, bf16[4,256,128]{2,1,0:T(8,128)(2,1)S(1)} %collective-permute-done.refs_1_, bf16[4,256,128]{2,1,0:T(8,128)(2,1)S(1)} %collective-permute-done.2.refs_2_, ...), custom_call_target="tpu_custom_call" | custom-call | flops 1 | bytes 1 | tf_op jit(solution)/shard_map/pallas_call | solution.py:148
  47.4 3.7 %collective-permute-done.6.refs_2_.refs_7_ = bf16[4,256,128]{2,1,0:T(8,128)(2,1)S(1)} collective-permute-done((bf16[4,256,128]{2,1,0:T(8,128)(2,1)S(1)}, bf16[4,256,128]{2,1,0:T(8,128)(2,1)S(1)}, u32[]{:S(2)}, u32[]{:S(2)}) %collective-permute-start.6) | collective-permute-done | bytes 262176 | tf_op jit(solution)/shard_map/ppermute | solution.py:233
  51.2 0.6 collective-permute-start.9
  51.8 0.0 collective-permute-done.7.refs_0_.refs_8_
  51.8 0.0 collective-permute-done.8.refs_1_.refs_9_
  51.8 1.9 %shard_map.70 = (f32[7,128,128]{2,1,0:T(8,128)S(1)}, f32[7,128,128]{2,1,0:T(8,128)S(1)}, f32[7,3,64,256]{3,2,1,0:T(8,128)S(1)}) custom-call(bf16[12,256,128]{2,1,0:T(8,128)(2,1)S(1)} %collective-permute-done.7.refs_0_.refs_8_, bf16[12,256,128]{2,1,0:T(8,128)(2,1)S(1)} %collective-permute-done.8.refs_1_.refs_9_, ...), custom_call_target="tpu_custom_call" | custom-call | flops 1 | bytes 1 | tf_op jit(solution)/shard_map/pallas_call | solution.py:148
  53.7 0.0 collective-permute-done.9.refs_10_
  53.7 2.7 %shard_map.71 = (bf16[64,4096]{1,0:T(8,128)(2,1)}, bf16[64,4096]{1,0:T(8,128)(2,1)}, bf16[64,4096]{1,0:T(8,128)(2,1)}) custom-call(bf16[4,256,128]{2,1,0:T(8,128)(2,1)S(1)} %get-tuple-element.24.refs_0_, bf16[4,256,128]{2,1,0:T(8,128)(2,1)S(1)} %collective-permute-done.refs_1_, bf16[4,256,128]{2,1,0:T(8,128)(2,1)S(1)} %collective-permute-done.2.refs_2_, ...), custom_call_target="tpu_custom_call" | custom-call | tf_op jit(solution)/shard_map/pallas_call | solution.py:212
  (1 shorter events, 0.0 us)
Async XLA Ops:
  1.6 16.4 %collective-permute-start.1 = (bf16[4,256,128]{2,1,0:T(8,128)(2,1)S(1)}, bf16[4,256,128]{2,1,0:T(8,128)(2,1)S(1)}, u32[]{:S(2)}, u32[]{:S(2)}) collective-permute-start(bf16[4,256,128]{2,1,0:T(8,128)(2,1)S(1)} %shard_map.68), channel_id=1, source_target_pairs={{0,8},{1,9},{2,10},{3,11},{4,12},{5,13},{6,14},{7,15},{8,0},{9,1},... | collective-permute-start | bytes 786440 | tf_op jit(solution)/shard_map/ppermute | solution.py:233
  3.5 21.7 %collective-permute-start = (bf16[4,256,128]{2,1,0:T(8,128)(2,1)S(1)}, bf16[4,256,128]{2,1,0:T(8,128)(2,1)S(1)}, u32[]{:S(2)}, u32[]{:S(2)}) collective-permute-start(bf16[4,256,128]{2,1,0:T(8,128)(2,1)S(1)} %get-tuple-element.25), channel_id=1, source_target_pairs={{0,2},{1,3},{2,0},{3,1},{4,6},{5,7},{6,4},{7,5},{8,10},{9,11},{10,... | collective-permute-start | bytes 786440 | tf_op jit(solution)/shard_map/ppermute | solution.py:233
  4.8 24.4 %collective-permute-start.3 = (bf16[4,256,128]{2,1,0:T(8,128)(2,1)S(1)}, bf16[4,256,128]{2,1,0:T(8,128)(2,1)S(1)}, u32[]{:S(2)}, u32[]{:S(2)}) collective-permute-start(bf16[4,256,128]{2,1,0:T(8,128)(2,1)S(1)} %get-tuple-element.28), channel_id=1, source_target_pairs={{0,10},{1,11},{2,8},{3,9},{4,14},{5,15},{6,12},{7,13},{8,2},{9,3},... | collective-permute-start | bytes 786440 | tf_op jit(solution)/shard_map/ppermute | solution.py:233
  7.1 22.2 %collective-permute-start.2 = (bf16[4,256,128]{2,1,0:T(8,128)(2,1)S(1)}, bf16[4,256,128]{2,1,0:T(8,128)(2,1)S(1)}, u32[]{:S(2)}, u32[]{:S(2)}) collective-permute-start(bf16[4,256,128]{2,1,0:T(8,128)(2,1)S(1)} %get-tuple-element.27), channel_id=1, source_target_pairs={{0,4},{1,5},{2,6},{3,7},{4,0},{5,1},{6,2},{7,3},{8,12},{9,13},{10,... | collective-permute-start | bytes 786440 | tf_op jit(solution)/shard_map/ppermute | solution.py:233
  8.4 36.2 %collective-permute-start.5 = (bf16[4,256,128]{2,1,0:T(8,128)(2,1)S(1)}, bf16[4,256,128]{2,1,0:T(8,128)(2,1)S(1)}, u32[]{:S(2)}, u32[]{:S(2)}) collective-permute-start(bf16[4,256,128]{2,1,0:T(8,128)(2,1)S(1)} %get-tuple-element.32), channel_id=1, source_target_pairs={{0,12},{1,13},{2,14},{3,15},{4,8},{5,9},{6,10},{7,11},{8,4},{9,5},... | collective-permute-start | bytes 786440 | tf_op jit(solution)/shard_map/ppermute | solution.py:233
  18.0 26.6 %collective-permute-start.4 = (bf16[4,256,128]{2,1,0:T(8,128)(2,1)S(1)}, bf16[4,256,128]{2,1,0:T(8,128)(2,1)S(1)}, u32[]{:S(2)}, u32[]{:S(2)}) collective-permute-start(bf16[4,256,128]{2,1,0:T(8,128)(2,1)S(1)} %get-tuple-element.31), channel_id=1, source_target_pairs={{0,6},{1,7},{2,4},{3,5},{4,2},{5,3},{6,0},{7,1},{8,14},{9,15},{10,... | collective-permute-start | bytes 786440 | tf_op jit(solution)/shard_map/ppermute | solution.py:233
  25.2 25.9 %collective-permute-start.6 = (bf16[4,256,128]{2,1,0:T(8,128)(2,1)S(1)}, bf16[4,256,128]{2,1,0:T(8,128)(2,1)S(1)}, u32[]{:S(2)}, u32[]{:S(2)}) collective-permute-start(bf16[4,256,128]{2,1,0:T(8,128)(2,1)S(1)} %get-tuple-element.35), channel_id=1, source_target_pairs={{0,14},{1,15},{2,12},{3,13},{4,10},{5,11},{6,8},{7,9},{8,6},{9,7},... | collective-permute-start | bytes 786440 | tf_op jit(solution)/shard_map/ppermute | solution.py:233
  44.8 7.0 %collective-permute-start.7 = (bf16[12,256,128]{2,1,0:T(8,128)(2,1)S(1)}, bf16[12,256,128]{2,1,0:T(8,128)(2,1)S(1)}, u32[]{:S(2)}, u32[]{:S(2)}) collective-permute-start(bf16[12,256,128]{2,1,0:T(8,128)(2,1)S(1)} %pad_maximum_fusion), channel_id=1, source_target_pairs={{0,1},{1,0},{2,3},{3,2},{4,5},{5,4},{6,7},{7,6},{8,9},{9,8},{10,11... | collective-permute-start | bytes 2359304 | tf_op jit(solution)/shard_map/ppermute | solution.py:233
  45.4 6.3 %collective-permute-start.8 = (bf16[12,256,128]{2,1,0:T(8,128)(2,1)S(1)}, bf16[12,256,128]{2,1,0:T(8,128)(2,1)S(1)}, u32[]{:S(2)}, u32[]{:S(2)}) collective-permute-start(bf16[12,256,128]{2,1,0:T(8,128)(2,1)S(1)} %pad_maximum_fusion.1), channel_id=1, source_target_pairs={{0,1},{1,0},{2,3},{3,2},{4,5},{5,4},{6,7},{7,6},{8,9},{9,8},{10,11... | collective-permute-start | bytes 2359304 | tf_op jit(solution)/shard_map/ppermute | solution.py:233
  51.2 2.5 %collective-permute-start.9 = (bf16[8,256,128]{2,1,0:T(8,128)(2,1)S(1)}, bf16[8,256,128]{2,1,0:T(8,128)(2,1)S(1)}, u32[]{:S(2)}, u32[]{:S(2)}) collective-permute-start(bf16[8,256,128]{2,1,0:T(8,128)(2,1)S(1)} %pad_maximum_fusion.2), channel_id=1, source_target_pairs={{0,1},{1,0},{2,3},{3,2},{4,5},{5,4},{6,7},{7,6},{8,9},{9,8},{10,11... | collective-permute-start | bytes 1572872 | tf_op jit(solution)/shard_map/ppermute | solution.py:233

commit v5 on v4

--- a/solution.py
+++ b/solution.py
@@ -54,9 +54,9 @@
 
 
 CHIPS = 8
-OWN, NEAR, FAR = 0, (1, 2, 3), (4, 5, 6, 7)
-ISSUED = (4, 1, 5, 2, 6, 3, 7)
-RELAYS = ((0, 1, 2), (3, 4, 5), (6, 7))
+OWN, NEAR, FAR = 0, (1, 2, 3), (4, 5, 7, 6)
+ISSUED = (4, 1, 5, 2, 7, 3, 6)
+RELAYS = ((0, 1, 2), (3, 4, 5), (7, 6))
 TENSORS = 4
 VMEM_SPEC = pl.BlockSpec(memory_space=pltpu.VMEM)
 PARAMS = pltpu.CompilerParams(vmem_limit_bytes=40 * 1024 * 1024)
@@ -108,18 +108,18 @@
     row = lax.broadcasted_iota(jnp.int32, (length, length), 0)
     column = lax.broadcasted_iota(jnp.int32, (length, length), 1)
     causal = row >= column
+    masked = lambda x: jnp.where(causal, x, 0.0).astype(jnp.bfloat16)
+    scores_gv = [masked(dot(block[3], block[2], NT)) for block in blocks]
+    scores_qk = [masked(dot(block[0], block[1], NT)) for block in blocks]
     for i, block in enumerate(blocks):
-        q, k, v, g = (block[t] for t in range(TENSORS))
-        scores_gv = jnp.where(causal, dot(g, v, NT), 0.0).astype(jnp.bfloat16)
-        scores_qk = jnp.where(causal, dot(q, k, NT), 0.0).astype(jnp.bfloat16)
-        turned[i, 0] = k.T
-        turned[i, 1] = q.T
-        turned[i, 2] = g.T
-        states[i] = dot(turned[i, 0], v, NN)
-        grads[i] = dot(turned[i, 1], g, NN)
-        intra[i, 0] = dot(turned[i, 0, own_rows, :], scores_gv, NT)
-        intra[i, 1] = dot(turned[i, 1, own_rows, :], scores_gv, NN)
-        intra[i, 2] = dot(turned[i, 2, own_rows, :], scores_qk, NN)
+        for j, t in enumerate((1, 0, 3)):
+            turned[i, j] = block[t].T
+    for i, block in enumerate(blocks):
+        states[i] = dot(turned[i, 0], block[2], NN)
+        grads[i] = dot(turned[i, 1], block[3], NN)
+    for j, (scores, form) in enumerate(((scores_gv, NT), (scores_gv, NN), (scores_qk, NN))):
+        for i in range(len(blocks)):
+            intra[i, j] = dot(turned[i, j, own_rows, :], scores[i], form)
 
 
 def within_shapes(count, length):

time: 56.7 us -> 55.1 us (0.972)
  Pallas kernels: 9.36 us -> 8.19 us
    pallas_call x2, Pallas kernels: 3.87 us -> 2.89 us  [within(): pl.pallas_call(functools.partial(within_kernel, where, len(arrays)), out_...]
  transfers between devices with their start and end apart: 10 -> 10, of which waited for: 4 -> 5; matrix products, arithmetic and copies ran while one was open for 0% -> 0% of each run, Pallas kernels for 10% -> 8%
where the time goes in v5:
time: 55.1 us; the launch traced here: 54.9 us
  waiting for transfers between devices  32.3 us (59%)
  starting transfers between devices  13.5 us (25%)
  Pallas kernels  8.19 us (15%)
  between operations  0.68 us (1%)
    ppermute x10, waiting for transfers between devices, chip_body(): lax.ppermute(x, 'seq', [(i, i ^ flip) for i in range(size)])  32.3 us
    ppermute x10, starting transfers between devices, chip_body(): lax.ppermute(x, 'seq', [(i, i ^ flip) for i in range(size)])  13.5 us
    pallas_call x2, Pallas kernels, within(): pl.pallas_call(functools.partial(within_kernel, where, len(arrays)), out_...  2.89 us
    pallas_call x2, Pallas kernels, pack(): pl.pallas_call(functools.partial(pack_kernel, flips), out_shape=[shape] *...  2.76 us
    pallas_call x1, Pallas kernels, finish(): pl.pallas_call(functools.partial(finish_kernel, where, slots, sizes, len(...  2.54 us
  transfers between devices with their start and end apart: 10, of which 5 were waited for; matrix products, arithmetic and copies ran while one was open for 0% of the time, Pallas kernels for 8%

profile of v5, /device:TPU:19, one launch (start us, length us, event | category | flops | bytes accessed | tf_op | source)
XLA Modules:
  0.0 54.9 jit_solution(8324114477290613797)
XLA Ops:
  0.6 1.0 %shard_map.68 = bf16[4,256,128]{2,1,0:T(8,128)(2,1)S(1)} custom-call(bf16[256,1024]{1,0:T(8,128)(2,1)} %refs_0_.3, bf16[256,1024]{1,0:T(8,128)(2,1)} %refs_1_.3, bf16[256,1024]{1,0:T(8,128)(2,1)} %refs_2_.3, bf16[256,1024]{1,0:T(8,128)(2,1)} %refs_3_.3), custom_call_target="tpu_custom_call" | custom-call | flops 1 | bytes 1 | tf_op jit(solution)/shard_map/pallas_call | solution.py:93
  1.6 0.1 collective-permute-start.1
  1.7 1.8 %shard_map.67 = (bf16[4,256,128]{2,1,0:T(8,128)(2,1)S(1)}, bf16[4,256,128]{2,1,0:T(8,128)(2,1)S(1)}, bf16[4,256,128]{2,1,0:T(8,128)(2,1)S(1)}, bf16[4,256,128]{2...) custom-call(bf16[256,1024]{1,0:T(8,128)(2,1)} %refs_0_.3, ...), custom_call_target="tpu_custom_call" | custom-call | flops 1 | bytes 1 | tf_op jit(solution)/shard_map/pallas_call | solution.py:93
  3.5 1.3 %collective-permute-start = (bf16[4,256,128]{2,1,0:T(8,128)(2,1)S(1)}, bf16[4,256,128]{2,1,0:T(8,128)(2,1)S(1)}, u32[]{:S(2)}, u32[]{:S(2)}) collective-permute-start(bf16[4,256,128]{2,1,0:T(8,128)(2,1)S(1)} %get-tuple-element.25), channel_id=1, source_target_pairs={{0,2},{1,3},{2,0},{3,1},{4,6},{5,7},{6,4},{7,5},{8,10},{9,11},{10,... | collective-permute-start | bytes 786440 | tf_op jit(solution)/shard_map/ppermute | solution.py:233
  4.8 2.3 %collective-permute-start.3 = (bf16[4,256,128]{2,1,0:T(8,128)(2,1)S(1)}, bf16[4,256,128]{2,1,0:T(8,128)(2,1)S(1)}, u32[]{:S(2)}, u32[]{:S(2)}) collective-permute-start(bf16[4,256,128]{2,1,0:T(8,128)(2,1)S(1)} %get-tuple-element.28), channel_id=1, source_target_pairs={{0,10},{1,11},{2,8},{3,9},{4,14},{5,15},{6,12},{7,13},{8,2},{9,3},... | collective-permute-start | bytes 786440 | tf_op jit(solution)/shard_map/ppermute | solution.py:233
  7.1 1.3 %collective-permute-start.2 = (bf16[4,256,128]{2,1,0:T(8,128)(2,1)S(1)}, bf16[4,256,128]{2,1,0:T(8,128)(2,1)S(1)}, u32[]{:S(2)}, u32[]{:S(2)}) collective-permute-start(bf16[4,256,128]{2,1,0:T(8,128)(2,1)S(1)} %get-tuple-element.27), channel_id=1, source_target_pairs={{0,4},{1,5},{2,6},{3,7},{4,0},{5,1},{6,2},{7,3},{8,12},{9,13},{10,... | collective-permute-start | bytes 786440 | tf_op jit(solution)/shard_map/ppermute | solution.py:233
  8.4 0.0 collective-permute-start.5
  8.4 9.6 %collective-permute-done.1.refs_4_ = bf16[4,256,128]{2,1,0:T(8,128)(2,1)S(1)} collective-permute-done((bf16[4,256,128]{2,1,0:T(8,128)(2,1)S(1)}, bf16[4,256,128]{2,1,0:T(8,128)(2,1)S(1)}, u32[]{:S(2)}, u32[]{:S(2)}) %collective-permute-start.1) | collective-permute-done | bytes 262176 | tf_op jit(solution)/shard_map/ppermute | solution.py:233
  18.0 7.2 %collective-permute-start.4 = (bf16[4,256,128]{2,1,0:T(8,128)(2,1)S(1)}, bf16[4,256,128]{2,1,0:T(8,128)(2,1)S(1)}, u32[]{:S(2)}, u32[]{:S(2)}) collective-permute-start(bf16[4,256,128]{2,1,0:T(8,128)(2,1)S(1)} %get-tuple-element.31), channel_id=1, source_target_pairs={{0,6},{1,7},{2,4},{3,5},{4,2},{5,3},{6,0},{7,1},{8,14},{9,15},{10,... | collective-permute-start | bytes 786440 | tf_op jit(solution)/shard_map/ppermute | solution.py:233
  25.2 0.0 collective-permute-done.refs_1_
  25.2 0.0 collective-permute-start.6
  25.2 4.1 %collective-permute-done.3.refs_5_ = bf16[4,256,128]{2,1,0:T(8,128)(2,1)S(1)} collective-permute-done((bf16[4,256,128]{2,1,0:T(8,128)(2,1)S(1)}, bf16[4,256,128]{2,1,0:T(8,128)(2,1)S(1)}, u32[]{:S(2)}, u32[]{:S(2)}) %collective-permute-start.3) | collective-permute-done | bytes 262176 | tf_op jit(solution)/shard_map/ppermute | solution.py:233
  29.3 0.0 collective-permute-done.2.refs_2_
  29.3 16.3 %collective-permute-done.5.refs_6_ = bf16[4,256,128]{2,1,0:T(8,128)(2,1)S(1)} collective-permute-done((bf16[4,256,128]{2,1,0:T(8,128)(2,1)S(1)}, bf16[4,256,128]{2,1,0:T(8,128)(2,1)S(1)}, u32[]{:S(2)}, u32[]{:S(2)}) %collective-permute-start.5) | collective-permute-done | bytes 262176 | tf_op jit(solution)/shard_map/ppermute | solution.py:233
  45.5 0.0 collective-permute-done.4.refs_3_
  45.5 0.1 pad_maximum_fusion.1
  45.6 0.1 pad_maximum_fusion
  45.7 0.7 %collective-permute-start.7 = (bf16[12,256,128]{2,1,0:T(8,128)(2,1)S(1)}, bf16[12,256,128]{2,1,0:T(8,128)(2,1)S(1)}, u32[]{:S(2)}, u32[]{:S(2)}) collective-permute-start(bf16[12,256,128]{2,1,0:T(8,128)(2,1)S(1)} %pad_maximum_fusion), channel_id=1, source_target_pairs={{0,1},{1,0},{2,3},{3,2},{4,5},{5,4},{6,7},{7,6},{8,9},{9,8},{10,11... | collective-permute-start | bytes 2359304 | tf_op jit(solution)/shard_map/ppermute | solution.py:233
  46.4 0.1 collective-permute-start.8
  46.4 1.4 %shard_map.69 = (f32[7,128,128]{2,1,0:T(8,128)S(1)}, f32[7,128,128]{2,1,0:T(8,128)S(1)}, f32[7,3,64,256]{3,2,1,0:T(8,128)S(1)}) custom-call(bf16[4,256,128]{2,1,0:T(8,128)(2,1)S(1)} %get-tuple-element.24.refs_0_, bf16[4,256,128]{2,1,0:T(8,128)(2,1)S(1)} %collective-permute-done.refs_1_, bf16[4,256,128]{2,1,0:T(8,128)(2,1)S(1)} %collective-permute-done.2.refs_2_, ...), custom_call_target="tpu_custom_call" | custom-call | flops 1 | bytes 1 | tf_op jit(solution)/shard_map/pallas_call | solution.py:148
  47.9 2.3 %collective-permute-done.6.refs_2_.refs_7_ = bf16[4,256,128]{2,1,0:T(8,128)(2,1)S(1)} collective-permute-done((bf16[4,256,128]{2,1,0:T(8,128)(2,1)S(1)}, bf16[4,256,128]{2,1,0:T(8,128)(2,1)S(1)}, u32[]{:S(2)}, u32[]{:S(2)}) %collective-permute-start.6) | collective-permute-done | bytes 262176 | tf_op jit(solution)/shard_map/ppermute | solution.py:233
  50.2 0.6 %collective-permute-start.9 = (bf16[8,256,128]{2,1,0:T(8,128)(2,1)S(1)}, bf16[8,256,128]{2,1,0:T(8,128)(2,1)S(1)}, u32[]{:S(2)}, u32[]{:S(2)}) collective-permute-start(bf16[8,256,128]{2,1,0:T(8,128)(2,1)S(1)} %pad_maximum_fusion.2), channel_id=1, source_target_pairs={{0,1},{1,0},{2,3},{3,2},{4,5},{5,4},{6,7},{7,6},{8,9},{9,8},{10,11... | collective-permute-start | bytes 1572872 | tf_op jit(solution)/shard_map/ppermute | solution.py:233
  50.8 0.0 collective-permute-done.7.refs_0_.refs_8_
  50.8 0.0 collective-permute-done.8.refs_1_.refs_9_
  50.8 1.4 %shard_map.70 = (f32[7,128,128]{2,1,0:T(8,128)S(1)}, f32[7,128,128]{2,1,0:T(8,128)S(1)}, f32[7,3,64,256]{3,2,1,0:T(8,128)S(1)}) custom-call(bf16[12,256,128]{2,1,0:T(8,128)(2,1)S(1)} %collective-permute-done.7.refs_0_.refs_8_, bf16[12,256,128]{2,1,0:T(8,128)(2,1)S(1)} %collective-permute-done.8.refs_1_.refs_9_, ...), custom_call_target="tpu_custom_call" | custom-call | flops 1 | bytes 1 | tf_op jit(solution)/shard_map/pallas_call | solution.py:148
  52.3 0.1 collective-permute-done.9.refs_10_
  52.3 2.5 %shard_map.71 = (bf16[64,4096]{1,0:T(8,128)(2,1)}, bf16[64,4096]{1,0:T(8,128)(2,1)}, bf16[64,4096]{1,0:T(8,128)(2,1)}) custom-call(bf16[4,256,128]{2,1,0:T(8,128)(2,1)S(1)} %get-tuple-element.24.refs_0_, bf16[4,256,128]{2,1,0:T(8,128)(2,1)S(1)} %collective-permute-done.refs_1_, bf16[4,256,128]{2,1,0:T(8,128)(2,1)S(1)} %collective-permute-done.2.refs_2_, ...), custom_call_target="tpu_custom_call" | custom-call | tf_op jit(solution)/shard_map/pallas_call | solution.py:212
  (1 shorter events, 0.0 us)
Async XLA Ops:
  1.6 16.4 %collective-permute-start.1 = (bf16[4,256,128]{2,1,0:T(8,128)(2,1)S(1)}, bf16[4,256,128]{2,1,0:T(8,128)(2,1)S(1)}, u32[]{:S(2)}, u32[]{:S(2)}) collective-permute-start(bf16[4,256,128]{2,1,0:T(8,128)(2,1)S(1)} %shard_map.68), channel_id=1, source_target_pairs={{0,8},{1,9},{2,10},{3,11},{4,12},{5,13},{6,14},{7,15},{8,0},{9,1},... | collective-permute-start | bytes 786440 | tf_op jit(solution)/shard_map/ppermute | solution.py:233
  3.5 21.7 %collective-permute-start = (bf16[4,256,128]{2,1,0:T(8,128)(2,1)S(1)}, bf16[4,256,128]{2,1,0:T(8,128)(2,1)S(1)}, u32[]{:S(2)}, u32[]{:S(2)}) collective-permute-start(bf16[4,256,128]{2,1,0:T(8,128)(2,1)S(1)} %get-tuple-element.25), channel_id=1, source_target_pairs={{0,2},{1,3},{2,0},{3,1},{4,6},{5,7},{6,4},{7,5},{8,10},{9,11},{10,... | collective-permute-start | bytes 786440 | tf_op jit(solution)/shard_map/ppermute | solution.py:233
  4.8 24.4 %collective-permute-start.3 = (bf16[4,256,128]{2,1,0:T(8,128)(2,1)S(1)}, bf16[4,256,128]{2,1,0:T(8,128)(2,1)S(1)}, u32[]{:S(2)}, u32[]{:S(2)}) collective-permute-start(bf16[4,256,128]{2,1,0:T(8,128)(2,1)S(1)} %get-tuple-element.28), channel_id=1, source_target_pairs={{0,10},{1,11},{2,8},{3,9},{4,14},{5,15},{6,12},{7,13},{8,2},{9,3},... | collective-permute-start | bytes 786440 | tf_op jit(solution)/shard_map/ppermute | solution.py:233
  7.1 22.2 %collective-permute-start.2 = (bf16[4,256,128]{2,1,0:T(8,128)(2,1)S(1)}, bf16[4,256,128]{2,1,0:T(8,128)(2,1)S(1)}, u32[]{:S(2)}, u32[]{:S(2)}) collective-permute-start(bf16[4,256,128]{2,1,0:T(8,128)(2,1)S(1)} %get-tuple-element.27), channel_id=1, source_target_pairs={{0,4},{1,5},{2,6},{3,7},{4,0},{5,1},{6,2},{7,3},{8,12},{9,13},{10,... | collective-permute-start | bytes 786440 | tf_op jit(solution)/shard_map/ppermute | solution.py:233
  8.4 37.1 %collective-permute-start.5 = (bf16[4,256,128]{2,1,0:T(8,128)(2,1)S(1)}, bf16[4,256,128]{2,1,0:T(8,128)(2,1)S(1)}, u32[]{:S(2)}, u32[]{:S(2)}) collective-permute-start(bf16[4,256,128]{2,1,0:T(8,128)(2,1)S(1)} %get-tuple-element.32), channel_id=1, source_target_pairs={{0,14},{1,15},{2,12},{3,13},{4,10},{5,11},{6,8},{7,9},{8,6},{9,7},... | collective-permute-start | bytes 786440 | tf_op jit(solution)/shard_map/ppermute | solution.py:233
  18.0 27.5 %collective-permute-start.4 = (bf16[4,256,128]{2,1,0:T(8,128)(2,1)S(1)}, bf16[4,256,128]{2,1,0:T(8,128)(2,1)S(1)}, u32[]{:S(2)}, u32[]{:S(2)}) collective-permute-start(bf16[4,256,128]{2,1,0:T(8,128)(2,1)S(1)} %get-tuple-element.31), channel_id=1, source_target_pairs={{0,6},{1,7},{2,4},{3,5},{4,2},{5,3},{6,0},{7,1},{8,14},{9,15},{10,... | collective-permute-start | bytes 786440 | tf_op jit(solution)/shard_map/ppermute | solution.py:233
  25.2 25.0 %collective-permute-start.6 = (bf16[4,256,128]{2,1,0:T(8,128)(2,1)S(1)}, bf16[4,256,128]{2,1,0:T(8,128)(2,1)S(1)}, u32[]{:S(2)}, u32[]{:S(2)}) collective-permute-start(bf16[4,256,128]{2,1,0:T(8,128)(2,1)S(1)} %get-tuple-element.35), channel_id=1, source_target_pairs={{0,12},{1,13},{2,14},{3,15},{4,8},{5,9},{6,10},{7,11},{8,4},{9,5},... | collective-permute-start | bytes 786440 | tf_op jit(solution)/shard_map/ppermute | solution.py:233
  45.7 5.1 %collective-permute-start.7 = (bf16[12,256,128]{2,1,0:T(8,128)(2,1)S(1)}, bf16[12,256,128]{2,1,0:T(8,128)(2,1)S(1)}, u32[]{:S(2)}, u32[]{:S(2)}) collective-permute-start(bf16[12,256,128]{2,1,0:T(8,128)(2,1)S(1)} %pad_maximum_fusion), channel_id=1, source_target_pairs={{0,1},{1,0},{2,3},{3,2},{4,5},{5,4},{6,7},{7,6},{8,9},{9,8},{10,11... | collective-permute-start | bytes 2359304 | tf_op jit(solution)/shard_map/ppermute | solution.py:233
  46.4 4.4 %collective-permute-start.8 = (bf16[12,256,128]{2,1,0:T(8,128)(2,1)S(1)}, bf16[12,256,128]{2,1,0:T(8,128)(2,1)S(1)}, u32[]{:S(2)}, u32[]{:S(2)}) collective-permute-start(bf16[12,256,128]{2,1,0:T(8,128)(2,1)S(1)} %pad_maximum_fusion.1), channel_id=1, source_target_pairs={{0,1},{1,0},{2,3},{3,2},{4,5},{5,4},{6,7},{7,6},{8,9},{9,8},{10,11... | collective-permute-start | bytes 2359304 | tf_op jit(solution)/shard_map/ppermute | solution.py:233
  50.2 2.1 %collective-permute-start.9 = (bf16[8,256,128]{2,1,0:T(8,128)(2,1)S(1)}, bf16[8,256,128]{2,1,0:T(8,128)(2,1)S(1)}, u32[]{:S(2)}, u32[]{:S(2)}) collective-permute-start(bf16[8,256,128]{2,1,0:T(8,128)(2,1)S(1)} %pad_maximum_fusion.2), channel_id=1, source_target_pairs={{0,1},{1,0},{2,3},{3,2},{4,5},{5,4},{6,7},{7,6},{8,9},{9,8},{10,11... | collective-permute-start | bytes 1572872 | tf_op jit(solution)/shard_map/ppermute | solution.py:233

commit v6 on v5

--- a/solution.py
+++ b/solution.py
@@ -56,7 +56,8 @@
 CHIPS = 8
 OWN, NEAR, FAR = 0, (1, 2, 3), (4, 5, 7, 6)
 ISSUED = (4, 1, 5, 2, 7, 3, 6)
-RELAYS = ((0, 1, 2), (3, 4, 5), (7, 6))
+EARLY = (OWN,) + NEAR + FAR[:-1]
+RELAYS = 4
 TENSORS = 4
 VMEM_SPEC = pl.BlockSpec(memory_space=pltpu.VMEM)
 PARAMS = pltpu.CompilerParams(vmem_limit_bytes=40 * 1024 * 1024)
@@ -134,8 +135,17 @@
     return pltpu.VMEM((count, 3, HDIM, length), jnp.bfloat16)
 
 
+class Block:
+    def __init__(self, rows):
+        self.rows = rows
+
+    def __getitem__(self, t):
+        ref, row = self.rows[t]
+        return ref[row]
+
+
 def bind(where, refs):
-    return [refs[array].at[pl.ds(at * TENSORS, TENSORS)] for array, at in where]
+    return [Block([(refs[array], row) for array, row in rows]) for rows in where]
 
 
 def within_kernel(where, n_arrays, *refs):
@@ -236,25 +246,30 @@
         mine[flip] = after(flipped(packed[flip], flip * CORES), *previous)
         previous = (mine[flip],)
 
-    early = (OWN,) + NEAR + FAR[:-1]
-    done = within(tuple((i, 0) for i in range(len(early))), [mine[flip] for flip in early])
-    relayed = []
-    for flips in RELAYS:
-        held = [after(mine[flip], *done) if flips is RELAYS[-1] else mine[flip] for flip in flips]
-        relayed.append(flipped(jnp.concatenate(held), 1))
-    theirs = [(flip, j, at) for j, flips in enumerate(RELAYS) for at, flip in enumerate(flips)]
-    soon, late = theirs[: -len(RELAYS[-1])], theirs[-len(RELAYS[-1]) :]
-    beside = tuple((j, at) for _, j, at in soon) + ((len(relayed) - 1, 0),)
-    done += within(beside, relayed[:-1] + [mine[FAR[-1]]])
-
-    own = early + FAR[-1:]
-    arrays = [mine[flip] for flip in own] + relayed
-    where = {(flip, 0): (i, 0) for i, flip in enumerate(own)}
-    where |= {(flip, 1): (len(own) + j, at) for flip, j, at in theirs}
-    slots = tuple((flip, 0) for flip in early) + tuple((flip, 1) for flip, _, _ in soon)
-    slots += ((FAR[-1], 0),) + tuple((flip, 1) for flip, _, _ in late)
-    sizes = (len(early), len(beside), len(late))
-    return tuple(finish(tuple(where[slot] for slot in slots), slots, arrays, sizes, done))
+    rows = [(flip, t) for flip in EARLY for t in range(TENSORS)]
+    share = len(rows) // RELAYS
+    theirs, relayed = {}, []
+    for j in range(RELAYS):
+        part = rows[j * share : (j + 1) * share]
+        theirs |= {row: (j, at) for at, row in enumerate(part)}
+        pieces = [[t for f, t in part if f == flip] for flip in EARLY]
+        pieces = [mine[f][ts[0] : ts[-1] + 1] for f, ts in zip(EARLY, pieces) if ts]
+        relayed.append(flipped(jnp.concatenate(pieces), 1))
+
+    whole = lambda array: tuple((array, t) for t in range(TENSORS))
+    done = within(tuple(whole(i) for i in range(len(EARLY))), [mine[flip] for flip in EARLY])
+    last = FAR[-1]
+    late = flipped(after(mine[last], *done), 1)
+    soon = tuple(tuple(theirs[flip, t] for t in range(TENSORS)) for flip in EARLY)
+    done += within(soon + (whole(RELAYS),), relayed + [mine[last]])
+
+    arrays = [mine[flip] for flip in EARLY] + relayed + [mine[last], late]
+    shifted = tuple(tuple((len(EARLY) + array, row) for array, row in rows) for rows in soon)
+    where = tuple(whole(i) for i in range(len(EARLY))) + shifted
+    where += (whole(len(arrays) - 2), whole(len(arrays) - 1))
+    slots = tuple((flip, other) for other in range(CORES) for flip in EARLY)
+    slots += ((last, 0), (last, 1))
+    return tuple(finish(where, slots, arrays, (len(EARLY), len(EARLY) + 1, 1), done))
 
 
 def solution(mesh):

time: 55.1 us -> 55 us (level)
  waiting for transfers between devices: 32.3 us -> 31.5 us
  starting transfers between devices: 13.5 us -> 14.1 us
    ppermute x10 -> x12, waiting for transfers between devices: 32.3 us -> 31.5 us  [chip_body(): lax.ppermute(x, 'seq', [(i, i ^ flip) for i in range(size)])]
    ppermute x10 -> x12, starting transfers between devices: 13.5 us -> 14.1 us  [chip_body(): lax.ppermute(x, 'seq', [(i, i ^ flip) for i in range(size)])]
  transfers between devices with their start and end apart: 10 -> 12, of which waited for: 5 -> 4; matrix products, arithmetic and copies ran while one was open for 0% -> 0% of each run, Pallas kernels for 8% -> 9%
where the time goes in v6:
time: 55 us; the launch traced here: 54.8 us
  waiting for transfers between devices  31.5 us (57%)
  starting transfers between devices  14.1 us (26%)
  Pallas kernels  8.25 us (15%)
  between operations  0.72 us (1%)
    ppermute x12, waiting for transfers between devices, chip_body(): lax.ppermute(x, 'seq', [(i, i ^ flip) for i in range(size)])  31.5 us
    ppermute x12, starting transfers between devices, chip_body(): lax.ppermute(x, 'seq', [(i, i ^ flip) for i in range(size)])  14.1 us
    pallas_call x2, Pallas kernels, within(): pl.pallas_call(functools.partial(within_kernel, where, len(arrays)), out_...  3.08 us
    pallas_call x2, Pallas kernels, pack(): pl.pallas_call(functools.partial(pack_kernel, flips), out_shape=[shape] *...  2.76 us
    pallas_call x1, Pallas kernels, finish(): pl.pallas_call(functools.partial(finish_kernel, where, slots, sizes, len(...  2.41 us
  transfers between devices with their start and end apart: 12, of which 4 were waited for; matrix products, arithmetic and copies ran while one was open for 0% of the time, Pallas kernels for 9%

profile of v6, /device:TPU:19, one launch (start us, length us, event | category | flops | bytes accessed | tf_op | source)
XLA Modules:
  0.0 54.8 jit_solution(17809867251903212005)
XLA Ops:
  0.6 1.0 %shard_map.68 = bf16[4,256,128]{2,1,0:T(8,128)(2,1)S(1)} custom-call(bf16[256,1024]{1,0:T(8,128)(2,1)} %refs_0_.3, bf16[256,1024]{1,0:T(8,128)(2,1)} %refs_1_.3, bf16[256,1024]{1,0:T(8,128)(2,1)} %refs_2_.3, bf16[256,1024]{1,0:T(8,128)(2,1)} %refs_3_.3), custom_call_target="tpu_custom_call" | custom-call | flops 1 | bytes 1 | tf_op jit(solution)/shard_map/pallas_call | solution.py:94
  1.6 0.1 collective-permute-start.1
  1.7 1.8 %shard_map.67 = (bf16[4,256,128]{2,1,0:T(8,128)(2,1)S(1)}, bf16[4,256,128]{2,1,0:T(8,128)(2,1)S(1)}, bf16[4,256,128]{2,1,0:T(8,128)(2,1)S(1)}, bf16[4,256,128]{2...) custom-call(bf16[256,1024]{1,0:T(8,128)(2,1)} %refs_0_.3, ...), custom_call_target="tpu_custom_call" | custom-call | flops 1 | bytes 1 | tf_op jit(solution)/shard_map/pallas_call | solution.py:94
  3.5 1.3 %collective-permute-start = (bf16[4,256,128]{2,1,0:T(8,128)(2,1)S(1)}, bf16[4,256,128]{2,1,0:T(8,128)(2,1)S(1)}, u32[]{:S(2)}, u32[]{:S(2)}) collective-permute-start(bf16[4,256,128]{2,1,0:T(8,128)(2,1)S(1)} %get-tuple-element.24), channel_id=1, source_target_pairs={{0,2},{1,3},{2,0},{3,1},{4,6},{5,7},{6,4},{7,5},{8,10},{9,11},{10,... | collective-permute-start | bytes 786440 | tf_op jit(solution)/shard_map/ppermute | solution.py:243
  4.8 2.3 %collective-permute-start.3 = (bf16[4,256,128]{2,1,0:T(8,128)(2,1)S(1)}, bf16[4,256,128]{2,1,0:T(8,128)(2,1)S(1)}, u32[]{:S(2)}, u32[]{:S(2)}) collective-permute-start(bf16[4,256,128]{2,1,0:T(8,128)(2,1)S(1)} %get-tuple-element.27), channel_id=1, source_target_pairs={{0,10},{1,11},{2,8},{3,9},{4,14},{5,15},{6,12},{7,13},{8,2},{9,3},... | collective-permute-start | bytes 786440 | tf_op jit(solution)/shard_map/ppermute | solution.py:243
  7.1 1.3 %collective-permute-start.2 = (bf16[4,256,128]{2,1,0:T(8,128)(2,1)S(1)}, bf16[4,256,128]{2,1,0:T(8,128)(2,1)S(1)}, u32[]{:S(2)}, u32[]{:S(2)}) collective-permute-start(bf16[4,256,128]{2,1,0:T(8,128)(2,1)S(1)} %get-tuple-element.26), channel_id=1, source_target_pairs={{0,4},{1,5},{2,6},{3,7},{4,0},{5,1},{6,2},{7,3},{8,12},{9,13},{10,... | collective-permute-start | bytes 786440 | tf_op jit(solution)/shard_map/ppermute | solution.py:243
  8.4 0.0 collective-permute-start.5
  8.4 9.6 %collective-permute-done.1.refs_4_ = bf16[4,256,128]{2,1,0:T(8,128)(2,1)S(1)} collective-permute-done((bf16[4,256,128]{2,1,0:T(8,128)(2,1)S(1)}, bf16[4,256,128]{2,1,0:T(8,128)(2,1)S(1)}, u32[]{:S(2)}, u32[]{:S(2)}) %collective-permute-start.1) | collective-permute-done | bytes 262176 | tf_op jit(solution)/shard_map/ppermute | solution.py:243
  18.0 7.2 %collective-permute-start.4 = (bf16[4,256,128]{2,1,0:T(8,128)(2,1)S(1)}, bf16[4,256,128]{2,1,0:T(8,128)(2,1)S(1)}, u32[]{:S(2)}, u32[]{:S(2)}) collective-permute-start(bf16[4,256,128]{2,1,0:T(8,128)(2,1)S(1)} %get-tuple-element.30), channel_id=1, source_target_pairs={{0,6},{1,7},{2,4},{3,5},{4,2},{5,3},{6,0},{7,1},{8,14},{9,15},{10,... | collective-permute-start | bytes 786440 | tf_op jit(solution)/shard_map/ppermute | solution.py:243
  25.2 0.0 collective-permute-done.refs_1_
  25.2 0.0 collective-permute-start.10
  25.2 4.0 %collective-permute-done.3.refs_5_ = bf16[4,256,128]{2,1,0:T(8,128)(2,1)S(1)} collective-permute-done((bf16[4,256,128]{2,1,0:T(8,128)(2,1)S(1)}, bf16[4,256,128]{2,1,0:T(8,128)(2,1)S(1)}, u32[]{:S(2)}, u32[]{:S(2)}) %collective-permute-start.3) | collective-permute-done | bytes 262176 | tf_op jit(solution)/shard_map/ppermute | solution.py:243
  29.3 0.0 collective-permute-done.2.refs_2_
  29.3 16.2 %collective-permute-done.5.refs_6_ = bf16[4,256,128]{2,1,0:T(8,128)(2,1)S(1)} collective-permute-done((bf16[4,256,128]{2,1,0:T(8,128)(2,1)S(1)}, bf16[4,256,128]{2,1,0:T(8,128)(2,1)S(1)}, u32[]{:S(2)}, u32[]{:S(2)}) %collective-permute-start.5) | collective-permute-done | bytes 262176 | tf_op jit(solution)/shard_map/ppermute | solution.py:243
  45.5 0.0 collective-permute-done.4.refs_3_
  45.6 0.1 pad_maximum_fusion.1
  45.7 0.7 %collective-permute-start.7 = (bf16[7,256,128]{2,1,0:T(8,128)(2,1)S(1)}, bf16[7,256,128]{2,1,0:T(8,128)(2,1)S(1)}, u32[]{:S(2)}, u32[]{:S(2)}) collective-permute-start(bf16[7,256,128]{2,1,0:T(8,128)(2,1)S(1)} %pad_maximum_fusion.1), channel_id=1, source_target_pairs={{0,1},{1,0},{2,3},{3,2},{4,5},{5,4},{6,7},{7,6},{8,9},{9,8},{10,11... | collective-permute-start | bytes 1376264 | tf_op jit(solution)/shard_map/ppermute | solution.py:243
  46.3 0.1 pad_maximum_fusion.2
  46.4 0.1 collective-permute-start.8
  46.5 0.5 collective-permute-start.9
  47.0 0.1 collective-permute-start.6
  47.1 1.4 %shard_map.69 = (f32[7,128,128]{2,1,0:T(8,128)S(1)}, f32[7,128,128]{2,1,0:T(8,128)S(1)}, f32[7,3,64,256]{3,2,1,0:T(8,128)S(1)}) custom-call(bf16[4,256,128]{2,1,0:T(8,128)(2,1)S(1)} %get-tuple-element.23.refs_0_, bf16[4,256,128]{2,1,0:T(8,128)(2,1)S(1)} %collective-permute-done.refs_1_, bf16[4,256,128]{2,1,0:T(8,128)(2,1)S(1)} %collective-permute-done.2.refs_2_, ...), custom_call_target="tpu_custom_call" | custom-call | flops 1 | bytes 1 | tf_op jit(solution)/shard_map/pallas_call | solution.py:158
  48.6 1.6 %collective-permute-done.10.refs_4_.refs_11_ = bf16[4,256,128]{2,1,0:T(8,128)(2,1)S(1)} collective-permute-done((bf16[4,256,128]{2,1,0:T(8,128)(2,1)S(1)}, bf16[4,256,128]{2,1,0:T(8,128)(2,1)S(1)}, u32[]{:S(2)}, u32[]{:S(2)}) %collective-permute-start.10) | collective-permute-done | bytes 262176 | tf_op jit(solution)/shard_map/ppermute | solution.py:243
  50.2 0.5 collective-permute-start.11
  50.7 0.0 collective-permute-done.7.refs_1_.refs_8_
  50.7 0.0 collective-permute-done.8.refs_2_.refs_9_
  50.7 0.0 collective-permute-done.9.refs_3_.refs_10_
  50.7 0.0 collective-permute-done.6.refs_0_.refs_7_
  50.7 1.6 %shard_map.70 = (f32[8,128,128]{2,1,0:T(8,128)S(1)}, f32[8,128,128]{2,1,0:T(8,128)S(1)}, f32[8,3,64,256]{3,2,1,0:T(8,128)S(1)}) custom-call(bf16[7,256,128]{2,1,0:T(8,128)(2,1)S(1)} %collective-permute-done.6.refs_0_.refs_7_, bf16[7,256,128]{2,1,0:T(8,128)(2,1)S(1)} %collective-permute-done.7.refs_1_.refs_8_, ...), custom_call_target="tpu_custom_call" | custom-call | flops 1 | bytes 1 | tf_op jit(solution)/shard_map/pallas_call | solution.py:158
  52.3 0.0 collective-permute-done.11.refs_12_
  52.3 2.4 %shard_map.71 = (bf16[64,4096]{1,0:T(8,128)(2,1)}, bf16[64,4096]{1,0:T(8,128)(2,1)}, bf16[64,4096]{1,0:T(8,128)(2,1)}) custom-call(bf16[4,256,128]{2,1,0:T(8,128)(2,1)S(1)} %get-tuple-element.23.refs_0_, bf16[4,256,128]{2,1,0:T(8,128)(2,1)S(1)} %collective-permute-done.refs_1_, bf16[4,256,128]{2,1,0:T(8,128)(2,1)S(1)} %collective-permute-done.2.refs_2_, ...), custom_call_target="tpu_custom_call" | custom-call | tf_op jit(solution)/shard_map/pallas_call | solution.py:222
  (7 shorter events, 0.1 us)
Async XLA Ops:
  1.6 16.4 %collective-permute-start.1 = (bf16[4,256,128]{2,1,0:T(8,128)(2,1)S(1)}, bf16[4,256,128]{2,1,0:T(8,128)(2,1)S(1)}, u32[]{:S(2)}, u32[]{:S(2)}) collective-permute-start(bf16[4,256,128]{2,1,0:T(8,128)(2,1)S(1)} %shard_map.68), channel_id=1, source_target_pairs={{0,8},{1,9},{2,10},{3,11},{4,12},{5,13},{6,14},{7,15},{8,0},{9,1},... | collective-permute-start | bytes 786440 | tf_op jit(solution)/shard_map/ppermute | solution.py:243
  3.5 21.7 %collective-permute-start = (bf16[4,256,128]{2,1,0:T(8,128)(2,1)S(1)}, bf16[4,256,128]{2,1,0:T(8,128)(2,1)S(1)}, u32[]{:S(2)}, u32[]{:S(2)}) collective-permute-start(bf16[4,256,128]{2,1,0:T(8,128)(2,1)S(1)} %get-tuple-element.24), channel_id=1, source_target_pairs={{0,2},{1,3},{2,0},{3,1},{4,6},{5,7},{6,4},{7,5},{8,10},{9,11},{10,... | collective-permute-start | bytes 786440 | tf_op jit(solution)/shard_map/ppermute | solution.py:243
  4.8 24.4 %collective-permute-start.3 = (bf16[4,256,128]{2,1,0:T(8,128)(2,1)S(1)}, bf16[4,256,128]{2,1,0:T(8,128)(2,1)S(1)}, u32[]{:S(2)}, u32[]{:S(2)}) collective-permute-start(bf16[4,256,128]{2,1,0:T(8,128)(2,1)S(1)} %get-tuple-element.27), channel_id=1, source_target_pairs={{0,10},{1,11},{2,8},{3,9},{4,14},{5,15},{6,12},{7,13},{8,2},{9,3},... | collective-permute-start | bytes 786440 | tf_op jit(solution)/shard_map/ppermute | solution.py:243
  7.1 22.2 %collective-permute-start.2 = (bf16[4,256,128]{2,1,0:T(8,128)(2,1)S(1)}, bf16[4,256,128]{2,1,0:T(8,128)(2,1)S(1)}, u32[]{:S(2)}, u32[]{:S(2)}) collective-permute-start(bf16[4,256,128]{2,1,0:T(8,128)(2,1)S(1)} %get-tuple-element.26), channel_id=1, source_target_pairs={{0,4},{1,5},{2,6},{3,7},{4,0},{5,1},{6,2},{7,3},{8,12},{9,13},{10,... | collective-permute-start | bytes 786440 | tf_op jit(solution)/shard_map/ppermute | solution.py:243
  8.4 37.1 %collective-permute-start.5 = (bf16[4,256,128]{2,1,0:T(8,128)(2,1)S(1)}, bf16[4,256,128]{2,1,0:T(8,128)(2,1)S(1)}, u32[]{:S(2)}, u32[]{:S(2)}) collective-permute-start(bf16[4,256,128]{2,1,0:T(8,128)(2,1)S(1)} %get-tuple-element.31), channel_id=1, source_target_pairs={{0,14},{1,15},{2,12},{3,13},{4,10},{5,11},{6,8},{7,9},{8,6},{9,7},... | collective-permute-start | bytes 786440 | tf_op jit(solution)/shard_map/ppermute | solution.py:243
  18.0 27.5 %collective-permute-start.4 = (bf16[4,256,128]{2,1,0:T(8,128)(2,1)S(1)}, bf16[4,256,128]{2,1,0:T(8,128)(2,1)S(1)}, u32[]{:S(2)}, u32[]{:S(2)}) collective-permute-start(bf16[4,256,128]{2,1,0:T(8,128)(2,1)S(1)} %get-tuple-element.30), channel_id=1, source_target_pairs={{0,6},{1,7},{2,4},{3,5},{4,2},{5,3},{6,0},{7,1},{8,14},{9,15},{10,... | collective-permute-start | bytes 786440 | tf_op jit(solution)/shard_map/ppermute | solution.py:243
  25.2 25.0 %collective-permute-start.10 = (bf16[4,256,128]{2,1,0:T(8,128)(2,1)S(1)}, bf16[4,256,128]{2,1,0:T(8,128)(2,1)S(1)}, u32[]{:S(2)}, u32[]{:S(2)}) collective-permute-start(bf16[4,256,128]{2,1,0:T(8,128)(2,1)S(1)} %get-tuple-element.34), channel_id=1, source_target_pairs={{0,12},{1,13},{2,14},{3,15},{4,8},{5,9},{6,10},{7,11},{8,4},{9,5},... | collective-permute-start | bytes 786440 | tf_op jit(solution)/shard_map/ppermute | solution.py:243
  45.7 5.0 %collective-permute-start.7 = (bf16[7,256,128]{2,1,0:T(8,128)(2,1)S(1)}, bf16[7,256,128]{2,1,0:T(8,128)(2,1)S(1)}, u32[]{:S(2)}, u32[]{:S(2)}) collective-permute-start(bf16[7,256,128]{2,1,0:T(8,128)(2,1)S(1)} %pad_maximum_fusion.1), channel_id=1, source_target_pairs={{0,1},{1,0},{2,3},{3,2},{4,5},{5,4},{6,7},{7,6},{8,9},{9,8},{10,11... | collective-permute-start | bytes 1376264 | tf_op jit(solution)/shard_map/ppermute | solution.py:243
  46.4 4.3 %collective-permute-start.8 = (bf16[7,256,128]{2,1,0:T(8,128)(2,1)S(1)}, bf16[7,256,128]{2,1,0:T(8,128)(2,1)S(1)}, u32[]{:S(2)}, u32[]{:S(2)}) collective-permute-start(bf16[7,256,128]{2,1,0:T(8,128)(2,1)S(1)} %pad_maximum_fusion.2), channel_id=1, source_target_pairs={{0,1},{1,0},{2,3},{3,2},{4,5},{5,4},{6,7},{7,6},{8,9},{9,8},{10,11... | collective-permute-start | bytes 1376264 | tf_op jit(solution)/shard_map/ppermute | solution.py:243
  46.5 4.2 %collective-permute-start.9 = (bf16[7,256,128]{2,1,0:T(8,128)(2,1)S(1)}, bf16[7,256,128]{2,1,0:T(8,128)(2,1)S(1)}, u32[]{:S(2)}, u32[]{:S(2)}) collective-permute-start(bf16[7,256,128]{2,1,0:T(8,128)(2,1)S(1)} %pad_maximum_fusion.3), channel_id=1, source_target_pairs={{0,1},{1,0},{2,3},{3,2},{4,5},{5,4},{6,7},{7,6},{8,9},{9,8},{10,11... | collective-permute-start | bytes 1376264 | tf_op jit(solution)/shard_map/ppermute | solution.py:243
  47.0 3.7 %collective-permute-start.6 = (bf16[7,256,128]{2,1,0:T(8,128)(2,1)S(1)}, bf16[7,256,128]{2,1,0:T(8,128)(2,1)S(1)}, u32[]{:S(2)}, u32[]{:S(2)}) collective-permute-start(bf16[7,256,128]{2,1,0:T(8,128)(2,1)S(1)} %pad_maximum_fusion), channel_id=1, source_target_pairs={{0,1},{1,0},{2,3},{3,2},{4,5},{5,4},{6,7},{7,6},{8,9},{9,8},{10,11... | collective-permute-start | bytes 1376264 | tf_op jit(solution)/shard_map/ppermute | solution.py:243
  50.2 2.2 %collective-permute-start.11 = (bf16[4,256,128]{2,1,0:T(8,128)(2,1)S(1)}, bf16[4,256,128]{2,1,0:T(8,128)(2,1)S(1)}, u32[]{:S(2)}, u32[]{:S(2)}) collective-permute-start(bf16[4,256,128]{2,1,0:T(8,128)(2,1)S(1)} %collective-permute-done.10.refs_4_.refs_11_), channel_id=1, source_target_pairs={{0,1},{1,0},{2,3},{3,2},{4,5},{5,4},{6,7},{7,6},{8,9},{9,8},{10,11... | collective-permute-start | bytes 786440 | tf_op jit(solution)/shard_map/ppermute | solution.py:243

commit v7 on v6

--- a/solution.py
+++ b/solution.py
@@ -102,7 +102,7 @@
     return dict(zip(flips, packed))
 
 
-def within_blocks(blocks, core, turned, states, grads, intra):
+def within_blocks(blocks, core, turned, states, grads, intra, meanwhile=lambda: None):
     length = turned.shape[-1]
     half = HDIM // CORES
     own_rows = pl.ds(pl.multiple_of(core * half, half), half)
@@ -112,6 +112,7 @@
     masked = lambda x: jnp.where(causal, x, 0.0).astype(jnp.bfloat16)
     scores_gv = [masked(dot(block[3], block[2], NT)) for block in blocks]
     scores_qk = [masked(dot(block[0], block[1], NT)) for block in blocks]
+    meanwhile()
     for i, block in enumerate(blocks):
         for j, t in enumerate((1, 0, 3)):
             turned[i, j] = block[t].T
@@ -176,42 +177,50 @@
     chip, core = place()
     half, length = HDIM // CORES, turned.shape[-1]
     own_rows = pl.ds(pl.multiple_of(core * half, half), half)
-    within_blocks(blocks[n_blocks - sizes[-1] :], core, turned, *last)
     done.append(last)
-
-    found = []
-    for size, (states, grads, intra) in zip(sizes, done):
-        for i in range(size):
-            flip, other = slots[len(found)]
-            b = (chip ^ flip) * CORES + (core ^ other)
+    counts = [(states, grads, i) for size, (states, grads, _) in zip(sizes, done) for i in range(size)]
+    found = [(chip ^ flip) * CORES + (core ^ other) for flip, other in slots]
+    intra = [ref.at[i] for size, (_, _, ref) in zip(sizes, done) for i in range(size)]
+
+    def put(first, end):
+        for (states, grads, i), b in list(zip(counts, found))[first:end]:
             in_order[b, 0] = states[i]
             in_order[b, 1] = grads[i]
-            found.append((b, intra.at[i]))
+
+    early = n_blocks - sizes[-1]
+    within_blocks(blocks[early:], core, turned, *last, meanwhile=lambda: put(0, early))
+    put(early, n_blocks)
 
     total = jnp.zeros((HDIM, HDIM), jnp.float32)
     for b in range(n_blocks):
         state_half[b] = total.astype(jnp.bfloat16)
         total = total + in_order[b, 0]
-    total = jnp.zeros((HDIM, HDIM), jnp.float32)
-    for b in reversed(range(n_blocks)):
-        rounded = total.astype(jnp.bfloat16)
-        grad_half[b, 0] = rounded
-        grad_half[b, 1] = rounded.T
-        total = total + in_order[b, 1]
 
     copies = []
-    factors = (
-        lambda b: state_half[b, own_rows, :],
-        lambda b: grad_half[b, 0, own_rows, :],
-        lambda b: grad_half[b, 1, own_rows, :],
-    )
-    for j, (factor, t) in enumerate(zip(factors, (3, 2, 1))):
-        for block, (b, intra) in zip(blocks, found):
-            columns = pl.ds(pl.multiple_of(b * length, length), length)
-            total = intra[j] + dot(factor(b), block[t], NT)
-            ready[j, :, columns] = total.astype(ready.dtype)
+
+    def product(j, i, factor, t):
+        columns = pl.ds(pl.multiple_of(found[i] * length, length), length)
+        total = intra[i][j] + dot(factor, blocks[i][t], NT)
+        ready[j, :, columns] = total.astype(ready.dtype)
+
+    def leave(j):
         copies.append(pltpu.make_async_copy(ready.at[j], outs[j], sems.at[j]))
         copies[-1].start()
+
+    total = jnp.zeros((HDIM, HDIM), jnp.float32)
+    for i in range(n_blocks):
+        product(0, i, state_half[found[i], own_rows, :], 3)
+        b = n_blocks - 1 - i
+        grad_half[b, 0] = total.astype(jnp.bfloat16)
+        total = total + in_order[b, 1]
+    leave(0)
+    for i in range(n_blocks):
+        product(1, i, grad_half[found[i], 0, own_rows, :], 2)
+        grad_half[i, 1] = grad_half[i, 0].T
+    leave(1)
+    for i in range(n_blocks):
+        product(2, i, grad_half[found[i], 1, own_rows, :], 1)
+    leave(2)
     for copy in copies:
         copy.wait()
 

time: 55 us -> 54.8 us (level)
  no operation moved by 1% of the time
where the time goes in v7:
time: 54.8 us; the launch traced here: 54.6 us
  waiting for transfers between devices  31.5 us (57%)
  starting transfers between devices  14.1 us (26%)
  Pallas kernels  8.06 us (15%)
  between operations  0.72 us (1%)
    ppermute x12, waiting for transfers between devices, chip_body(): lax.ppermute(x, 'seq', [(i, i ^ flip) for i in range(size)])  31.5 us
    ppermute x12, starting transfers between devices, chip_body(): lax.ppermute(x, 'seq', [(i, i ^ flip) for i in range(size)])  14.1 us
    pallas_call x2, Pallas kernels, within(): pl.pallas_call(functools.partial(within_kernel, where, len(arrays)), out_...  3.08 us
    pallas_call x2, Pallas kernels, pack(): pl.pallas_call(functools.partial(pack_kernel, flips), out_shape=[shape] *...  2.76 us
    pallas_call x1, Pallas kernels, finish(): pl.pallas_call(functools.partial(finish_kernel, where, slots, sizes, len(...  2.21 us
  transfers between devices with their start and end apart: 12, of which 4 were waited for; matrix products, arithmetic and copies ran while one was open for 0% of the time, Pallas kernels for 9%

profile of v7, /device:TPU:19, one launch (start us, length us, event | category | flops | bytes accessed | tf_op | source)
XLA Modules:
  0.0 54.6 jit_solution(10561969526144990017)
XLA Ops:
  0.6 1.0 %shard_map.68 = bf16[4,256,128]{2,1,0:T(8,128)(2,1)S(1)} custom-call(bf16[256,1024]{1,0:T(8,128)(2,1)} %refs_0_.3, bf16[256,1024]{1,0:T(8,128)(2,1)} %refs_1_.3, bf16[256,1024]{1,0:T(8,128)(2,1)} %refs_2_.3, bf16[256,1024]{1,0:T(8,128)(2,1)} %refs_3_.3), custom_call_target="tpu_custom_call" | custom-call | flops 1 | bytes 1 | tf_op jit(solution)/shard_map/pallas_call | solution.py:94
  1.6 0.1 collective-permute-start.1
  1.7 1.8 %shard_map.67 = (bf16[4,256,128]{2,1,0:T(8,128)(2,1)S(1)}, bf16[4,256,128]{2,1,0:T(8,128)(2,1)S(1)}, bf16[4,256,128]{2,1,0:T(8,128)(2,1)S(1)}, bf16[4,256,128]{2...) custom-call(bf16[256,1024]{1,0:T(8,128)(2,1)} %refs_0_.3, ...), custom_call_target="tpu_custom_call" | custom-call | flops 1 | bytes 1 | tf_op jit(solution)/shard_map/pallas_call | solution.py:94
  3.5 1.3 %collective-permute-start = (bf16[4,256,128]{2,1,0:T(8,128)(2,1)S(1)}, bf16[4,256,128]{2,1,0:T(8,128)(2,1)S(1)}, u32[]{:S(2)}, u32[]{:S(2)}) collective-permute-start(bf16[4,256,128]{2,1,0:T(8,128)(2,1)S(1)} %get-tuple-element.24), channel_id=1, source_target_pairs={{0,2},{1,3},{2,0},{3,1},{4,6},{5,7},{6,4},{7,5},{8,10},{9,11},{10,... | collective-permute-start | bytes 786440 | tf_op jit(solution)/shard_map/ppermute | solution.py:252
  4.8 2.3 %collective-permute-start.3 = (bf16[4,256,128]{2,1,0:T(8,128)(2,1)S(1)}, bf16[4,256,128]{2,1,0:T(8,128)(2,1)S(1)}, u32[]{:S(2)}, u32[]{:S(2)}) collective-permute-start(bf16[4,256,128]{2,1,0:T(8,128)(2,1)S(1)} %get-tuple-element.27), channel_id=1, source_target_pairs={{0,10},{1,11},{2,8},{3,9},{4,14},{5,15},{6,12},{7,13},{8,2},{9,3},... | collective-permute-start | bytes 786440 | tf_op jit(solution)/shard_map/ppermute | solution.py:252
  7.1 1.3 %collective-permute-start.2 = (bf16[4,256,128]{2,1,0:T(8,128)(2,1)S(1)}, bf16[4,256,128]{2,1,0:T(8,128)(2,1)S(1)}, u32[]{:S(2)}, u32[]{:S(2)}) collective-permute-start(bf16[4,256,128]{2,1,0:T(8,128)(2,1)S(1)} %get-tuple-element.26), channel_id=1, source_target_pairs={{0,4},{1,5},{2,6},{3,7},{4,0},{5,1},{6,2},{7,3},{8,12},{9,13},{10,... | collective-permute-start | bytes 786440 | tf_op jit(solution)/shard_map/ppermute | solution.py:252
  8.4 0.0 collective-permute-start.5
  8.4 9.6 %collective-permute-done.1.refs_4_ = bf16[4,256,128]{2,1,0:T(8,128)(2,1)S(1)} collective-permute-done((bf16[4,256,128]{2,1,0:T(8,128)(2,1)S(1)}, bf16[4,256,128]{2,1,0:T(8,128)(2,1)S(1)}, u32[]{:S(2)}, u32[]{:S(2)}) %collective-permute-start.1) | collective-permute-done | bytes 262176 | tf_op jit(solution)/shard_map/ppermute | solution.py:252
  18.0 7.2 %collective-permute-start.4 = (bf16[4,256,128]{2,1,0:T(8,128)(2,1)S(1)}, bf16[4,256,128]{2,1,0:T(8,128)(2,1)S(1)}, u32[]{:S(2)}, u32[]{:S(2)}) collective-permute-start(bf16[4,256,128]{2,1,0:T(8,128)(2,1)S(1)} %get-tuple-element.30), channel_id=1, source_target_pairs={{0,6},{1,7},{2,4},{3,5},{4,2},{5,3},{6,0},{7,1},{8,14},{9,15},{10,... | collective-permute-start | bytes 786440 | tf_op jit(solution)/shard_map/ppermute | solution.py:252
  25.2 0.0 collective-permute-done.refs_1_
  25.2 0.0 collective-permute-start.10
  25.2 4.0 %collective-permute-done.3.refs_5_ = bf16[4,256,128]{2,1,0:T(8,128)(2,1)S(1)} collective-permute-done((bf16[4,256,128]{2,1,0:T(8,128)(2,1)S(1)}, bf16[4,256,128]{2,1,0:T(8,128)(2,1)S(1)}, u32[]{:S(2)}, u32[]{:S(2)}) %collective-permute-start.3) | collective-permute-done | bytes 262176 | tf_op jit(solution)/shard_map/ppermute | solution.py:252
  29.3 0.0 collective-permute-done.2.refs_2_
  29.3 16.2 %collective-permute-done.5.refs_6_ = bf16[4,256,128]{2,1,0:T(8,128)(2,1)S(1)} collective-permute-done((bf16[4,256,128]{2,1,0:T(8,128)(2,1)S(1)}, bf16[4,256,128]{2,1,0:T(8,128)(2,1)S(1)}, u32[]{:S(2)}, u32[]{:S(2)}) %collective-permute-start.5) | collective-permute-done | bytes 262176 | tf_op jit(solution)/shard_map/ppermute | solution.py:252
  45.5 0.0 collective-permute-done.4.refs_3_
  45.6 0.1 pad_maximum_fusion.1
  45.7 0.7 %collective-permute-start.7 = (bf16[7,256,128]{2,1,0:T(8,128)(2,1)S(1)}, bf16[7,256,128]{2,1,0:T(8,128)(2,1)S(1)}, u32[]{:S(2)}, u32[]{:S(2)}) collective-permute-start(bf16[7,256,128]{2,1,0:T(8,128)(2,1)S(1)} %pad_maximum_fusion.1), channel_id=1, source_target_pairs={{0,1},{1,0},{2,3},{3,2},{4,5},{5,4},{6,7},{7,6},{8,9},{9,8},{10,11... | collective-permute-start | bytes 1376264 | tf_op jit(solution)/shard_map/ppermute | solution.py:252
  46.3 0.1 pad_maximum_fusion.2
  46.4 0.1 collective-permute-start.8
  46.5 0.5 collective-permute-start.9
  47.0 0.1 collective-permute-start.6
  47.1 1.4 %shard_map.69 = (f32[7,128,128]{2,1,0:T(8,128)S(1)}, f32[7,128,128]{2,1,0:T(8,128)S(1)}, f32[7,3,64,256]{3,2,1,0:T(8,128)S(1)}) custom-call(bf16[4,256,128]{2,1,0:T(8,128)(2,1)S(1)} %get-tuple-element.23.refs_0_, bf16[4,256,128]{2,1,0:T(8,128)(2,1)S(1)} %collective-permute-done.refs_1_, bf16[4,256,128]{2,1,0:T(8,128)(2,1)S(1)} %collective-permute-done.2.refs_2_, ...), custom_call_target="tpu_custom_call" | custom-call | flops 1 | bytes 1 | tf_op jit(solution)/shard_map/pallas_call | solution.py:159
  48.6 1.6 %collective-permute-done.10.refs_4_.refs_11_ = bf16[4,256,128]{2,1,0:T(8,128)(2,1)S(1)} collective-permute-done((bf16[4,256,128]{2,1,0:T(8,128)(2,1)S(1)}, bf16[4,256,128]{2,1,0:T(8,128)(2,1)S(1)}, u32[]{:S(2)}, u32[]{:S(2)}) %collective-permute-start.10) | collective-permute-done | bytes 262176 | tf_op jit(solution)/shard_map/ppermute | solution.py:252
  50.2 0.5 collective-permute-start.11
  50.7 0.0 collective-permute-done.7.refs_1_.refs_8_
  50.7 0.0 collective-permute-done.8.refs_2_.refs_9_
  50.7 0.0 collective-permute-done.9.refs_3_.refs_10_
  50.7 0.0 collective-permute-done.6.refs_0_.refs_7_
  50.7 1.6 %shard_map.70 = (f32[8,128,128]{2,1,0:T(8,128)S(1)}, f32[8,128,128]{2,1,0:T(8,128)S(1)}, f32[8,3,64,256]{3,2,1,0:T(8,128)S(1)}) custom-call(bf16[7,256,128]{2,1,0:T(8,128)(2,1)S(1)} %collective-permute-done.6.refs_0_.refs_7_, bf16[7,256,128]{2,1,0:T(8,128)(2,1)S(1)} %collective-permute-done.7.refs_1_.refs_8_, ...), custom_call_target="tpu_custom_call" | custom-call | flops 1 | bytes 1 | tf_op jit(solution)/shard_map/pallas_call | solution.py:159
  52.3 0.0 collective-permute-done.11.refs_12_
  52.3 2.2 %shard_map.71 = (bf16[64,4096]{1,0:T(8,128)(2,1)}, bf16[64,4096]{1,0:T(8,128)(2,1)}, bf16[64,4096]{1,0:T(8,128)(2,1)}) custom-call(bf16[4,256,128]{2,1,0:T(8,128)(2,1)S(1)} %get-tuple-element.23.refs_0_, bf16[4,256,128]{2,1,0:T(8,128)(2,1)S(1)} %collective-permute-done.refs_1_, bf16[4,256,128]{2,1,0:T(8,128)(2,1)S(1)} %collective-permute-done.2.refs_2_, ...), custom_call_target="tpu_custom_call" | custom-call | tf_op jit(solution)/shard_map/pallas_call | solution.py:231
  (7 shorter events, 0.1 us)
Async XLA Ops:
  1.6 16.4 %collective-permute-start.1 = (bf16[4,256,128]{2,1,0:T(8,128)(2,1)S(1)}, bf16[4,256,128]{2,1,0:T(8,128)(2,1)S(1)}, u32[]{:S(2)}, u32[]{:S(2)}) collective-permute-start(bf16[4,256,128]{2,1,0:T(8,128)(2,1)S(1)} %shard_map.68), channel_id=1, source_target_pairs={{0,8},{1,9},{2,10},{3,11},{4,12},{5,13},{6,14},{7,15},{8,0},{9,1},... | collective-permute-start | bytes 786440 | tf_op jit(solution)/shard_map/ppermute | solution.py:252
  3.5 21.7 %collective-permute-start = (bf16[4,256,128]{2,1,0:T(8,128)(2,1)S(1)}, bf16[4,256,128]{2,1,0:T(8,128)(2,1)S(1)}, u32[]{:S(2)}, u32[]{:S(2)}) collective-permute-start(bf16[4,256,128]{2,1,0:T(8,128)(2,1)S(1)} %get-tuple-element.24), channel_id=1, source_target_pairs={{0,2},{1,3},{2,0},{3,1},{4,6},{5,7},{6,4},{7,5},{8,10},{9,11},{10,... | collective-permute-start | bytes 786440 | tf_op jit(solution)/shard_map/ppermute | solution.py:252
  4.8 24.4 %collective-permute-start.3 = (bf16[4,256,128]{2,1,0:T(8,128)(2,1)S(1)}, bf16[4,256,128]{2,1,0:T(8,128)(2,1)S(1)}, u32[]{:S(2)}, u32[]{:S(2)}) collective-permute-start(bf16[4,256,128]{2,1,0:T(8,128)(2,1)S(1)} %get-tuple-element.27), channel_id=1, source_target_pairs={{0,10},{1,11},{2,8},{3,9},{4,14},{5,15},{6,12},{7,13},{8,2},{9,3},... | collective-permute-start | bytes 786440 | tf_op jit(solution)/shard_map/ppermute | solution.py:252
  7.1 22.2 %collective-permute-start.2 = (bf16[4,256,128]{2,1,0:T(8,128)(2,1)S(1)}, bf16[4,256,128]{2,1,0:T(8,128)(2,1)S(1)}, u32[]{:S(2)}, u32[]{:S(2)}) collective-permute-start(bf16[4,256,128]{2,1,0:T(8,128)(2,1)S(1)} %get-tuple-element.26), channel_id=1, source_target_pairs={{0,4},{1,5},{2,6},{3,7},{4,0},{5,1},{6,2},{7,3},{8,12},{9,13},{10,... | collective-permute-start | bytes 786440 | tf_op jit(solution)/shard_map/ppermute | solution.py:252
  8.4 37.1 %collective-permute-start.5 = (bf16[4,256,128]{2,1,0:T(8,128)(2,1)S(1)}, bf16[4,256,128]{2,1,0:T(8,128)(2,1)S(1)}, u32[]{:S(2)}, u32[]{:S(2)}) collective-permute-start(bf16[4,256,128]{2,1,0:T(8,128)(2,1)S(1)} %get-tuple-element.31), channel_id=1, source_target_pairs={{0,14},{1,15},{2,12},{3,13},{4,10},{5,11},{6,8},{7,9},{8,6},{9,7},... | collective-permute-start | bytes 786440 | tf_op jit(solution)/shard_map/ppermute | solution.py:252
  18.0 27.5 %collective-permute-start.4 = (bf16[4,256,128]{2,1,0:T(8,128)(2,1)S(1)}, bf16[4,256,128]{2,1,0:T(8,128)(2,1)S(1)}, u32[]{:S(2)}, u32[]{:S(2)}) collective-permute-start(bf16[4,256,128]{2,1,0:T(8,128)(2,1)S(1)} %get-tuple-element.30), channel_id=1, source_target_pairs={{0,6},{1,7},{2,4},{3,5},{4,2},{5,3},{6,0},{7,1},{8,14},{9,15},{10,... | collective-permute-start | bytes 786440 | tf_op jit(solution)/shard_map/ppermute | solution.py:252
  25.2 25.0 %collective-permute-start.10 = (bf16[4,256,128]{2,1,0:T(8,128)(2,1)S(1)}, bf16[4,256,128]{2,1,0:T(8,128)(2,1)S(1)}, u32[]{:S(2)}, u32[]{:S(2)}) collective-permute-start(bf16[4,256,128]{2,1,0:T(8,128)(2,1)S(1)} %get-tuple-element.34), channel_id=1, source_target_pairs={{0,12},{1,13},{2,14},{3,15},{4,8},{5,9},{6,10},{7,11},{8,4},{9,5},... | collective-permute-start | bytes 786440 | tf_op jit(solution)/shard_map/ppermute | solution.py:252
  45.7 5.0 %collective-permute-start.7 = (bf16[7,256,128]{2,1,0:T(8,128)(2,1)S(1)}, bf16[7,256,128]{2,1,0:T(8,128)(2,1)S(1)}, u32[]{:S(2)}, u32[]{:S(2)}) collective-permute-start(bf16[7,256,128]{2,1,0:T(8,128)(2,1)S(1)} %pad_maximum_fusion.1), channel_id=1, source_target_pairs={{0,1},{1,0},{2,3},{3,2},{4,5},{5,4},{6,7},{7,6},{8,9},{9,8},{10,11... | collective-permute-start | bytes 1376264 | tf_op jit(solution)/shard_map/ppermute | solution.py:252
  46.4 4.3 %collective-permute-start.8 = (bf16[7,256,128]{2,1,0:T(8,128)(2,1)S(1)}, bf16[7,256,128]{2,1,0:T(8,128)(2,1)S(1)}, u32[]{:S(2)}, u32[]{:S(2)}) collective-permute-start(bf16[7,256,128]{2,1,0:T(8,128)(2,1)S(1)} %pad_maximum_fusion.2), channel_id=1, source_target_pairs={{0,1},{1,0},{2,3},{3,2},{4,5},{5,4},{6,7},{7,6},{8,9},{9,8},{10,11... | collective-permute-start | bytes 1376264 | tf_op jit(solution)/shard_map/ppermute | solution.py:252
  46.5 4.2 %collective-permute-start.9 = (bf16[7,256,128]{2,1,0:T(8,128)(2,1)S(1)}, bf16[7,256,128]{2,1,0:T(8,128)(2,1)S(1)}, u32[]{:S(2)}, u32[]{:S(2)}) collective-permute-start(bf16[7,256,128]{2,1,0:T(8,128)(2,1)S(1)} %pad_maximum_fusion.3), channel_id=1, source_target_pairs={{0,1},{1,0},{2,3},{3,2},{4,5},{5,4},{6,7},{7,6},{8,9},{9,8},{10,11... | collective-permute-start | bytes 1376264 | tf_op jit(solution)/shard_map/ppermute | solution.py:252
  47.0 3.7 %collective-permute-start.6 = (bf16[7,256,128]{2,1,0:T(8,128)(2,1)S(1)}, bf16[7,256,128]{2,1,0:T(8,128)(2,1)S(1)}, u32[]{:S(2)}, u32[]{:S(2)}) collective-permute-start(bf16[7,256,128]{2,1,0:T(8,128)(2,1)S(1)} %pad_maximum_fusion), channel_id=1, source_target_pairs={{0,1},{1,0},{2,3},{3,2},{4,5},{5,4},{6,7},{7,6},{8,9},{9,8},{10,11... | collective-permute-start | bytes 1376264 | tf_op jit(solution)/shard_map/ppermute | solution.py:252
  50.2 2.2 %collective-permute-start.11 = (bf16[4,256,128]{2,1,0:T(8,128)(2,1)S(1)}, bf16[4,256,128]{2,1,0:T(8,128)(2,1)S(1)}, u32[]{:S(2)}, u32[]{:S(2)}) collective-permute-start(bf16[4,256,128]{2,1,0:T(8,128)(2,1)S(1)} %collective-permute-done.10.refs_4_.refs_11_), channel_id=1, source_target_pairs={{0,1},{1,0},{2,3},{3,2},{4,5},{5,4},{6,7},{7,6},{8,9},{9,8},{10,11... | collective-permute-start | bytes 786440 | tf_op jit(solution)/shard_map/ppermute | solution.py:252

commit v8 on v7

--- a/solution.py
+++ b/solution.py
@@ -102,14 +102,33 @@
     return dict(zip(flips, packed))
 
 
-def within_blocks(blocks, core, turned, states, grads, intra, meanwhile=lambda: None):
-    length = turned.shape[-1]
+def setting(core, length):
     half = HDIM // CORES
     own_rows = pl.ds(pl.multiple_of(core * half, half), half)
     row = lax.broadcasted_iota(jnp.int32, (length, length), 0)
     column = lax.broadcasted_iota(jnp.int32, (length, length), 1)
-    causal = row >= column
-    masked = lambda x: jnp.where(causal, x, 0.0).astype(jnp.bfloat16)
+    return own_rows, lambda x: jnp.where(row >= column, x, 0.0).astype(jnp.bfloat16)
+
+
+def within_blocks(blocks, core, turned, states, grads, intra):
+    own_rows, masked = setting(core, turned.shape[-1])
+    scores_gv, scores_qk = [], []
+    for i, block in enumerate(blocks):
+        for j, t in enumerate((1, 0, 3)):
+            turned[i, j] = block[t].T
+        scores_gv.append(masked(dot(block[3], block[2], NT)))
+    for i, block in enumerate(blocks):
+        scores_qk.append(masked(dot(block[0], block[1], NT)))
+        intra[i, 0] = dot(turned[i, 0, own_rows, :], scores_gv[i], NT)
+        intra[i, 1] = dot(turned[i, 1, own_rows, :], scores_gv[i], NN)
+    for i, block in enumerate(blocks):
+        states[i] = dot(turned[i, 0], block[2], NN)
+        grads[i] = dot(turned[i, 1], block[3], NN)
+        intra[i, 2] = dot(turned[i, 2, own_rows, :], scores_qk[i], NN)
+
+
+def within_last(blocks, core, turned, states, grads, intra, meanwhile):
+    own_rows, masked = setting(core, turned.shape[-1])
     scores_gv = [masked(dot(block[3], block[2], NT)) for block in blocks]
     scores_qk = [masked(dot(block[0], block[1], NT)) for block in blocks]
     meanwhile()
@@ -188,7 +207,7 @@
             in_order[b, 1] = grads[i]
 
     early = n_blocks - sizes[-1]
-    within_blocks(blocks[early:], core, turned, *last, meanwhile=lambda: put(0, early))
+    within_last(blocks[early:], core, turned, *last, meanwhile=lambda: put(0, early))
     put(early, n_blocks)
 
     total = jnp.zeros((HDIM, HDIM), jnp.float32)

time: 54.8 us -> 54.7 us (level)
  transfers between devices with their start and end apart: 12 -> 12, of which waited for: 4 -> 4; matrix products, arithmetic and copies ran while one was open for 0% -> 0% of each run, Pallas kernels for 9% -> 8%
where the time goes in v8:
time: 54.7 us; the launch traced here: 54.4 us
  waiting for transfers between devices  31.6 us (58%)
  starting transfers between devices  14.1 us (26%)
  Pallas kernels  7.79 us (14%)
  between operations  0.74 us (1%)
    ppermute x12, waiting for transfers between devices, chip_body(): lax.ppermute(x, 'seq', [(i, i ^ flip) for i in range(size)])  31.6 us
    ppermute x12, starting transfers between devices, chip_body(): lax.ppermute(x, 'seq', [(i, i ^ flip) for i in range(size)])  14.1 us
    pallas_call x2, Pallas kernels, within(): pl.pallas_call(functools.partial(within_kernel, where, len(arrays)), out_...  2.82 us
    pallas_call x2, Pallas kernels, pack(): pl.pallas_call(functools.partial(pack_kernel, flips), out_shape=[shape] *...  2.76 us
    pallas_call x1, Pallas kernels, finish(): pl.pallas_call(functools.partial(finish_kernel, where, slots, sizes, len(...  2.21 us
  transfers between devices with their start and end apart: 12, of which 4 were waited for; matrix products, arithmetic and copies ran while one was open for 0% of the time, Pallas kernels for 8%

profile of v8, /device:TPU:19, one launch (start us, length us, event | category | flops | bytes accessed | tf_op | source)
XLA Modules:
  0.0 54.4 jit_solution(1301120710925425422)
XLA Ops:
  0.6 1.0 %shard_map.68 = bf16[4,256,128]{2,1,0:T(8,128)(2,1)S(1)} custom-call(bf16[256,1024]{1,0:T(8,128)(2,1)} %refs_0_.3, bf16[256,1024]{1,0:T(8,128)(2,1)} %refs_1_.3, bf16[256,1024]{1,0:T(8,128)(2,1)} %refs_2_.3, bf16[256,1024]{1,0:T(8,128)(2,1)} %refs_3_.3), custom_call_target="tpu_custom_call" | custom-call | flops 1 | bytes 1 | tf_op jit(solution)/shard_map/pallas_call | solution.py:94
  1.6 0.1 collective-permute-start.1
  1.7 1.8 %shard_map.67 = (bf16[4,256,128]{2,1,0:T(8,128)(2,1)S(1)}, bf16[4,256,128]{2,1,0:T(8,128)(2,1)S(1)}, bf16[4,256,128]{2,1,0:T(8,128)(2,1)S(1)}, bf16[4,256,128]{2...) custom-call(bf16[256,1024]{1,0:T(8,128)(2,1)} %refs_0_.3, ...), custom_call_target="tpu_custom_call" | custom-call | flops 1 | bytes 1 | tf_op jit(solution)/shard_map/pallas_call | solution.py:94
  3.5 1.3 %collective-permute-start = (bf16[4,256,128]{2,1,0:T(8,128)(2,1)S(1)}, bf16[4,256,128]{2,1,0:T(8,128)(2,1)S(1)}, u32[]{:S(2)}, u32[]{:S(2)}) collective-permute-start(bf16[4,256,128]{2,1,0:T(8,128)(2,1)S(1)} %get-tuple-element.24), channel_id=1, source_target_pairs={{0,2},{1,3},{2,0},{3,1},{4,6},{5,7},{6,4},{7,5},{8,10},{9,11},{10,... | collective-permute-start | bytes 786440 | tf_op jit(solution)/shard_map/ppermute | solution.py:271
  4.8 2.3 %collective-permute-start.3 = (bf16[4,256,128]{2,1,0:T(8,128)(2,1)S(1)}, bf16[4,256,128]{2,1,0:T(8,128)(2,1)S(1)}, u32[]{:S(2)}, u32[]{:S(2)}) collective-permute-start(bf16[4,256,128]{2,1,0:T(8,128)(2,1)S(1)} %get-tuple-element.27), channel_id=1, source_target_pairs={{0,10},{1,11},{2,8},{3,9},{4,14},{5,15},{6,12},{7,13},{8,2},{9,3},... | collective-permute-start | bytes 786440 | tf_op jit(solution)/shard_map/ppermute | solution.py:271
  7.1 1.3 %collective-permute-start.2 = (bf16[4,256,128]{2,1,0:T(8,128)(2,1)S(1)}, bf16[4,256,128]{2,1,0:T(8,128)(2,1)S(1)}, u32[]{:S(2)}, u32[]{:S(2)}) collective-permute-start(bf16[4,256,128]{2,1,0:T(8,128)(2,1)S(1)} %get-tuple-element.26), channel_id=1, source_target_pairs={{0,4},{1,5},{2,6},{3,7},{4,0},{5,1},{6,2},{7,3},{8,12},{9,13},{10,... | collective-permute-start | bytes 786440 | tf_op jit(solution)/shard_map/ppermute | solution.py:271
  8.4 0.0 collective-permute-start.5
  8.4 9.6 %collective-permute-done.1.refs_4_ = bf16[4,256,128]{2,1,0:T(8,128)(2,1)S(1)} collective-permute-done((bf16[4,256,128]{2,1,0:T(8,128)(2,1)S(1)}, bf16[4,256,128]{2,1,0:T(8,128)(2,1)S(1)}, u32[]{:S(2)}, u32[]{:S(2)}) %collective-permute-start.1) | collective-permute-done | bytes 262176 | tf_op jit(solution)/shard_map/ppermute | solution.py:271
  18.0 7.2 %collective-permute-start.4 = (bf16[4,256,128]{2,1,0:T(8,128)(2,1)S(1)}, bf16[4,256,128]{2,1,0:T(8,128)(2,1)S(1)}, u32[]{:S(2)}, u32[]{:S(2)}) collective-permute-start(bf16[4,256,128]{2,1,0:T(8,128)(2,1)S(1)} %get-tuple-element.30), channel_id=1, source_target_pairs={{0,6},{1,7},{2,4},{3,5},{4,2},{5,3},{6,0},{7,1},{8,14},{9,15},{10,... | collective-permute-start | bytes 786440 | tf_op jit(solution)/shard_map/ppermute | solution.py:271
  25.2 0.0 collective-permute-done.refs_1_
  25.2 0.0 collective-permute-start.10
  25.2 4.0 %collective-permute-done.3.refs_5_ = bf16[4,256,128]{2,1,0:T(8,128)(2,1)S(1)} collective-permute-done((bf16[4,256,128]{2,1,0:T(8,128)(2,1)S(1)}, bf16[4,256,128]{2,1,0:T(8,128)(2,1)S(1)}, u32[]{:S(2)}, u32[]{:S(2)}) %collective-permute-start.3) | collective-permute-done | bytes 262176 | tf_op jit(solution)/shard_map/ppermute | solution.py:271
  29.3 0.0 collective-permute-done.2.refs_2_
  29.3 16.2 %collective-permute-done.5.refs_6_ = bf16[4,256,128]{2,1,0:T(8,128)(2,1)S(1)} collective-permute-done((bf16[4,256,128]{2,1,0:T(8,128)(2,1)S(1)}, bf16[4,256,128]{2,1,0:T(8,128)(2,1)S(1)}, u32[]{:S(2)}, u32[]{:S(2)}) %collective-permute-start.5) | collective-permute-done | bytes 262176 | tf_op jit(solution)/shard_map/ppermute | solution.py:271
  45.5 0.0 collective-permute-done.4.refs_3_
  45.6 0.1 pad_maximum_fusion.1
  45.7 0.7 %collective-permute-start.7 = (bf16[7,256,128]{2,1,0:T(8,128)(2,1)S(1)}, bf16[7,256,128]{2,1,0:T(8,128)(2,1)S(1)}, u32[]{:S(2)}, u32[]{:S(2)}) collective-permute-start(bf16[7,256,128]{2,1,0:T(8,128)(2,1)S(1)} %pad_maximum_fusion.1), channel_id=1, source_target_pairs={{0,1},{1,0},{2,3},{3,2},{4,5},{5,4},{6,7},{7,6},{8,9},{9,8},{10,11... | collective-permute-start | bytes 1376264 | tf_op jit(solution)/shard_map/ppermute | solution.py:271
  46.3 0.1 pad_maximum_fusion.2
  46.4 0.1 collective-permute-start.8
  46.5 0.5 collective-permute-start.9
  47.0 0.1 collective-permute-start.6
  47.1 1.3 %shard_map.69 = (f32[7,128,128]{2,1,0:T(8,128)S(1)}, f32[7,128,128]{2,1,0:T(8,128)S(1)}, f32[7,3,64,256]{3,2,1,0:T(8,128)S(1)}) custom-call(bf16[4,256,128]{2,1,0:T(8,128)(2,1)S(1)} %get-tuple-element.23.refs_0_, bf16[4,256,128]{2,1,0:T(8,128)(2,1)S(1)} %collective-permute-done.refs_1_, bf16[4,256,128]{2,1,0:T(8,128)(2,1)S(1)} %collective-permute-done.2.refs_2_, ...), custom_call_target="tpu_custom_call" | custom-call | flops 1 | bytes 1 | tf_op jit(solution)/shard_map/pallas_call | solution.py:178
  48.5 1.7 %collective-permute-done.10.refs_4_.refs_11_ = bf16[4,256,128]{2,1,0:T(8,128)(2,1)S(1)} collective-permute-done((bf16[4,256,128]{2,1,0:T(8,128)(2,1)S(1)}, bf16[4,256,128]{2,1,0:T(8,128)(2,1)S(1)}, u32[]{:S(2)}, u32[]{:S(2)}) %collective-permute-start.10) | collective-permute-done | bytes 262176 | tf_op jit(solution)/shard_map/ppermute | solution.py:271
  50.2 0.5 collective-permute-start.11
  50.7 0.0 collective-permute-done.7.refs_1_.refs_8_
  50.7 0.0 collective-permute-done.8.refs_2_.refs_9_
  50.7 0.0 collective-permute-done.9.refs_3_.refs_10_
  50.7 0.0 collective-permute-done.6.refs_0_.refs_7_
  50.7 1.5 %shard_map.70 = (f32[8,128,128]{2,1,0:T(8,128)S(1)}, f32[8,128,128]{2,1,0:T(8,128)S(1)}, f32[8,3,64,256]{3,2,1,0:T(8,128)S(1)}) custom-call(bf16[7,256,128]{2,1,0:T(8,128)(2,1)S(1)} %collective-permute-done.6.refs_0_.refs_7_, bf16[7,256,128]{2,1,0:T(8,128)(2,1)S(1)} %collective-permute-done.7.refs_1_.refs_8_, ...), custom_call_target="tpu_custom_call" | custom-call | flops 1 | bytes 1 | tf_op jit(solution)/shard_map/pallas_call | solution.py:178
  52.2 0.0 collective-permute-done.11.refs_12_
  52.2 2.2 %shard_map.71 = (bf16[64,4096]{1,0:T(8,128)(2,1)}, bf16[64,4096]{1,0:T(8,128)(2,1)}, bf16[64,4096]{1,0:T(8,128)(2,1)}) custom-call(bf16[4,256,128]{2,1,0:T(8,128)(2,1)S(1)} %get-tuple-element.23.refs_0_, bf16[4,256,128]{2,1,0:T(8,128)(2,1)S(1)} %collective-permute-done.refs_1_, bf16[4,256,128]{2,1,0:T(8,128)(2,1)S(1)} %collective-permute-done.2.refs_2_, ...), custom_call_target="tpu_custom_call" | custom-call | tf_op jit(solution)/shard_map/pallas_call | solution.py:250
  (7 shorter events, 0.1 us)
Async XLA Ops:
  1.6 16.4 %collective-permute-start.1 = (bf16[4,256,128]{2,1,0:T(8,128)(2,1)S(1)}, bf16[4,256,128]{2,1,0:T(8,128)(2,1)S(1)}, u32[]{:S(2)}, u32[]{:S(2)}) collective-permute-start(bf16[4,256,128]{2,1,0:T(8,128)(2,1)S(1)} %shard_map.68), channel_id=1, source_target_pairs={{0,8},{1,9},{2,10},{3,11},{4,12},{5,13},{6,14},{7,15},{8,0},{9,1},... | collective-permute-start | bytes 786440 | tf_op jit(solution)/shard_map/ppermute | solution.py:271
  3.5 21.7 %collective-permute-start = (bf16[4,256,128]{2,1,0:T(8,128)(2,1)S(1)}, bf16[4,256,128]{2,1,0:T(8,128)(2,1)S(1)}, u32[]{:S(2)}, u32[]{:S(2)}) collective-permute-start(bf16[4,256,128]{2,1,0:T(8,128)(2,1)S(1)} %get-tuple-element.24), channel_id=1, source_target_pairs={{0,2},{1,3},{2,0},{3,1},{4,6},{5,7},{6,4},{7,5},{8,10},{9,11},{10,... | collective-permute-start | bytes 786440 | tf_op jit(solution)/shard_map/ppermute | solution.py:271
  4.8 24.4 %collective-permute-start.3 = (bf16[4,256,128]{2,1,0:T(8,128)(2,1)S(1)}, bf16[4,256,128]{2,1,0:T(8,128)(2,1)S(1)}, u32[]{:S(2)}, u32[]{:S(2)}) collective-permute-start(bf16[4,256,128]{2,1,0:T(8,128)(2,1)S(1)} %get-tuple-element.27), channel_id=1, source_target_pairs={{0,10},{1,11},{2,8},{3,9},{4,14},{5,15},{6,12},{7,13},{8,2},{9,3},... | collective-permute-start | bytes 786440 | tf_op jit(solution)/shard_map/ppermute | solution.py:271
  7.1 22.2 %collective-permute-start.2 = (bf16[4,256,128]{2,1,0:T(8,128)(2,1)S(1)}, bf16[4,256,128]{2,1,0:T(8,128)(2,1)S(1)}, u32[]{:S(2)}, u32[]{:S(2)}) collective-permute-start(bf16[4,256,128]{2,1,0:T(8,128)(2,1)S(1)} %get-tuple-element.26), channel_id=1, source_target_pairs={{0,4},{1,5},{2,6},{3,7},{4,0},{5,1},{6,2},{7,3},{8,12},{9,13},{10,... | collective-permute-start | bytes 786440 | tf_op jit(solution)/shard_map/ppermute | solution.py:271
  8.4 37.1 %collective-permute-start.5 = (bf16[4,256,128]{2,1,0:T(8,128)(2,1)S(1)}, bf16[4,256,128]{2,1,0:T(8,128)(2,1)S(1)}, u32[]{:S(2)}, u32[]{:S(2)}) collective-permute-start(bf16[4,256,128]{2,1,0:T(8,128)(2,1)S(1)} %get-tuple-element.31), channel_id=1, source_target_pairs={{0,14},{1,15},{2,12},{3,13},{4,10},{5,11},{6,8},{7,9},{8,6},{9,7},... | collective-permute-start | bytes 786440 | tf_op jit(solution)/shard_map/ppermute | solution.py:271
  18.0 27.5 %collective-permute-start.4 = (bf16[4,256,128]{2,1,0:T(8,128)(2,1)S(1)}, bf16[4,256,128]{2,1,0:T(8,128)(2,1)S(1)}, u32[]{:S(2)}, u32[]{:S(2)}) collective-permute-start(bf16[4,256,128]{2,1,0:T(8,128)(2,1)S(1)} %get-tuple-element.30), channel_id=1, source_target_pairs={{0,6},{1,7},{2,4},{3,5},{4,2},{5,3},{6,0},{7,1},{8,14},{9,15},{10,... | collective-permute-start | bytes 786440 | tf_op jit(solution)/shard_map/ppermute | solution.py:271
  25.2 25.0 %collective-permute-start.10 = (bf16[4,256,128]{2,1,0:T(8,128)(2,1)S(1)}, bf16[4,256,128]{2,1,0:T(8,128)(2,1)S(1)}, u32[]{:S(2)}, u32[]{:S(2)}) collective-permute-start(bf16[4,256,128]{2,1,0:T(8,128)(2,1)S(1)} %get-tuple-element.34), channel_id=1, source_target_pairs={{0,12},{1,13},{2,14},{3,15},{4,8},{5,9},{6,10},{7,11},{8,4},{9,5},... | collective-permute-start | bytes 786440 | tf_op jit(solution)/shard_map/ppermute | solution.py:271
  45.7 5.0 %collective-permute-start.7 = (bf16[7,256,128]{2,1,0:T(8,128)(2,1)S(1)}, bf16[7,256,128]{2,1,0:T(8,128)(2,1)S(1)}, u32[]{:S(2)}, u32[]{:S(2)}) collective-permute-start(bf16[7,256,128]{2,1,0:T(8,128)(2,1)S(1)} %pad_maximum_fusion.1), channel_id=1, source_target_pairs={{0,1},{1,0},{2,3},{3,2},{4,5},{5,4},{6,7},{7,6},{8,9},{9,8},{10,11... | collective-permute-start | bytes 1376264 | tf_op jit(solution)/shard_map/ppermute | solution.py:271
  46.4 4.3 %collective-permute-start.8 = (bf16[7,256,128]{2,1,0:T(8,128)(2,1)S(1)}, bf16[7,256,128]{2,1,0:T(8,128)(2,1)S(1)}, u32[]{:S(2)}, u32[]{:S(2)}) collective-permute-start(bf16[7,256,128]{2,1,0:T(8,128)(2,1)S(1)} %pad_maximum_fusion.2), channel_id=1, source_target_pairs={{0,1},{1,0},{2,3},{3,2},{4,5},{5,4},{6,7},{7,6},{8,9},{9,8},{10,11... | collective-permute-start | bytes 1376264 | tf_op jit(solution)/shard_map/ppermute | solution.py:271
  46.5 4.2 %collective-permute-start.9 = (bf16[7,256,128]{2,1,0:T(8,128)(2,1)S(1)}, bf16[7,256,128]{2,1,0:T(8,128)(2,1)S(1)}, u32[]{:S(2)}, u32[]{:S(2)}) collective-permute-start(bf16[7,256,128]{2,1,0:T(8,128)(2,1)S(1)} %pad_maximum_fusion.3), channel_id=1, source_target_pairs={{0,1},{1,0},{2,3},{3,2},{4,5},{5,4},{6,7},{7,6},{8,9},{9,8},{10,11... | collective-permute-start | bytes 1376264 | tf_op jit(solution)/shard_map/ppermute | solution.py:271
  47.0 3.7 %collective-permute-start.6 = (bf16[7,256,128]{2,1,0:T(8,128)(2,1)S(1)}, bf16[7,256,128]{2,1,0:T(8,128)(2,1)S(1)}, u32[]{:S(2)}, u32[]{:S(2)}) collective-permute-start(bf16[7,256,128]{2,1,0:T(8,128)(2,1)S(1)} %pad_maximum_fusion), channel_id=1, source_target_pairs={{0,1},{1,0},{2,3},{3,2},{4,5},{5,4},{6,7},{7,6},{8,9},{9,8},{10,11... | collective-permute-start | bytes 1376264 | tf_op jit(solution)/shard_map/ppermute | solution.py:271
  50.2 2.0 %collective-permute-start.11 = (bf16[4,256,128]{2,1,0:T(8,128)(2,1)S(1)}, bf16[4,256,128]{2,1,0:T(8,128)(2,1)S(1)}, u32[]{:S(2)}, u32[]{:S(2)}) collective-permute-start(bf16[4,256,128]{2,1,0:T(8,128)(2,1)S(1)} %collective-permute-done.10.refs_4_.refs_11_), channel_id=1, source_target_pairs={{0,1},{1,0},{2,3},{3,2},{4,5},{5,4},{6,7},{7,6},{8,9},{9,8},{10,11... | collective-permute-start | bytes 786440 | tf_op jit(solution)/shard_map/ppermute | solution.py:271

commit v9 on v8

--- a/solution.py
+++ b/solution.py
@@ -54,8 +54,8 @@
 
 
 CHIPS = 8
-OWN, NEAR, FAR = 0, (1, 2, 3), (4, 5, 7, 6)
-ISSUED = (4, 1, 5, 2, 7, 3, 6)
+OWN, NEAR, FAR = 0, (2, 3, 1), (4, 5, 7, 6)
+ISSUED = (4, 2, 5, 3, 7, 1, 6)
 EARLY = (OWN,) + NEAR + FAR[:-1]
 RELAYS = 4
 TENSORS = 4
@@ -239,7 +239,11 @@
     leave(1)
     for i in range(n_blocks):
         product(2, i, grad_half[found[i], 1, own_rows, :], 1)
-    leave(2)
+        window = (slice(None), pl.ds(pl.multiple_of(found[i] * length, length), length))
+        copies.append(
+            pltpu.make_async_copy(ready.at[(2,) + window], outs[2].at[window], sems.at[2 + i])
+        )
+        copies[-1].start()
     for copy in copies:
         copy.wait()
 
@@ -259,7 +263,7 @@
         ]
         + [pltpu.VMEM(*s) for s in within_shapes(sizes[-1], length)]
         + [turned_scratch(sizes[-1], length)]
-        + [pltpu.VMEM((3,) + out.shape, out.dtype), pltpu.SemaphoreType.DMA((3,))],
+        + [pltpu.VMEM((3,) + out.shape, out.dtype), pltpu.SemaphoreType.DMA((2 + n_blocks,))],
         compiler_params=PARAMS,
     )(*arrays, *done)
 

time: 54.7 us -> 54.7 us (level)
  starting transfers between devices: 14.1 us -> 12.2 us
  waiting for transfers between devices: 31.6 us -> 33.5 us
    ppermute x12, waiting for transfers between devices: 31.6 us -> 33.5 us  [chip_body(): lax.ppermute(x, 'seq', [(i, i ^ flip) for i in range(size)])]
    ppermute x12, starting transfers between devices: 14.1 us -> 12.2 us  [chip_body(): lax.ppermute(x, 'seq', [(i, i ^ flip) for i in range(size)])]
  transfers between devices with their start and end apart: 12 -> 12, of which waited for: 4 -> 6; matrix products, arithmetic and copies ran while one was open for 0% -> 0% of each run, Pallas kernels for 8% -> 8%
where the time goes in v9:
time: 54.7 us; the launch traced here: 54.5 us
  waiting for transfers between devices  33.5 us (61%)
  starting transfers between devices  12.2 us (22%)
  Pallas kernels  7.82 us (14%)
  between operations  0.72 us (1%)
    ppermute x12, waiting for transfers between devices, chip_body(): lax.ppermute(x, 'seq', [(i, i ^ flip) for i in range(size)])  33.5 us
    ppermute x12, starting transfers between devices, chip_body(): lax.ppermute(x, 'seq', [(i, i ^ flip) for i in range(size)])  12.2 us
    pallas_call x2, Pallas kernels, within(): pl.pallas_call(functools.partial(within_kernel, where, len(arrays)), out_...  2.83 us
    pallas_call x2, Pallas kernels, pack(): pl.pallas_call(functools.partial(pack_kernel, flips), out_shape=[shape] *...  2.76 us
    pallas_call x1, Pallas kernels, finish(): pl.pallas_call(functools.partial(finish_kernel, where, slots, sizes, len(...  2.23 us
  transfers between devices with their start and end apart: 12, of which 6 were waited for; matrix products, arithmetic and copies ran while one was open for 0% of the time, Pallas kernels for 8%

profile of v9, /device:TPU:19, one launch (start us, length us, event | category | flops | bytes accessed | tf_op | source)
XLA Modules:
  0.0 54.5 jit_solution(780112477662997886)
XLA Ops:
  0.6 1.0 %shard_map.68 = bf16[4,256,128]{2,1,0:T(8,128)(2,1)S(1)} custom-call(bf16[256,1024]{1,0:T(8,128)(2,1)} %refs_0_.3, bf16[256,1024]{1,0:T(8,128)(2,1)} %refs_1_.3, bf16[256,1024]{1,0:T(8,128)(2,1)} %refs_2_.3, bf16[256,1024]{1,0:T(8,128)(2,1)} %refs_3_.3), custom_call_target="tpu_custom_call" | custom-call | flops 1 | bytes 1 | tf_op jit(solution)/shard_map/pallas_call | solution.py:94
  1.6 0.1 collective-permute-start.1
  1.7 1.8 %shard_map.67 = (bf16[4,256,128]{2,1,0:T(8,128)(2,1)S(1)}, bf16[4,256,128]{2,1,0:T(8,128)(2,1)S(1)}, bf16[4,256,128]{2,1,0:T(8,128)(2,1)S(1)}, bf16[4,256,128]{2...) custom-call(bf16[256,1024]{1,0:T(8,128)(2,1)} %refs_0_.3, ...), custom_call_target="tpu_custom_call" | custom-call | flops 1 | bytes 1 | tf_op jit(solution)/shard_map/pallas_call | solution.py:94
  3.5 1.4 %collective-permute-start = (bf16[4,256,128]{2,1,0:T(8,128)(2,1)S(1)}, bf16[4,256,128]{2,1,0:T(8,128)(2,1)S(1)}, u32[]{:S(2)}, u32[]{:S(2)}) collective-permute-start(bf16[4,256,128]{2,1,0:T(8,128)(2,1)S(1)} %get-tuple-element.24), channel_id=1, source_target_pairs={{0,4},{1,5},{2,6},{3,7},{4,0},{5,1},{6,2},{7,3},{8,12},{9,13},{10,... | collective-permute-start | bytes 786440 | tf_op jit(solution)/shard_map/ppermute | solution.py:275
  4.9 3.3 %collective-permute-start.3 = (bf16[4,256,128]{2,1,0:T(8,128)(2,1)S(1)}, bf16[4,256,128]{2,1,0:T(8,128)(2,1)S(1)}, u32[]{:S(2)}, u32[]{:S(2)}) collective-permute-start(bf16[4,256,128]{2,1,0:T(8,128)(2,1)S(1)} %get-tuple-element.27), channel_id=1, source_target_pairs={{0,10},{1,11},{2,8},{3,9},{4,14},{5,15},{6,12},{7,13},{8,2},{9,3},... | collective-permute-start | bytes 786440 | tf_op jit(solution)/shard_map/ppermute | solution.py:275
  8.2 0.1 collective-permute-start.2
  8.3 1.1 %collective-permute-start.5 = (bf16[4,256,128]{2,1,0:T(8,128)(2,1)S(1)}, bf16[4,256,128]{2,1,0:T(8,128)(2,1)S(1)}, u32[]{:S(2)}, u32[]{:S(2)}) collective-permute-start(bf16[4,256,128]{2,1,0:T(8,128)(2,1)S(1)} %get-tuple-element.31), channel_id=1, source_target_pairs={{0,14},{1,15},{2,12},{3,13},{4,10},{5,11},{6,8},{7,9},{8,6},{9,7},... | collective-permute-start | bytes 786440 | tf_op jit(solution)/shard_map/ppermute | solution.py:275
  9.4 3.0 %collective-permute-done.1.refs_4_ = bf16[4,256,128]{2,1,0:T(8,128)(2,1)S(1)} collective-permute-done((bf16[4,256,128]{2,1,0:T(8,128)(2,1)S(1)}, bf16[4,256,128]{2,1,0:T(8,128)(2,1)S(1)}, u32[]{:S(2)}, u32[]{:S(2)}) %collective-permute-start.1) | collective-permute-done | bytes 262176 | tf_op jit(solution)/shard_map/ppermute | solution.py:275
  12.4 1.2 %collective-permute-start.4 = (bf16[4,256,128]{2,1,0:T(8,128)(2,1)S(1)}, bf16[4,256,128]{2,1,0:T(8,128)(2,1)S(1)}, u32[]{:S(2)}, u32[]{:S(2)}) collective-permute-start(bf16[4,256,128]{2,1,0:T(8,128)(2,1)S(1)} %get-tuple-element.30), channel_id=1, source_target_pairs={{0,2},{1,3},{2,0},{3,1},{4,6},{5,7},{6,4},{7,5},{8,10},{9,11},{10,... | collective-permute-start | bytes 786440 | tf_op jit(solution)/shard_map/ppermute | solution.py:275
  13.6 0.8 %collective-permute-done.refs_1_ = bf16[4,256,128]{2,1,0:T(8,128)(2,1)S(1)} collective-permute-done((bf16[4,256,128]{2,1,0:T(8,128)(2,1)S(1)}, bf16[4,256,128]{2,1,0:T(8,128)(2,1)S(1)}, u32[]{:S(2)}, u32[]{:S(2)}) %collective-permute-start) | collective-permute-done | bytes 262176 | tf_op jit(solution)/shard_map/ppermute | solution.py:275
  14.5 3.1 %collective-permute-start.10 = (bf16[4,256,128]{2,1,0:T(8,128)(2,1)S(1)}, bf16[4,256,128]{2,1,0:T(8,128)(2,1)S(1)}, u32[]{:S(2)}, u32[]{:S(2)}) collective-permute-start(bf16[4,256,128]{2,1,0:T(8,128)(2,1)S(1)} %get-tuple-element.34), channel_id=1, source_target_pairs={{0,12},{1,13},{2,14},{3,15},{4,8},{5,9},{6,10},{7,11},{8,4},{9,5},... | collective-permute-start | bytes 786440 | tf_op jit(solution)/shard_map/ppermute | solution.py:275
  17.6 6.1 %collective-permute-done.3.refs_5_ = bf16[4,256,128]{2,1,0:T(8,128)(2,1)S(1)} collective-permute-done((bf16[4,256,128]{2,1,0:T(8,128)(2,1)S(1)}, bf16[4,256,128]{2,1,0:T(8,128)(2,1)S(1)}, u32[]{:S(2)}, u32[]{:S(2)}) %collective-permute-start.3) | collective-permute-done | bytes 262176 | tf_op jit(solution)/shard_map/ppermute | solution.py:275
  23.7 4.1 %collective-permute-done.2.refs_2_ = bf16[4,256,128]{2,1,0:T(8,128)(2,1)S(1)} collective-permute-done((bf16[4,256,128]{2,1,0:T(8,128)(2,1)S(1)}, bf16[4,256,128]{2,1,0:T(8,128)(2,1)S(1)}, u32[]{:S(2)}, u32[]{:S(2)}) %collective-permute-start.2) | collective-permute-done | bytes 262176 | tf_op jit(solution)/shard_map/ppermute | solution.py:275
  27.8 17.8 %collective-permute-done.5.refs_6_ = bf16[4,256,128]{2,1,0:T(8,128)(2,1)S(1)} collective-permute-done((bf16[4,256,128]{2,1,0:T(8,128)(2,1)S(1)}, bf16[4,256,128]{2,1,0:T(8,128)(2,1)S(1)}, u32[]{:S(2)}, u32[]{:S(2)}) %collective-permute-start.5) | collective-permute-done | bytes 262176 | tf_op jit(solution)/shard_map/ppermute | solution.py:275
  45.5 0.0 collective-permute-done.4.refs_3_
  45.6 0.1 pad_maximum_fusion.1
  45.7 0.7 %collective-permute-start.7 = (bf16[7,256,128]{2,1,0:T(8,128)(2,1)S(1)}, bf16[7,256,128]{2,1,0:T(8,128)(2,1)S(1)}, u32[]{:S(2)}, u32[]{:S(2)}) collective-permute-start(bf16[7,256,128]{2,1,0:T(8,128)(2,1)S(1)} %pad_maximum_fusion.1), channel_id=1, source_target_pairs={{0,1},{1,0},{2,3},{3,2},{4,5},{5,4},{6,7},{7,6},{8,9},{9,8},{10,11... | collective-permute-start | bytes 1376264 | tf_op jit(solution)/shard_map/ppermute | solution.py:275
  46.3 0.1 pad_maximum_fusion.2
  46.4 0.1 collective-permute-start.8
  46.5 0.5 collective-permute-start.9
  47.0 0.1 collective-permute-start.6
  47.1 1.3 %shard_map.69 = (f32[7,128,128]{2,1,0:T(8,128)S(1)}, f32[7,128,128]{2,1,0:T(8,128)S(1)}, f32[7,3,64,256]{3,2,1,0:T(8,128)S(1)}) custom-call(bf16[4,256,128]{2,1,0:T(8,128)(2,1)S(1)} %get-tuple-element.23.refs_0_, bf16[4,256,128]{2,1,0:T(8,128)(2,1)S(1)} %collective-permute-done.refs_1_, bf16[4,256,128]{2,1,0:T(8,128)(2,1)S(1)} %collective-permute-done.2.refs_2_, ...), custom_call_target="tpu_custom_call" | custom-call | flops 1 | bytes 1 | tf_op jit(solution)/shard_map/pallas_call | solution.py:178
  48.5 1.7 %collective-permute-done.10.refs_4_.refs_11_ = bf16[4,256,128]{2,1,0:T(8,128)(2,1)S(1)} collective-permute-done((bf16[4,256,128]{2,1,0:T(8,128)(2,1)S(1)}, bf16[4,256,128]{2,1,0:T(8,128)(2,1)S(1)}, u32[]{:S(2)}, u32[]{:S(2)}) %collective-permute-start.10) | collective-permute-done | bytes 262176 | tf_op jit(solution)/shard_map/ppermute | solution.py:275
  50.2 0.5 collective-permute-start.11
  50.7 0.0 collective-permute-done.7.refs_1_.refs_8_
  50.7 0.0 collective-permute-done.8.refs_2_.refs_9_
  50.7 0.0 collective-permute-done.9.refs_3_.refs_10_
  50.7 0.0 collective-permute-done.6.refs_0_.refs_7_
  50.7 1.5 %shard_map.70 = (f32[8,128,128]{2,1,0:T(8,128)S(1)}, f32[8,128,128]{2,1,0:T(8,128)S(1)}, f32[8,3,64,256]{3,2,1,0:T(8,128)S(1)}) custom-call(bf16[7,256,128]{2,1,0:T(8,128)(2,1)S(1)} %collective-permute-done.6.refs_0_.refs_7_, bf16[7,256,128]{2,1,0:T(8,128)(2,1)S(1)} %collective-permute-done.7.refs_1_.refs_8_, ...), custom_call_target="tpu_custom_call" | custom-call | flops 1 | bytes 1 | tf_op jit(solution)/shard_map/pallas_call | solution.py:178
  52.2 0.0 collective-permute-done.11.refs_12_
  52.2 2.2 %shard_map.71 = (bf16[64,4096]{1,0:T(8,128)(2,1)}, bf16[64,4096]{1,0:T(8,128)(2,1)}, bf16[64,4096]{1,0:T(8,128)(2,1)}) custom-call(bf16[4,256,128]{2,1,0:T(8,128)(2,1)S(1)} %get-tuple-element.23.refs_0_, bf16[4,256,128]{2,1,0:T(8,128)(2,1)S(1)} %collective-permute-done.refs_1_, bf16[4,256,128]{2,1,0:T(8,128)(2,1)S(1)} %collective-permute-done.2.refs_2_, ...), custom_call_target="tpu_custom_call" | custom-call | tf_op jit(solution)/shard_map/pallas_call | solution.py:254
  (7 shorter events, 0.1 us)
Async XLA Ops:
  1.6 10.8 %collective-permute-start.1 = (bf16[4,256,128]{2,1,0:T(8,128)(2,1)S(1)}, bf16[4,256,128]{2,1,0:T(8,128)(2,1)S(1)}, u32[]{:S(2)}, u32[]{:S(2)}) collective-permute-start(bf16[4,256,128]{2,1,0:T(8,128)(2,1)S(1)} %shard_map.68), channel_id=1, source_target_pairs={{0,8},{1,9},{2,10},{3,11},{4,12},{5,13},{6,14},{7,15},{8,0},{9,1},... | collective-permute-start | bytes 786440 | tf_op jit(solution)/shard_map/ppermute | solution.py:275
  3.5 10.9 %collective-permute-start = (bf16[4,256,128]{2,1,0:T(8,128)(2,1)S(1)}, bf16[4,256,128]{2,1,0:T(8,128)(2,1)S(1)}, u32[]{:S(2)}, u32[]{:S(2)}) collective-permute-start(bf16[4,256,128]{2,1,0:T(8,128)(2,1)S(1)} %get-tuple-element.24), channel_id=1, source_target_pairs={{0,4},{1,5},{2,6},{3,7},{4,0},{5,1},{6,2},{7,3},{8,12},{9,13},{10,... | collective-permute-start | bytes 786440 | tf_op jit(solution)/shard_map/ppermute | solution.py:275
  4.9 18.8 %collective-permute-start.3 = (bf16[4,256,128]{2,1,0:T(8,128)(2,1)S(1)}, bf16[4,256,128]{2,1,0:T(8,128)(2,1)S(1)}, u32[]{:S(2)}, u32[]{:S(2)}) collective-permute-start(bf16[4,256,128]{2,1,0:T(8,128)(2,1)S(1)} %get-tuple-element.27), channel_id=1, source_target_pairs={{0,10},{1,11},{2,8},{3,9},{4,14},{5,15},{6,12},{7,13},{8,2},{9,3},... | collective-permute-start | bytes 786440 | tf_op jit(solution)/shard_map/ppermute | solution.py:275
  8.2 19.6 %collective-permute-start.2 = (bf16[4,256,128]{2,1,0:T(8,128)(2,1)S(1)}, bf16[4,256,128]{2,1,0:T(8,128)(2,1)S(1)}, u32[]{:S(2)}, u32[]{:S(2)}) collective-permute-start(bf16[4,256,128]{2,1,0:T(8,128)(2,1)S(1)} %get-tuple-element.26), channel_id=1, source_target_pairs={{0,6},{1,7},{2,4},{3,5},{4,2},{5,3},{6,0},{7,1},{8,14},{9,15},{10,... | collective-permute-start | bytes 786440 | tf_op jit(solution)/shard_map/ppermute | solution.py:275
  8.3 37.3 %collective-permute-start.5 = (bf16[4,256,128]{2,1,0:T(8,128)(2,1)S(1)}, bf16[4,256,128]{2,1,0:T(8,128)(2,1)S(1)}, u32[]{:S(2)}, u32[]{:S(2)}) collective-permute-start(bf16[4,256,128]{2,1,0:T(8,128)(2,1)S(1)} %get-tuple-element.31), channel_id=1, source_target_pairs={{0,14},{1,15},{2,12},{3,13},{4,10},{5,11},{6,8},{7,9},{8,6},{9,7},... | collective-permute-start | bytes 786440 | tf_op jit(solution)/shard_map/ppermute | solution.py:275
  12.4 33.1 %collective-permute-start.4 = (bf16[4,256,128]{2,1,0:T(8,128)(2,1)S(1)}, bf16[4,256,128]{2,1,0:T(8,128)(2,1)S(1)}, u32[]{:S(2)}, u32[]{:S(2)}) collective-permute-start(bf16[4,256,128]{2,1,0:T(8,128)(2,1)S(1)} %get-tuple-element.30), channel_id=1, source_target_pairs={{0,2},{1,3},{2,0},{3,1},{4,6},{5,7},{6,4},{7,5},{8,10},{9,11},{10,... | collective-permute-start | bytes 786440 | tf_op jit(solution)/shard_map/ppermute | solution.py:275
  14.5 35.7 %collective-permute-start.10 = (bf16[4,256,128]{2,1,0:T(8,128)(2,1)S(1)}, bf16[4,256,128]{2,1,0:T(8,128)(2,1)S(1)}, u32[]{:S(2)}, u32[]{:S(2)}) collective-permute-start(bf16[4,256,128]{2,1,0:T(8,128)(2,1)S(1)} %get-tuple-element.34), channel_id=1, source_target_pairs={{0,12},{1,13},{2,14},{3,15},{4,8},{5,9},{6,10},{7,11},{8,4},{9,5},... | collective-permute-start | bytes 786440 | tf_op jit(solution)/shard_map/ppermute | solution.py:275
  45.7 5.0 %collective-permute-start.7 = (bf16[7,256,128]{2,1,0:T(8,128)(2,1)S(1)}, bf16[7,256,128]{2,1,0:T(8,128)(2,1)S(1)}, u32[]{:S(2)}, u32[]{:S(2)}) collective-permute-start(bf16[7,256,128]{2,1,0:T(8,128)(2,1)S(1)} %pad_maximum_fusion.1), channel_id=1, source_target_pairs={{0,1},{1,0},{2,3},{3,2},{4,5},{5,4},{6,7},{7,6},{8,9},{9,8},{10,11... | collective-permute-start | bytes 1376264 | tf_op jit(solution)/shard_map/ppermute | solution.py:275
  46.4 4.3 %collective-permute-start.8 = (bf16[7,256,128]{2,1,0:T(8,128)(2,1)S(1)}, bf16[7,256,128]{2,1,0:T(8,128)(2,1)S(1)}, u32[]{:S(2)}, u32[]{:S(2)}) collective-permute-start(bf16[7,256,128]{2,1,0:T(8,128)(2,1)S(1)} %pad_maximum_fusion.2), channel_id=1, source_target_pairs={{0,1},{1,0},{2,3},{3,2},{4,5},{5,4},{6,7},{7,6},{8,9},{9,8},{10,11... | collective-permute-start | bytes 1376264 | tf_op jit(solution)/shard_map/ppermute | solution.py:275
  46.5 4.2 %collective-permute-start.9 = (bf16[7,256,128]{2,1,0:T(8,128)(2,1)S(1)}, bf16[7,256,128]{2,1,0:T(8,128)(2,1)S(1)}, u32[]{:S(2)}, u32[]{:S(2)}) collective-permute-start(bf16[7,256,128]{2,1,0:T(8,128)(2,1)S(1)} %pad_maximum_fusion.3), channel_id=1, source_target_pairs={{0,1},{1,0},{2,3},{3,2},{4,5},{5,4},{6,7},{7,6},{8,9},{9,8},{10,11... | collective-permute-start | bytes 1376264 | tf_op jit(solution)/shard_map/ppermute | solution.py:275
  47.0 3.7 %collective-permute-start.6 = (bf16[7,256,128]{2,1,0:T(8,128)(2,1)S(1)}, bf16[7,256,128]{2,1,0:T(8,128)(2,1)S(1)}, u32[]{:S(2)}, u32[]{:S(2)}) collective-permute-start(bf16[7,256,128]{2,1,0:T(8,128)(2,1)S(1)} %pad_maximum_fusion), channel_id=1, source_target_pairs={{0,1},{1,0},{2,3},{3,2},{4,5},{5,4},{6,7},{7,6},{8,9},{9,8},{10,11... | collective-permute-start | bytes 1376264 | tf_op jit(solution)/shard_map/ppermute | solution.py:275
  50.2 2.0 %collective-permute-start.11 = (bf16[4,256,128]{2,1,0:T(8,128)(2,1)S(1)}, bf16[4,256,128]{2,1,0:T(8,128)(2,1)S(1)}, u32[]{:S(2)}, u32[]{:S(2)}) collective-permute-start(bf16[4,256,128]{2,1,0:T(8,128)(2,1)S(1)} %collective-permute-done.10.refs_4_.refs_11_), channel_id=1, source_target_pairs={{0,1},{1,0},{2,3},{3,2},{4,5},{5,4},{6,7},{7,6},{8,9},{9,8},{10,11... | collective-permute-start | bytes 786440 | tf_op jit(solution)/shard_map/ppermute | solution.py:275
